TPU v7x, 32 devices: a whole 2x2x4 slice. The times are simulated.
32 devices in a mesh: tm: 4 (over y, core), tile: 8 (over z, x).
Axes of the slice: x: 2, y: 2, z: 4, core: 2. Of those that a mesh axis runs over, the one named last changes fastest.
Arguments:
- basis_fields: bfloat16 [4, 3, 256, 64, 256], P('tm', None, None, 'tile'), may hold values from -0.5 to 0.5
- mean_depth: float32 [64, 256], P('tile'), may hold values from 0.5 to 1.9
- obs_cells: int32 [4, 2048], P('tm', 'tile'), may hold values from 0 to 16383, as said below
- obs_fields: int32 [4, 2048], P('tm', 'tile'), may hold values from 0 to 2
- obs_weight: float32 [4, 2048], P('tm', 'tile'), may hold values from 0.05 to 0.5
- innovation: float32 [4, 2048], P('tm', 'tile'), may hold values from -6 to 6
- transition: float32 [256, 256], replicated, may hold values from -1 to 1
- model_error: float32 [256], replicated, may hold values from 0.2 to 1
Outputs:
- reduced_mean: float32 [4, 256], P('tm')
- increments: float32 [4, 3, 64, 256], P('tm', None, 'tile')
Inputs may be any that keep to these rules, and one draw needn't show every extreme that they name: obs_cells[k, o] lies in grid rows (o // 256) * 8 to (o // 256) * 8 + 7. `obs_fields`: 0 is height, 1 eastward velocity, 2 northward velocity.
All inputs are finite; a program needn't handle non-finite values.
Results may differ from a plain program's by a relative error of at most 0.0003.
Values sent between devices are 32-bit elements; how exact they have to be, the bound alone decides.
No kernel may reach another device: no remote copies, remote signals or barrier semaphores. Data moves between devices by JAX's collectives and lax.ppermute only.
A program may use at most 64 MiB of HBM per device.

v0:
```python
import jax
import jax.numpy as jnp
from jax import lax
from jax.sharding import PartitionSpec as P

STEPS = 4


A_COEF = 0.5
B_COEF = 0.5
CORIOLIS = 0.3
NEWTON_TURNS = 18


def padded_2(block, sides, width):
    for axis, dim in sides:
        count = lax.axis_size(axis)
        forward = [(i, i + 1) for i in range(count - 1)]
        backward = [(target, source) for source, target in forward]
        low = lax.ppermute(
            lax.slice_in_dim(block, block.shape[dim] - width, None, axis=dim), axis, forward
        )
        high = lax.ppermute(lax.slice_in_dim(block, 0, width, axis=dim), axis, backward)
        block = jnp.concatenate([low, block, high], axis=dim)
    return block


def from_behind(array, axis, by):
    count = lax.axis_size(axis)
    pairs = [(i, i + by) for i in range(count) if 0 <= i + by < count]
    return lax.ppermute(array, axis, pairs)


def matmul_high(left, right):
    return jnp.dot(left, right, precision=lax.Precision.HIGHEST)


def diff_cols(values):
    return jnp.roll(values, -1, axis=-1) - jnp.roll(values, 1, axis=-1)


def advance(current, mean_depth):
    height, eastward, northward = (current[0], current[1], current[2])
    padded = padded_2(height, (("tile", 1),), 1)
    east_new = eastward + CORIOLIS * northward - A_COEF * diff_cols(height)
    north_new = northward - CORIOLIS * eastward - A_COEF * (padded[:, 2:, :] - padded[:, :-2, :])
    rimmed = padded_2(north_new, (("tile", 1),), 1)
    height_new = height - B_COEF * mean_depth * (
        diff_cols(east_new) + rimmed[:, 2:, :] - rimmed[:, :-2, :]
    )
    return jnp.stack([height_new, east_new, north_new])


def unpack(packed):
    order = packed.shape[1]
    return (
        packed[:order],
        packed[order : 2 * order],
        packed[2 * order : 3 * order],
        packed[3 * order],
        packed[3 * order + 1],
    )


def pack(trans, cov, prec, mean, info):
    return jnp.concatenate([trans, cov, prec, mean[None, :], info[None, :]], axis=0)


def invert_shifted(offdiag):
    identity_mat = jnp.eye(offdiag.shape[0], dtype=jnp.float32)
    system = identity_mat + offdiag
    spread = 1.0 + jnp.sqrt(jnp.sum(offdiag * offdiag))
    start = identity_mat / spread

    def newton_turn(turn_index, estimate):
        return matmul_high(estimate, 2.0 * identity_mat - matmul_high(system, estimate))

    return lax.fori_loop(0, NEWTON_TURNS, newton_turn, start)


def form_element(gram_sum, rhs_sum, transition, model_error, position):
    root_q = jnp.sqrt(model_error)
    coupled = transition * (position > 0).astype(jnp.float32)
    precise = invert_shifted(root_q[:, None] * gram_sum * root_q[None, :])
    trans = root_q[:, None] * matmul_high(precise, coupled / root_q[:, None])
    cov = root_q[:, None] * precise * root_q[None, :]
    vector = matmul_high(precise, root_q * rhs_sum)
    mean = root_q * vector
    info = matmul_high(coupled.T, vector / root_q)
    inner = matmul_high(precise, root_q[:, None] * gram_sum) / root_q[:, None]
    prec = matmul_high(coupled.T, matmul_high(inner, coupled))
    return pack(trans, cov, prec, mean, info)


def combine(earlier, latter):
    trans_one, cov_one, prec_one, mean_one, info_one = unpack(earlier)
    trans_two, cov_two, prec_two, mean_two, info_two = unpack(latter)
    inverse = invert_shifted(matmul_high(cov_one, prec_two))
    scaled = matmul_high(trans_two, inverse)
    trans = matmul_high(scaled, trans_one)
    mean = matmul_high(scaled, mean_one + matmul_high(cov_one, info_two)) + mean_two
    cov = matmul_high(matmul_high(scaled, cov_one), trans_two.T) + cov_two
    back = inverse.T
    info = (
        matmul_high(trans_one.T, matmul_high(back, info_two - matmul_high(prec_two, mean_one)))
        + info_one
    )
    prec = matmul_high(trans_one.T, matmul_high(matmul_high(back, prec_two), trans_one)) + prec_one
    return pack(trans, cov, prec, mean, info)


def on_device(
    basis_fields, mean_depth, obs_cells, obs_fields, obs_weight, innovation, transition, model_error
):
    rows = basis_fields.shape[3]
    cols = basis_fields.shape[4]
    order = transition.shape[0]
    current = basis_fields[0].astype(jnp.float32)
    for repeat in range(STEPS):
        current = advance(current, mean_depth)
    flattened = current.reshape(3, order, rows * cols)
    local_cells = obs_cells[0] - lax.axis_index("tile") * (rows * cols)
    projected = flattened[obs_fields[0], :, local_cells]
    weighted = projected * obs_weight[0][:, None]
    gram_part = matmul_high(weighted.T, projected)
    rhs_part = matmul_high(innovation[0] * obs_weight[0], projected)
    gram_sum, rhs_sum = lax.psum((gram_part, rhs_part), "tile")
    position = lax.axis_index("tm")
    element = form_element(gram_sum, rhs_sum, transition, model_error, position)

    def turn(turn_index, running):
        incoming = from_behind(running, "tm", 1)
        joined = combine(incoming, element)
        return jnp.where(position == turn_index + 1, joined, running)

    combined = lax.fori_loop(0, lax.axis_size("tm") - 1, turn, element)
    reduced = combined[3 * order]
    summed = jnp.einsum("r,frc->fc", reduced, flattened, precision=lax.Precision.HIGHEST)
    return (reduced[None, :], summed.reshape(3, rows, cols)[None])


def solution(mesh):
    return jax.shard_map(
        on_device,
        mesh=mesh,
        in_specs=(
            P("tm", None, None, "tile", None),
            P("tile", None),
            P("tm", "tile"),
            P("tm", "tile"),
            P("tm", "tile"),
            P("tm", "tile"),
            P(),
            P(),
        ),
        out_specs=(P("tm", None), P("tm", None, "tile", None)),
        check_vma=False,
    )
```

profile of v0, /device:TPU:14, one launch (start us, length us, event | category | flops | bytes accessed | tf_op | source)
XLA Modules:
  0.0 428.8 jit_solution(3810142237021589285)
XLA Ops:
  13.7 4.3 %collective-permute-start.2 = (f32[256,1,256]{2,1,0:T(1,128)}, f32[256,1,256]{2,1,0:T(1,128)}, u32[]{:S(2)}, u32[]{:S(2)}) collective-permute-start(f32[256,1,256]{2,1,0:T(1,128)} %get-tuple-element.302), channel_id=1, source_target_pairs={{0,1},{1,2},{2,3},{3,4},{4,5},{5,6},{6,7},{8,9},{9,10},{10,11},{11... | collective-permute-start | bytes 786440 | tf_op jit(solution)/shard_map/ppermute | solution.py:20
  28.0 4.7 %fusion.55 = (f32[256,8,256]{2,1,0:T(8,128)S(1)}, f32[256,8,256]{2,1,0:T(8,128)S(1)}) fusion(f32[256,8,1]{2,1,0:T(8,128)} %get-tuple-element.296, f32[256,8,255]{2,1,0:T(8,128)} %get-tuple-element.298, f32[256,8,255]{2,1,0:T(8,128)} %get-tuple-element.297, f32[256,8,1]{2,1,0:T(8,128)S(1)} %get-tuple-element.295, f32[1,3,256,8,256]{4,3,2,1,0:T(8,128)} %copy-done.1, ...), kind=kLoop, calls=%fused_computation.88 | loop fusion | flops 7340032 | bytes 15204352 | tf_op jit(solution)/shard_map/sub | solution.py:45
  35.6 4.8 %collective-permute-start.4 = (f32[256,1,256]{2,1,0:T(1,128)S(1)}, f32[256,1,256]{2,1,0:T(1,128)S(1)}, u32[]{:S(2)}, u32[]{:S(2)}) collective-permute-start(f32[256,1,256]{2,1,0:T(1,128)S(1)} %get-tuple-element.300), channel_id=1, source_target_pairs={{0,1},{1,2},{2,3},{3,4},{4,5},{5,6},{6,7},{8,9},{9,10},{10,11},{11... | collective-permute-start | bytes 786440 | tf_op jit(solution)/shard_map/ppermute | solution.py:20
  40.8 6.5 %collective-permute-done.3 = f32[256,1,256]{2,1,0:T(1,128)S(1)} collective-permute-done((f32[256,1,256]{2,1,0:T(1,128)S(1)}, f32[256,1,256]{2,1,0:T(1,128)S(1)}, u32[]{:S(2)}, u32[]{:S(2)}) %collective-permute-start.3) | collective-permute-done | bytes 262176 | tf_op jit(solution)/shard_map/ppermute | solution.py:23
  50.4 3.1 fusion.49
  56.4 4.8 %collective-permute-start.6 = (f32[256,1,256]{2,1,0:T(1,128)S(1)}, f32[256,1,256]{2,1,0:T(1,128)S(1)}, u32[]{:S(2)}, u32[]{:S(2)}) collective-permute-start(f32[256,1,256]{2,1,0:T(1,128)S(1)} %get-tuple-element.290), channel_id=1, source_target_pairs={{0,1},{1,2},{2,3},{3,4},{4,5},{5,6},{6,7},{8,9},{9,10},{10,11},{11... | collective-permute-start | bytes 786440 | tf_op jit(solution)/shard_map/ppermute | solution.py:20
  61.6 6.5 %collective-permute-done.5 = f32[256,1,256]{2,1,0:T(1,128)S(1)} collective-permute-done((f32[256,1,256]{2,1,0:T(1,128)S(1)}, f32[256,1,256]{2,1,0:T(1,128)S(1)}, u32[]{:S(2)}, u32[]{:S(2)}) %collective-permute-start.5) | collective-permute-done | bytes 262176 | tf_op jit(solution)/shard_map/ppermute | solution.py:23
  76.0 5.0 %collective-permute-start.8 = (f32[256,1,256]{2,1,0:T(1,128)S(1)}, f32[256,1,256]{2,1,0:T(1,128)S(1)}, u32[]{:S(2)}, u32[]{:S(2)}) collective-permute-start(f32[256,1,256]{2,1,0:T(1,128)S(1)} %get-tuple-element.288), channel_id=1, source_target_pairs={{0,1},{1,2},{2,3},{3,4},{4,5},{5,6},{6,7},{8,9},{9,10},{10,11},{11... | collective-permute-start | bytes 786440 | tf_op jit(solution)/shard_map/ppermute | solution.py:20
  81.3 6.3 %collective-permute-done.7 = f32[256,1,256]{2,1,0:T(1,128)S(1)} collective-permute-done((f32[256,1,256]{2,1,0:T(1,128)S(1)}, f32[256,1,256]{2,1,0:T(1,128)S(1)}, u32[]{:S(2)}, u32[]{:S(2)}) %collective-permute-start.7) | collective-permute-done | bytes 262176 | tf_op jit(solution)/shard_map/ppermute | solution.py:23
  96.0 3.4 collective-permute-start.9
  99.8 9.5 %collective-permute-done.10 = f32[256,1,256]{2,1,0:T(1,128)S(1)} collective-permute-done((f32[256,1,256]{2,1,0:T(1,128)S(1)}, f32[256,1,256]{2,1,0:T(1,128)S(1)}, u32[]{:S(2)}, u32[]{:S(2)}) %collective-permute-start.10) | collective-permute-done | bytes 262176 | tf_op jit(solution)/shard_map/ppermute | solution.py:20
  114.6 4.4 %collective-permute-start.12 = (f32[256,1,256]{2,1,0:T(1,128)S(1)}, f32[256,1,256]{2,1,0:T(1,128)S(1)}, u32[]{:S(2)}, u32[]{:S(2)}) collective-permute-start(f32[256,1,256]{2,1,0:T(1,128)S(1)} %get-tuple-element.276), channel_id=1, source_target_pairs={{0,1},{1,2},{2,3},{3,4},{4,5},{5,6},{6,7},{8,9},{9,10},{10,11},{11... | collective-permute-start | bytes 786440 | tf_op jit(solution)/shard_map/ppermute | solution.py:20
  119.3 6.6 %collective-permute-done.11 = f32[256,1,256]{2,1,0:T(1,128)S(1)} collective-permute-done((f32[256,1,256]{2,1,0:T(1,128)S(1)}, f32[256,1,256]{2,1,0:T(1,128)S(1)}, u32[]{:S(2)}, u32[]{:S(2)}) %collective-permute-start.11) | collective-permute-done | bytes 262176 | tf_op jit(solution)/shard_map/ppermute | solution.py:23
  133.2 4.6 %collective-permute-start.14 = (f32[256,1,256]{2,1,0:T(1,128)S(1)}, f32[256,1,256]{2,1,0:T(1,128)S(1)}, u32[]{:S(2)}, u32[]{:S(2)}) collective-permute-start(f32[256,1,256]{2,1,0:T(1,128)S(1)} %get-tuple-element.266), channel_id=1, source_target_pairs={{0,1},{1,2},{2,3},{3,4},{4,5},{5,6},{6,7},{8,9},{9,10},{10,11},{11... | collective-permute-start | bytes 786440 | tf_op jit(solution)/shard_map/ppermute | solution.py:20
  138.2 6.2 %collective-permute-done.13 = f32[256,1,256]{2,1,0:T(1,128)S(1)} collective-permute-done((f32[256,1,256]{2,1,0:T(1,128)S(1)}, f32[256,1,256]{2,1,0:T(1,128)S(1)}, u32[]{:S(2)}, u32[]{:S(2)}) %collective-permute-start.13) | collective-permute-done | bytes 262176 | tf_op jit(solution)/shard_map/ppermute | solution.py:23
  157.4 3.4 fusion.92
  165.7 5.1 %collective-permute-start.16 = (f32[256,1,256]{2,1,0:T(1,128)}, f32[256,1,256]{2,1,0:T(1,128)S(1)}, u32[]{:S(2)}, u32[]{:S(2)}) collective-permute-start(f32[256,1,256]{2,1,0:T(1,128)} %get-tuple-element.260), channel_id=1, source_target_pairs={{0,1},{1,2},{2,3},{3,4},{4,5},{5,6},{6,7},{8,9},{9,10},{10,11},{11... | collective-permute-start | bytes 786440 | tf_op jit(solution)/shard_map/ppermute | solution.py:20
  172.6 4.9 %collective-permute-done.15 = f32[256,1,256]{2,1,0:T(1,128)S(1)} collective-permute-done((f32[256,1,256]{2,1,0:T(1,128)}, f32[256,1,256]{2,1,0:T(1,128)S(1)}, u32[]{:S(2)}, u32[]{:S(2)}) %collective-permute-start.15) | collective-permute-done | bytes 262176 | tf_op jit(solution)/shard_map/ppermute | solution.py:23
  180.6 4.9 %fusion.28 = f32[256,8,256]{2,1,0:T(8,128)} fusion(f32[256,8,256]{2,1,0:T(8,128)S(1)} %fusion.35, f32[256,8,256]{2,1,0:T(8,128)S(1)} %copy-done.2, f32[256,1,256]{2,1,0:T(1,128)S(1)} %collective-permute-done.16, f32[256,1,256]{2,1,0:T(1,128)S(1)} %collective-permute-done.15, f32[256,8,1]{2,1,0:T(8,128)S(1)} %get-tuple-element.256, ...), kind=kLoop, calls=%fused_computation.42 | loop fusion | flops 4718592 | bytes 11018240 | tf_op jit(solution)/shard_map/sub | solution.py:48
  185.5 3.1 copy.17
  188.6 5.6 %pad_maximum_fusion = f32[3,256,2048]{1,2,0:T(8,128)} fusion(f32[1,256,2048]{1,2,0:T(8,128)} %bitcast.205, f32[1,256,2048]{1,2,0:T(8,128)S(1)} %bitcast.204, f32[1,256,2048]{1,2,0:T(8,128)} %bitcast.206), kind=kLoop, calls=%fused_computation.38 | loop fusion | flops 3145728 | bytes 12582912 | tf_op jit(solution)/shard_map/stack | solution.py:51
  198.2 14.3 %psum.15 = f32[256]{0:T(256)S(1)} all-reduce(f32[256]{0:T(256)S(1)} %bitcast.223), channel_id=1, replica_groups=mesh['tm'=4,'tile'=8] {'tile'}, use_global_device_ids=true, to_apply=%region_4.5 | all-reduce | flops 256 | bytes 2048 | tf_op jit(solution)/shard_map/psum | solution.py:127
  212.5 56.3 %all-reduce.2.cloned.1.call-done = f32[256,256]{1,0:T(8,128)} async-done(((f32[256,256]{1,0:T(8,128)}), f32[256,256]{1,0:T(8,128)}) %all-reduce.2.cloned.1.call-update) | async-done | bytes 262160 | tf_op jit(solution)/shard_map/psum | solution.py:127
  271.3 19.1 %while.49 = (s32[]{:T(128)}, f32[256,256]{0,1:T(8,128)S(1)}, f32[256,256]{1,0:T(8,128)S(1)}, s32[]{:T(128)}) while((s32[]{:T(128)}, f32[256,256]{0,1:T(8,128)S(1)}, f32[256,256]{1,0:T(8,128)S(1)}, s32[]{:T(128)}) %tuple.111), condition=%wide.region_3.4_spmd.clone, body=%wide.region_2.3_spmd.clone.sunk | while | flops 402849792 | bytes 2097205 | solution.py:78
  293.7 119.2 %while.48 = (s32[]{:T(128)}, f32[770,256]{1,0:T(8,128)S(1)}, s32[]{:T(128)}, f32[256,256]{1,0:T(8,128)S(1)}, f32[256,256]{1,0:T(8,128)S(1)}, /*index=5*/f32[256,...) while((s32[]{:T(128)}, f32[770,256]{1,0:T(8,128)S(1)}, ...), condition=%wide.region_9.10_spmd, body=%wide.region_5.9_spmd.sunk | while | flops 2018182656 | bytes 18133292 | solution.py:136
  295.6 11.5 %collective-permute-done = f32[770,256]{1,0:T(8,128)S(1)} collective-permute-done((f32[770,256]{1,0:T(8,128)S(1)}, f32[770,256]{1,0:T(8,128)S(1)}, u32[]{:S(2)}, u32[]{:S(2)}) %collective-permute-start) | collective-permute-done | bytes 788512 | tf_op jit(solution)/shard_map/while/body/eval_jaxpr/ppermute | solution.py:31
  308.9 19.2 %while.50 = (s32[]{:T(128)}, f32[256,256]{0,1:T(8,128)S(1)}, f32[256,256]{1,0:T(8,128)S(1)}, s32[]{:T(128)}) while((s32[]{:T(128)}, f32[256,256]{0,1:T(8,128)S(1)}, f32[256,256]{1,0:T(8,128)S(1)}, s32[]{:T(128)}) %tuple.108), condition=%wide.region_8.8_spmd.clone, body=%wide.region_7.7_spmd.clone.sunk | while | flops 402849792 | bytes 2097205 | solution.py:78
  335.3 11.5 %collective-permute-done = f32[770,256]{1,0:T(8,128)S(1)} collective-permute-done((f32[770,256]{1,0:T(8,128)S(1)}, f32[770,256]{1,0:T(8,128)S(1)}, u32[]{:S(2)}, u32[]{:S(2)}) %collective-permute-start) | collective-permute-done | bytes 788512 | tf_op jit(solution)/shard_map/while/body/eval_jaxpr/ppermute | solution.py:31
  348.6 19.2 %while.50 = (s32[]{:T(128)}, f32[256,256]{0,1:T(8,128)S(1)}, f32[256,256]{1,0:T(8,128)S(1)}, s32[]{:T(128)}) while((s32[]{:T(128)}, f32[256,256]{0,1:T(8,128)S(1)}, f32[256,256]{1,0:T(8,128)S(1)}, s32[]{:T(128)}) %tuple.108), condition=%wide.region_8.8_spmd.clone, body=%wide.region_7.7_spmd.clone.sunk | while | flops 402849792 | bytes 2097205 | solution.py:78
  374.9 11.5 %collective-permute-done = f32[770,256]{1,0:T(8,128)S(1)} collective-permute-done((f32[770,256]{1,0:T(8,128)S(1)}, f32[770,256]{1,0:T(8,128)S(1)}, u32[]{:S(2)}, u32[]{:S(2)}) %collective-permute-start) | collective-permute-done | bytes 788512 | tf_op jit(solution)/shard_map/while/body/eval_jaxpr/ppermute | solution.py:31
  388.2 19.2 %while.50 = (s32[]{:T(128)}, f32[256,256]{0,1:T(8,128)S(1)}, f32[256,256]{1,0:T(8,128)S(1)}, s32[]{:T(128)}) while((s32[]{:T(128)}, f32[256,256]{0,1:T(8,128)S(1)}, f32[256,256]{1,0:T(8,128)S(1)}, s32[]{:T(128)}) %tuple.108), condition=%wide.region_8.8_spmd.clone, body=%wide.region_7.7_spmd.clone.sunk | while | flops 402849792 | bytes 2097205 | solution.py:78
  412.9 7.9 %fusion.87 = f32[1,3,8,256]{3,0,2,1:T(1,128)S(1)} fusion(f32[3,8,256,256]{3,2,1,0:T(8,128)} %bitcast.202, f32[1,256]{1,0:T(1,128)S(1)} %slice.329), kind=kOutput, calls=%fused_computation.136 | convolution fusion | flops 18874368 | bytes 6317056 | tf_op jit(solution)/shard_map/r,frc->fc/dot_general | solution.py:138
  (386 shorter events, 186.9 us)
Async XLA Ops:
  7.2 261.6 %all-reduce.2.cloned.1.call-start = ((), (), s32[]{:S(2)}) async-start(), calls=%async_computation | async-start | bytes 524288 | tf_op jit(solution)/shard_map/psum | solution.py:127
  9.6 11.0 %copy-start.1 = (f32[1,3,256,8,256]{4,3,2,1,0:T(8,128)}, f32[1,3,256,8,256]{4,3,2,1,0:T(8,128)S(1)}, u32[]{:S(2)}) copy-start(f32[1,3,256,8,256]{4,3,2,1,0:T(8,128)S(1)} %convert_element_type.21) | copy-start | bytes 18874372
  11.2 13.9 %collective-permute-start.1 = (f32[256,1,256]{2,1,0:T(1,128)}, f32[256,1,256]{2,1,0:T(1,128)S(1)}, u32[]{:S(2)}, u32[]{:S(2)}) collective-permute-start(f32[256,1,256]{2,1,0:T(1,128)} %get-tuple-element.301), channel_id=1, source_target_pairs={{1,0},{2,1},{3,2},{4,3},{5,4},{6,5},{7,6},{9,8},{10,9},{11,10},{12... | collective-permute-start | bytes 786440 | tf_op jit(solution)/shard_map/ppermute | solution.py:23
  13.7 14.3 %collective-permute-start.2 = (f32[256,1,256]{2,1,0:T(1,128)}, f32[256,1,256]{2,1,0:T(1,128)}, u32[]{:S(2)}, u32[]{:S(2)}) collective-permute-start(f32[256,1,256]{2,1,0:T(1,128)} %get-tuple-element.302), channel_id=1, source_target_pairs={{0,1},{1,2},{2,3},{3,4},{4,5},{5,6},{6,7},{8,9},{9,10},{10,11},{11... | collective-permute-start | bytes 786440 | tf_op jit(solution)/shard_map/ppermute | solution.py:20
  20.6 1.3 copy-start.12
  20.6 1.3 copy-start.8
  20.7 1.3 copy-start.13
  20.7 1.4 copy-start.7
  33.7 13.6 %collective-permute-start.3 = (f32[256,1,256]{2,1,0:T(1,128)S(1)}, f32[256,1,256]{2,1,0:T(1,128)S(1)}, u32[]{:S(2)}, u32[]{:S(2)}) collective-permute-start(f32[256,1,256]{2,1,0:T(1,128)S(1)} %get-tuple-element.299), channel_id=1, source_target_pairs={{1,0},{2,1},{3,2},{4,3},{5,4},{6,5},{7,6},{9,8},{10,9},{11,10},{12... | collective-permute-start | bytes 786440 | tf_op jit(solution)/shard_map/ppermute | solution.py:23
  35.6 14.7 %collective-permute-start.4 = (f32[256,1,256]{2,1,0:T(1,128)S(1)}, f32[256,1,256]{2,1,0:T(1,128)S(1)}, u32[]{:S(2)}, u32[]{:S(2)}) collective-permute-start(f32[256,1,256]{2,1,0:T(1,128)S(1)} %get-tuple-element.300), channel_id=1, source_target_pairs={{0,1},{1,2},{2,3},{3,4},{4,5},{5,6},{6,7},{8,9},{9,10},{10,11},{11... | collective-permute-start | bytes 786440 | tf_op jit(solution)/shard_map/ppermute | solution.py:20
  54.5 13.6 %collective-permute-start.5 = (f32[256,1,256]{2,1,0:T(1,128)S(1)}, f32[256,1,256]{2,1,0:T(1,128)S(1)}, u32[]{:S(2)}, u32[]{:S(2)}) collective-permute-start(f32[256,1,256]{2,1,0:T(1,128)S(1)} %get-tuple-element.289), channel_id=1, source_target_pairs={{1,0},{2,1},{3,2},{4,3},{5,4},{6,5},{7,6},{9,8},{10,9},{11,10},{12... | collective-permute-start | bytes 786440 | tf_op jit(solution)/shard_map/ppermute | solution.py:23
  56.4 14.7 %collective-permute-start.6 = (f32[256,1,256]{2,1,0:T(1,128)S(1)}, f32[256,1,256]{2,1,0:T(1,128)S(1)}, u32[]{:S(2)}, u32[]{:S(2)}) collective-permute-start(f32[256,1,256]{2,1,0:T(1,128)S(1)} %get-tuple-element.290), channel_id=1, source_target_pairs={{0,1},{1,2},{2,3},{3,4},{4,5},{5,6},{6,7},{8,9},{9,10},{10,11},{11... | collective-permute-start | bytes 786440 | tf_op jit(solution)/shard_map/ppermute | solution.py:20
  74.1 13.6 %collective-permute-start.7 = (f32[256,1,256]{2,1,0:T(1,128)S(1)}, f32[256,1,256]{2,1,0:T(1,128)S(1)}, u32[]{:S(2)}, u32[]{:S(2)}) collective-permute-start(f32[256,1,256]{2,1,0:T(1,128)S(1)} %get-tuple-element.287), channel_id=1, source_target_pairs={{1,0},{2,1},{3,2},{4,3},{5,4},{6,5},{7,6},{9,8},{10,9},{11,10},{12... | collective-permute-start | bytes 786440 | tf_op jit(solution)/shard_map/ppermute | solution.py:23
  76.0 14.7 %collective-permute-start.8 = (f32[256,1,256]{2,1,0:T(1,128)S(1)}, f32[256,1,256]{2,1,0:T(1,128)S(1)}, u32[]{:S(2)}, u32[]{:S(2)}) collective-permute-start(f32[256,1,256]{2,1,0:T(1,128)S(1)} %get-tuple-element.288), channel_id=1, source_target_pairs={{0,1},{1,2},{2,3},{3,4},{4,5},{5,6},{6,7},{8,9},{9,10},{10,11},{11... | collective-permute-start | bytes 786440 | tf_op jit(solution)/shard_map/ppermute | solution.py:20
  93.6 15.7 %collective-permute-start.10 = (f32[256,1,256]{2,1,0:T(1,128)S(1)}, f32[256,1,256]{2,1,0:T(1,128)S(1)}, u32[]{:S(2)}, u32[]{:S(2)}) collective-permute-start(f32[256,1,256]{2,1,0:T(1,128)S(1)} %get-tuple-element.278), channel_id=1, source_target_pairs={{0,1},{1,2},{2,3},{3,4},{4,5},{5,6},{6,7},{8,9},{9,10},{10,11},{11... | collective-permute-start | bytes 786440 | tf_op jit(solution)/shard_map/ppermute | solution.py:20
  96.0 13.3 %collective-permute-start.9 = (f32[256,1,256]{2,1,0:T(1,128)S(1)}, f32[256,1,256]{2,1,0:T(1,128)S(1)}, u32[]{:S(2)}, u32[]{:S(2)}) collective-permute-start(f32[256,1,256]{2,1,0:T(1,128)S(1)} %get-tuple-element.277), channel_id=1, source_target_pairs={{1,0},{2,1},{3,2},{4,3},{5,4},{6,5},{7,6},{9,8},{10,9},{11,10},{12... | collective-permute-start | bytes 786440 | tf_op jit(solution)/shard_map/ppermute | solution.py:23
  112.2 13.7 %collective-permute-start.11 = (f32[256,1,256]{2,1,0:T(1,128)S(1)}, f32[256,1,256]{2,1,0:T(1,128)S(1)}, u32[]{:S(2)}, u32[]{:S(2)}) collective-permute-start(f32[256,1,256]{2,1,0:T(1,128)S(1)} %get-tuple-element.275), channel_id=1, source_target_pairs={{1,0},{2,1},{3,2},{4,3},{5,4},{6,5},{7,6},{9,8},{10,9},{11,10},{12... | collective-permute-start | bytes 786440 | tf_op jit(solution)/shard_map/ppermute | solution.py:23
  114.6 13.4 %collective-permute-start.12 = (f32[256,1,256]{2,1,0:T(1,128)S(1)}, f32[256,1,256]{2,1,0:T(1,128)S(1)}, u32[]{:S(2)}, u32[]{:S(2)}) collective-permute-start(f32[256,1,256]{2,1,0:T(1,128)S(1)} %get-tuple-element.276), channel_id=1, source_target_pairs={{0,1},{1,2},{2,3},{3,4},{4,5},{5,6},{6,7},{8,9},{9,10},{10,11},{11... | collective-permute-start | bytes 786440 | tf_op jit(solution)/shard_map/ppermute | solution.py:20
  130.9 13.6 %collective-permute-start.13 = (f32[256,1,256]{2,1,0:T(1,128)S(1)}, f32[256,1,256]{2,1,0:T(1,128)S(1)}, u32[]{:S(2)}, u32[]{:S(2)}) collective-permute-start(f32[256,1,256]{2,1,0:T(1,128)S(1)} %get-tuple-element.265), channel_id=1, source_target_pairs={{1,0},{2,1},{3,2},{4,3},{5,4},{6,5},{7,6},{9,8},{10,9},{11,10},{12... | collective-permute-start | bytes 786440 | tf_op jit(solution)/shard_map/ppermute | solution.py:23
  133.2 14.3 %collective-permute-start.14 = (f32[256,1,256]{2,1,0:T(1,128)S(1)}, f32[256,1,256]{2,1,0:T(1,128)S(1)}, u32[]{:S(2)}, u32[]{:S(2)}) collective-permute-start(f32[256,1,256]{2,1,0:T(1,128)S(1)} %get-tuple-element.266), channel_id=1, source_target_pairs={{0,1},{1,2},{2,3},{3,4},{4,5},{5,6},{6,7},{8,9},{9,10},{10,11},{11... | collective-permute-start | bytes 786440 | tf_op jit(solution)/shard_map/ppermute | solution.py:20
  150.4 1.4 copy-start
  163.7 13.9 %collective-permute-start.15 = (f32[256,1,256]{2,1,0:T(1,128)}, f32[256,1,256]{2,1,0:T(1,128)S(1)}, u32[]{:S(2)}, u32[]{:S(2)}) collective-permute-start(f32[256,1,256]{2,1,0:T(1,128)} %get-tuple-element.259), channel_id=1, source_target_pairs={{1,0},{2,1},{3,2},{4,3},{5,4},{6,5},{7,6},{9,8},{10,9},{11,10},{12... | collective-permute-start | bytes 786440 | tf_op jit(solution)/shard_map/ppermute | solution.py:23
  165.7 14.9 %copy-start.2 = (f32[256,8,256]{2,1,0:T(8,128)S(1)}, f32[256,8,256]{2,1,0:T(8,128)}, u32[]{:S(2)}) copy-start(f32[256,8,256]{2,1,0:T(8,128)} %get-tuple-element.250) | copy-start | bytes 6291460
  165.7 14.9 %copy-start.4 = (f32[256,8,255]{2,1,0:T(8,128)S(1)}, f32[256,8,255]{2,1,0:T(8,128)}, u32[]{:S(2)}) copy-start(f32[256,8,255]{2,1,0:T(8,128)} %get-tuple-element.257) | copy-start | bytes 6266884
  165.7 14.9 %collective-permute-start.16 = (f32[256,1,256]{2,1,0:T(1,128)}, f32[256,1,256]{2,1,0:T(1,128)S(1)}, u32[]{:S(2)}, u32[]{:S(2)}) collective-permute-start(f32[256,1,256]{2,1,0:T(1,128)} %get-tuple-element.260), channel_id=1, source_target_pairs={{0,1},{1,2},{2,3},{3,4},{4,5},{5,6},{6,7},{8,9},{9,10},{10,11},{11... | collective-permute-start | bytes 786440 | tf_op jit(solution)/shard_map/ppermute | solution.py:20
  185.5 3.1 copy-start.3
  194.1 18.3 %copy-start.9 = (f32[256]{0:T(256)S(1)}, f32[256]{0:T(256)}, u32[]{:S(2)}) copy-start(f32[256]{0:T(256)} %param.21) | copy-start | bytes 3076
  271.3 19.6 %copy-start.5 = (f32[256,256]{1,0:T(8,128)S(1)}, f32[256,256]{1,0:T(8,128)}, u32[]{:S(2)}) copy-start(f32[256,256]{1,0:T(8,128)} %param.20) | copy-start | bytes 786436
  293.7 13.4 %collective-permute-start = (f32[770,256]{1,0:T(8,128)S(1)}, f32[770,256]{1,0:T(8,128)S(1)}, u32[]{:S(2)}, u32[]{:S(2)}) collective-permute-start(f32[770,256]{1,0:T(8,128)S(1)} %get-tuple-element.450), channel_id=1, source_target_pairs={{0,8},{8,16},{16,24},{1,9},{9,17},{17,25},{2,10},{10,18},{18,26},{... | collective-permute-start | bytes 2365448 | tf_op jit(solution)/shard_map/while/body/eval_jaxpr/ppermute | solution.py:31
  333.3 13.4 %collective-permute-start = (f32[770,256]{1,0:T(8,128)S(1)}, f32[770,256]{1,0:T(8,128)S(1)}, u32[]{:S(2)}, u32[]{:S(2)}) collective-permute-start(f32[770,256]{1,0:T(8,128)S(1)} %get-tuple-element.450), channel_id=1, source_target_pairs={{0,8},{8,16},{16,24},{1,9},{9,17},{17,25},{2,10},{10,18},{18,26},{... | collective-permute-start | bytes 2365448 | tf_op jit(solution)/shard_map/while/body/eval_jaxpr/ppermute | solution.py:31
  373.0 13.4 %collective-permute-start = (f32[770,256]{1,0:T(8,128)S(1)}, f32[770,256]{1,0:T(8,128)S(1)}, u32[]{:S(2)}, u32[]{:S(2)}) collective-permute-start(f32[770,256]{1,0:T(8,128)S(1)} %get-tuple-element.450), channel_id=1, source_target_pairs={{0,8},{8,16},{16,24},{1,9},{9,17},{17,25},{2,10},{10,18},{18,26},{... | collective-permute-start | bytes 2365448 | tf_op jit(solution)/shard_map/while/body/eval_jaxpr/ppermute | solution.py:31
  412.9 7.9 %copy-start.10 = (f32[1,256]{1,0:T(1,128)}, f32[1,256]{1,0:T(1,128)S(1)}, u32[]{:S(2)}) copy-start(f32[1,256]{1,0:T(1,128)S(1)} %slice.329) | copy-start | bytes 3076
  (2 other events, 2.6 us)
Sparse Core Ops, SparseCore 0:
  198.2 70.5 all-reduce.1
where the time goes:
time: 437 us; the launch traced here: 429 us
  waiting for transfers between devices  161 us (37%)
  matrix products  102 us (23%)
  starting transfers between devices  59.5 us (14%)
  local copies, waits for them, and re-layouts  37.3 us (9%)
  other arithmetic  33.6 us (8%)
  between operations  15.8 us (4%)
  blocking collectives  14.3 us (3%)
  loops' own time  5.6 us (1%)
    dot_general x191, matrix products, matmul_high(): return jnp.dot(left, right, precision=lax.Precision.HIGHEST)  94.3 us
    psum x1, waiting for transfers between devices, on_device(): gram_sum, rhs_sum = lax.psum((gram_part, rhs_part), 'tile')  56.3 us
    ppermute x8, waiting for transfers between devices, padded_2(): lax.ppermute(lax.slice_in_dim(block, 0, width, axis=dim), axis, backward)  40.1 us
    ppermute x8, starting transfers between devices, padded_2(): lax.ppermute(lax.slice_in_dim(block, block.shape[dim] - width, None, axis...  35.5 us
    ppermute x3, waiting for transfers between devices, from_behind(): return lax.ppermute(array, axis, pairs)  34.4 us
    ppermute x8, waiting for transfers between devices, padded_2(): lax.ppermute(lax.slice_in_dim(block, block.shape[dim] - width, None, axis...  29.8 us
    ppermute x8, starting transfers between devices, padded_2(): lax.ppermute(lax.slice_in_dim(block, 0, width, axis=dim), axis, backward)  18.1 us
    slice x16, local copies, waits for them, and re-layouts, diff_cols(): return jnp.roll(values, -1, axis=-1) - jnp.roll(values, 1, axis=-1)  14.6 us
  transfers between devices with their start and end apart: 20, of which 19 were waited for; matrix products, arithmetic and copies ran while one was open for 2% of the time, Pallas kernels for 0%

commit v1 on v0

v1 whole, which is shorter than its diff:
```python
import functools

import jax
import jax.numpy as jnp
from jax import lax
from jax.experimental import pallas as pl
from jax.experimental.pallas import tpu as pltpu
from jax.sharding import PartitionSpec as P

STEPS = 4
A_COEF = 0.5
B_COEF = 0.5
CORIOLIS = 0.3

F32 = jnp.float32
BF16 = jnp.bfloat16
LANES = 128
SUB = 8
REACH = 2 * STEPS
PADX = REACH + 1
FINE = 16
HIGH = lax.Precision.HIGHEST
NT = (((1,), (1,)), ((), ()))
NN = (((1,), (0,)), ((), ()))
TN = (((0,), (0,)), ((), ()))
VMEM = pl.BlockSpec(memory_space=pltpu.VMEM)
SMEM = pl.BlockSpec(memory_space=pltpu.SMEM)


def params(mib=60):
    return pltpu.CompilerParams(vmem_limit_bytes=mib << 20)


def dot6(left, right, dims=NN):
    return lax.dot_general(left, right, dims, precision=HIGH, preferred_element_type=F32)


def dot1(left, right, dims=NN):
    return lax.dot_general(left, right, dims, preferred_element_type=F32)


def halves(values):
    high = values.astype(BF16)
    return high, (values - high.astype(F32)).astype(BF16)


def thirds(values):
    high = values.astype(BF16)
    rest = values - high.astype(F32)
    mid = rest.astype(BF16)
    return high, mid, (rest - mid.astype(F32)).astype(BF16)


def dot3(left, right):
    (lh, ll), (rh, rl) = left, right
    return dot1(lh, rh) + (dot1(lh, rl) + dot1(ll, rh))


def window_rows(own_slot, rows, scal_ref, own_ref, first_ref, second_ref, obs_ref):
    even = scal_ref[0] == 0
    own = own_ref[0:rows, :] * B_COEF
    first = first_ref[0:rows, :] * B_COEF
    if own_slot:
        second = second_ref[0:rows, :] * B_COEF
        above = jnp.where(even, second, first)
        below = jnp.where(even, first, second)
        domain = jnp.concatenate([above[rows // 2 :], own, below[: rows // 2]], axis=0)
        base = rows // 2
    else:
        domain = jnp.concatenate(
            [jnp.where(even, own, first), jnp.where(even, first, own)], axis=0
        )
        base = jnp.where(even, rows, 0)
    return domain, base


def project_kernel(
    own_slot, rows, nx, scal_ref, own_ref, first_ref, second_ref, basis_ref, out_ref,
    bmw, p, g, qp, sp, w, sh, sl,
):
    obs_ref = own_ref if own_slot else first_ref
    domain, base = window_rows(
        own_slot, rows, scal_ref, own_ref, first_ref, second_ref, obs_ref
    )
    depth = 2 * rows
    nob = obs_ref.shape[1] // LANES
    inner = REACH - 2
    rolled = [
        pltpu.roll(domain, (-dx) % nx, 1) if dx else domain for dx in range(-inner, inner + 1)
    ]
    stacked = jnp.concatenate(rolled, axis=0)
    pieces = thirds(stacked)
    cells = obs_ref[rows : rows + 1, :]
    fields = obs_ref[rows + 1 : rows + 2, :]
    row_all = jnp.floor(cells * (1.0 / nx))
    col = (cells - row_all * nx).astype(jnp.int32)
    row = (row_all - rows * jnp.floor(row_all * (1.0 / rows))).astype(jnp.int32) + base
    field = fields.astype(jnp.int32)
    y_iota = lax.broadcasted_iota(jnp.int32, (depth, LANES), 0)
    x_iota = lax.broadcasted_iota(jnp.int32, (nx, LANES), 0)
    if own_slot:
        first_row = jnp.where(scal_ref[1] == 0, rows // 2, 0)
        last_row = jnp.where(scal_ref[1] == scal_ref[2] - 1, rows // 2 + rows, depth)
        inside = ((y_iota >= first_row) & (y_iota < last_row)).astype(F32)
    lo, hi = SUB, SUB + depth
    zero_rows = jnp.zeros((SUB, LANES), F32)
    for ob in range(nob):
        lane = slice(ob * LANES, (ob + 1) * LANES)
        onehot = (x_iota == col[:, lane]).astype(F32).astype(BF16)
        depths = dot1(pieces[0], onehot) + (dot1(pieces[1], onehot) + dot1(pieces[2], onehot))
        for i in range(2 * inner + 1):
            bmw[ob, i] = depths[i * depth : (i + 1) * depth]
        for i in range(2 * PADX + 1):
            g[ob, i, 0:lo] = zero_rows
            g[ob, i, hi : hi + SUB] = zero_rows
            sp[ob, i, 0:lo] = zero_rows
            sp[ob, i, hi : hi + SUB] = zero_rows
        at_row = y_iota == row[:, lane]
        start = [(at_row & (field[:, lane] == f)).astype(F32) for f in range(3)]

        def at(ref, dx):
            return ref[ob, dx + PADX, lo:hi]

        def slope(ref, dx):
            return ref[ob, dx + PADX, lo + 1 : hi + 1] - ref[ob, dx + PADX, lo - 1 : hi - 1]

        p[ob, PADX, lo:hi] = start[0]
        for step in range(STEPS):
            reach = 2 * step
            for dx in range(-reach, reach + 1):
                g[ob, dx + PADX, lo:hi] = bmw[ob, dx + inner] * at(p, dx)
            for dx in range(-reach - 1, reach + 2):
                if step == 0:
                    east, north = (start[1], start[2]) if dx == 0 else (None, None)
                elif abs(dx) <= reach - 2:
                    qv, sv = at(qp, dx), at(sp, dx)
                    east, north = qv - CORIOLIS * sv, sv + CORIOLIS * qv
                elif abs(dx) == reach - 1:
                    east = at(qp, dx)
                    north = CORIOLIS * east
                else:
                    east, north = None, None
                if abs(dx + 1) <= reach:
                    east = at(g, dx + 1) if east is None else east + at(g, dx + 1)
                if abs(dx - 1) <= reach:
                    east = -at(g, dx - 1) if east is None else east - at(g, dx - 1)
                qp[ob, dx + PADX, lo:hi] = east
                if abs(dx) <= reach:
                    rise = slope(g, dx)
                    north = rise if north is None else north + rise
                    if own_slot:
                        north = north * inside
                    sp[ob, dx + PADX, lo:hi] = north
            for dx in range(-reach - 2, reach + 3):
                change = None
                if abs(dx + 1) <= reach + 1:
                    change = at(qp, dx + 1)
                if abs(dx - 1) <= reach + 1:
                    change = -at(qp, dx - 1) if change is None else change - at(qp, dx - 1)
                if abs(dx) <= reach:
                    change = change + slope(sp, dx)
                change = A_COEF * change
                if abs(dx) <= reach:
                    change = change + at(p, dx)
                p[ob, dx + PADX, lo:hi] = change

        if own_slot:
            picked = slice(lo + rows // 2, lo + rows // 2 + rows)
        else:
            picked = pl.ds(pl.multiple_of(jnp.where(even_of(scal_ref), lo, lo + rows), SUB), rows)
        shift = lax.rem(col[:, lane] + (nx - REACH), nx)
        fine = jnp.broadcast_to(lax.rem(shift, FINE), (rows, LANES))
        bits = [(fine & (1 << i)) != 0 for i in range(4)]
        coarse = jnp.broadcast_to(shift // FINE, (FINE, LANES))
        blocks = nx // FINE
        marks = [(coarse == block).astype(F32).astype(BF16) for block in range(blocks)]
        zero = jnp.zeros((rows, LANES), F32)
        for f in range(3):
            values = [None] * (2 * FINE)
            for dx in range(-REACH, REACH + 1):
                if f == 0:
                    value = p[ob, dx + PADX, picked]
                elif abs(dx) <= REACH - 2:
                    qv, sv = qp[ob, dx + PADX, picked], sp[ob, dx + PADX, picked]
                    value = qv - CORIOLIS * sv if f == 1 else sv + CORIOLIS * qv
                elif abs(dx) == REACH - 1:
                    qv = qp[ob, dx + PADX, picked]
                    value = qv if f == 1 else CORIOLIS * qv
                else:
                    value = None
                values[dx + REACH] = value
            for i in range(4):
                moved = []
                for e in range(2 * FINE):
                    here = values[e]
                    there = values[e - (1 << i)] if e >= (1 << i) else None
                    if here is None and there is None:
                        moved.append(None)
                    else:
                        moved.append(
                            jnp.where(
                                bits[i],
                                zero if there is None else there,
                                zero if here is None else here,
                            )
                        )
                values = moved
            for e in range(2 * FINE):
                w[e * rows : (e + 1) * rows, :] = zero if values[e] is None else values[e]
            for y in range(rows):
                both = halves(w[pl.ds(y, 2 * FINE, stride=rows), :])
                for part, ref in zip(both, (sh, sl)):
                    near, far = part[:FINE], part[FINE:]
                    for block in range(blocks):
                        start_row = (f * rows + y) * nx + block * FINE
                        ref[start_row : start_row + FINE, lane] = (
                            near * marks[block] + far * marks[block - 1]
                        )
    out_ref[...] = dot1(basis_ref[...], sh[...]) + dot1(basis_ref[...], sl[...])


def even_of(scal_ref):
    return scal_ref[0] == 0


def project(own_slot, scal, own, first, second, basis, rows, nx):
    order, depth_all = basis.shape
    nobs = own.shape[1]
    nob = nobs // LANES
    wide = (nob, 2 * PADX + 1, 2 * rows + 2 * SUB, LANES)
    return pl.pallas_call(
        functools.partial(project_kernel, own_slot, rows, nx),
        out_shape=jax.ShapeDtypeStruct((order, nobs), F32),
        in_specs=[SMEM] + [VMEM] * 4,
        out_specs=VMEM,
        scratch_shapes=[
            pltpu.VMEM((nob, 2 * REACH - 3, 2 * rows, LANES), F32),
            pltpu.VMEM(wide, F32),
            pltpu.VMEM(wide, F32),
            pltpu.VMEM(wide, F32),
            pltpu.VMEM(wide, F32),
            pltpu.VMEM((2 * FINE * rows, LANES), F32),
            pltpu.VMEM((depth_all, nobs), BF16),
            pltpu.VMEM((depth_all, nobs), BF16),
        ],
        compiler_params=params(48),
        cost_estimate=pl.CostEstimate(
            flops=4 * order * depth_all * nobs,
            bytes_accessed=2 * order * depth_all,
            transcendentals=0,
        ),
        name="project_own" if own_slot else "project_partner",
    )(scal, own, first, second, basis)


def triangle_masks(half):
    rows = lax.broadcasted_iota(jnp.int32, (half, half), 0)
    cols = lax.broadcasted_iota(jnp.int32, (half, half), 1)
    return rows, cols


def store_packed(out_ref, matrix, vector):
    half = matrix.shape[0] // 2
    rows, cols = triangle_masks(half)
    corner = matrix[half:, half:]
    out_ref[0:half] = jnp.where(rows >= cols, matrix[:half, :half], corner)
    out_ref[half : 2 * half] = matrix[half:, :half]
    diagonal = jnp.sum(jnp.where(rows == cols, corner, 0.0), axis=0, keepdims=True)
    tail = jnp.concatenate(
        [vector[:, :half], vector[:, half:], diagonal, jnp.zeros((SUB - 3, half), F32)], axis=0
    )
    out_ref[2 * half : 2 * half + SUB] = tail


def load_packed(values):
    half = values.shape[1]
    rows, cols = triangle_masks(half)
    mixed = values[0:half]
    cross = values[half : 2 * half]
    vector = jnp.concatenate(
        [values[2 * half : 2 * half + 1], values[2 * half + 1 : 2 * half + 2]], axis=1
    )
    diagonal = values[2 * half + 2 : 2 * half + 3]
    turned = mixed.T
    first = jnp.where(rows >= cols, mixed, turned)
    last = jnp.where(rows == cols, diagonal, jnp.where(rows < cols, mixed, turned))
    top = jnp.concatenate([first, cross.T], axis=1)
    bottom = jnp.concatenate([cross, last], axis=1)
    return jnp.concatenate([top, bottom], axis=0), vector


def gram_kernel(own_ref, first_ref, second_ref, weight_ref, innovation_ref, out_ref):
    projected = own_ref[...] + first_ref[...] + second_ref[...]
    weight = weight_ref[...]
    gram = dot6(projected * weight, projected, NT)
    pulled = jnp.broadcast_to(weight * innovation_ref[...], (SUB, weight.shape[1]))
    rhs = dot6(pulled, projected, NT)[0:1]
    store_packed(out_ref, gram, rhs)


def gram(own, first, second, weight, innovation):
    order = own.shape[0]
    return pl.pallas_call(
        gram_kernel,
        out_shape=jax.ShapeDtypeStruct((order + SUB, order // 2), F32),
        in_specs=[VMEM] * 5,
        out_specs=VMEM,
        compiler_params=params(),
        name="gram",
    )(own, first, second, weight, innovation)


def identity_like(matrix):
    rows = lax.broadcasted_iota(jnp.int32, matrix.shape, 0)
    cols = lax.broadcasted_iota(jnp.int32, matrix.shape, 1)
    return (rows == cols).astype(F32)


def norm_of(matrix):
    size = jnp.abs(matrix)
    return jnp.minimum(jnp.max(jnp.sum(size, axis=0)), jnp.max(jnp.sum(size, axis=1)))


def invert_shifted(offdiags, refine, tol):
    eye = identity_like(offdiags[0])
    systems = [halves(eye + m) for m in offdiags]
    starts, errors = [], []
    for m in offdiags:
        bound = norm_of(m)
        alpha = 2.0 / (2.0 + bound)
        error = bound / (2.0 + bound)
        scale = 2.0 / (2.0 - error * error)
        starts.append((scale * alpha) * (2.0 * eye - alpha * (eye + m)))
        errors.append(error * error / (2.0 - error * error))

    def unfinished(state):
        return functools.reduce(jnp.maximum, state[1]) > tol

    def turn(state):
        estimates, errors = state
        new_estimates, new_errors = [], []
        for system, estimate, error in zip(systems, estimates, errors):
            parts = halves(estimate)
            residual = 2.0 * eye - dot3(system, parts)
            scale = 2.0 / (2.0 - error * error)
            new_estimates.append(scale * dot3(parts, halves(residual)))
            new_errors.append(error * error / (2.0 - error * error))
        return tuple(new_estimates), tuple(new_errors)

    estimates, errors = lax.while_loop(unfinished, turn, (tuple(starts), tuple(errors)))
    if not refine:
        return estimates
    bound = functools.reduce(jnp.maximum, [norm_of(m) for m in offdiags])
    turns = jnp.where(bound > 300.0, 4, 1)

    def polish(index, estimates):
        result = []
        for m, estimate in zip(offdiags, estimates):
            residual = eye - estimate - dot6(m, estimate)
            result.append(estimate + dot3(halves(estimate), halves(residual)))
        return tuple(result)

    return lax.fori_loop(0, turns, polish, estimates)


def times(matrix, row):
    return dot6(jnp.broadcast_to(row, (SUB, row.shape[1])), matrix, NT)[0:1]


def times_left(matrix, row):
    return dot6(jnp.broadcast_to(row, (SUB, row.shape[1])), matrix, NN)[0:1]


def column(row):
    size = row.shape[1]
    return jnp.broadcast_to(row, (size, size)).T


def pair_kernel(
    full, scal_ref, mine_ref, other_ref, transition_ref, model_error_ref,
    a_ref, j_ref, vec_ref, prefix_ref, *more,
):
    lower_core = scal_ref[0] == 0
    first_pair = scal_ref[1] == 0
    mine, other = mine_ref[...], other_ref[...]
    q2 = model_error_ref[...]
    root_row = jnp.sqrt(q2)
    root_col = column(root_row)
    q2_col = column(q2)
    transition = transition_ref[...]
    moves = [jnp.where(first_pair, 0.0, transition), transition]
    grams, rhss = [], []
    for packed in (jnp.where(lower_core, mine, other), jnp.where(lower_core, other, mine)):
        matrix, vector = load_packed(packed)
        grams.append(matrix)
        rhss.append(vector)
    precise = invert_shifted([root_col * m * root_row for m in grams], True, 2e-3)
    elements = []
    for inverse, rhs, move in zip(precise, rhss, moves):
        cov = root_col * inverse * root_row
        mean = times(cov, rhs)
        scaled = move / q2_col
        trans = dot6(cov, scaled)
        prec = dot6(scaled, move - trans, TN)
        info = times_left(scaled, mean)
        elements.append((trans, mean, cov, info, prec))
    (a1, b1, c1, eta1, j1), (a2, b2, c2, eta2, j2) = elements
    (inverse,) = invert_shifted([dot6(c1, j2)], True, 1e-3)
    outer = dot6(c1, a2, NT)
    spread = dot6(j2, a1)
    ahead = b1 + times(c1, eta2)
    behind = eta2 - times(j2, b1)
    scaled = dot6(a2, inverse)
    back = dot6(inverse, a1)
    cov = dot6(scaled, outer) + c2
    trans = dot6(scaled, a1)
    prec = dot6(back, spread, TN) + j1
    mean = times(scaled, ahead) + b2
    info = times_left(back, behind) + eta1
    a_ref[...] = jnp.where(lower_core, a1, trans)
    j_ref[...] = jnp.where(lower_core, j1, prec)
    vec_ref[0:1] = jnp.where(lower_core, b1, mean)
    vec_ref[1:2] = jnp.where(lower_core, eta1, info)
    vec_ref[2:3] = mean
    vec_ref[3:4] = info
    vec_ref[4:SUB] = jnp.zeros((SUB - 4, mean.shape[1]), F32)
    store_packed(prefix_ref, cov, mean)
    if full:
        for ref, value in zip(more, (trans, prec, cov)):
            ref[...] = value


def pair_up(scal, mine, other, transition, model_error, full):
    order = transition.shape[0]
    square = jax.ShapeDtypeStruct((order, order), F32)
    shapes = [
        square,
        square,
        jax.ShapeDtypeStruct((SUB, order), F32),
        jax.ShapeDtypeStruct(mine.shape, F32),
    ] + [square] * (3 if full else 0)
    return pl.pallas_call(
        functools.partial(pair_kernel, full),
        out_shape=shapes,
        in_specs=[SMEM] + [VMEM] * 4,
        out_specs=[VMEM] * len(shapes),
        compiler_params=params(),
        name="pair_up",
    )(scal, mine, other, transition, model_error)


def advance_kernel(incoming_ref, a_ref, j_ref, c_ref, vec_ref, out_ref):
    cov0, mean0 = load_packed(incoming_ref[...])
    (inverse,) = invert_shifted([dot6(cov0, j_ref[...])], True, 1e-3)
    scaled = dot6(a_ref[...], inverse)
    mean = times(scaled, mean0 + times(cov0, vec_ref[3:4])) + vec_ref[2:3]
    cov = dot6(scaled, dot6(cov0, a_ref[...], NT)) + c_ref[...]
    store_packed(out_ref, cov, mean)


def advance_prefix(incoming, a, j, c, vec):
    return pl.pallas_call(
        advance_kernel,
        out_shape=jax.ShapeDtypeStruct(incoming.shape, F32),
        in_specs=[VMEM] * 5,
        out_specs=VMEM,
        compiler_params=params(),
        name="advance_prefix",
    )(incoming, a, j, c, vec)


def finish_kernel(rows, nx, incoming_ref, a_ref, j_ref, vec_ref, basis_ref, mean_ref, sum_ref):
    cov0, mean0 = load_packed(incoming_ref[...])
    start = mean0 + times(cov0, vec_ref[1:2])
    middle = dot6(cov0, j_ref[...])
    (inverse,) = invert_shifted([middle], True, 1e-3)
    guess = times(inverse, start)
    guess = guess + times(inverse, start - guess - times(middle, guess))
    mean = times(a_ref[...], guess) + vec_ref[0:1]
    mean_ref[...] = mean
    pieces = jnp.concatenate(list(thirds(mean)) + [jnp.zeros((5, mean.shape[1]), BF16)], axis=0)
    sums = dot1(pieces, basis_ref[...])
    total = sums[0:1] + (sums[1:2] + sums[2:3])
    for i in range(3 * rows):
        sum_ref[i : i + 1, :] = total[:, i * nx : (i + 1) * nx]


def finish(incoming, a, j, vec, basis, rows, nx):
    order = a.shape[0]
    return pl.pallas_call(
        functools.partial(finish_kernel, rows, nx),
        out_shape=[
            jax.ShapeDtypeStruct((1, order), F32),
            jax.ShapeDtypeStruct((3 * rows, nx), F32),
        ],
        in_specs=[VMEM] * 5,
        out_specs=[VMEM] * 2,
        compiler_params=params(),
        name="finish",
    )(incoming, a, j, vec, basis)


def increments_kernel(rows, nx, scal_ref, own_ref, first_ref, second_ref, mo, mf, ms, out_ref):
    even = even_of(scal_ref)

    def extend(own, first, second):
        above = jnp.where(even, second, first)
        below = jnp.where(even, first, second)
        return jnp.concatenate([above, own, below], axis=0)

    depth = extend(mo[0:rows, :], mf[0:rows, :], ms[0:rows, :]) * B_COEF
    h, u, v = [
        extend(*(ref[f * rows : (f + 1) * rows, :] for ref in (own_ref, first_ref, second_ref)))
        for f in range(3)
    ]
    total = 3 * rows
    y_iota = lax.broadcasted_iota(jnp.int32, (total, nx), 0)
    first_row = jnp.where(scal_ref[1] == 0, rows, 0)
    last_row = jnp.where(scal_ref[1] == scal_ref[2] - 1, 2 * rows, total)
    inside = ((y_iota >= first_row) & (y_iota < last_row)).astype(F32)

    def diff_cols(values):
        return pltpu.roll(values, nx - 1, 1) - pltpu.roll(values, 1, 1)

    def diff_rows(values):
        return pltpu.roll(values, total - 1, 0) - pltpu.roll(values, 1, 0)

    for step in range(STEPS):
        east = u + CORIOLIS * v - A_COEF * diff_cols(h)
        north = (v - CORIOLIS * u - A_COEF * diff_rows(h)) * inside
        h = h - depth * (diff_cols(east) + diff_rows(north))
        u, v = east, north
    for f, values in enumerate((h, u, v)):
        out_ref[f] = values[rows : 2 * rows]


def propagate_sum(scal, own, first, second, mo, mf, ms, rows, nx):
    return pl.pallas_call(
        functools.partial(increments_kernel, rows, nx),
        out_shape=jax.ShapeDtypeStruct((3, rows, nx), F32),
        in_specs=[SMEM] + [VMEM] * 6,
        out_specs=VMEM,
        compiler_params=params(),
        name="propagate_sum",
    )(scal, own, first, second, mo, mf, ms)


def on_device(
    basis_fields, mean_depth, obs_cells, obs_fields, obs_weight, innovation, transition, model_error
):
    order, rows, nx = basis_fields.shape[2:]
    tiles = lax.axis_size("tile")
    windows = lax.axis_size("tm")
    tile = lax.axis_index("tile")
    window = lax.axis_index("tm")
    near = [(i, i ^ 1) for i in range(tiles)]
    far = [(i, i + 1) for i in range(1, tiles - 1, 2)]
    far = far + [(b, a) for a, b in far]
    scal = jnp.stack([tile % 2, tile, jnp.int32(tiles)]).astype(jnp.int32)
    scal_far = jnp.stack([1 - tile % 2, tile, jnp.int32(tiles)]).astype(jnp.int32)

    info = jnp.concatenate(
        [
            mean_depth,
            obs_cells.astype(F32),
            obs_fields.astype(F32),
            jnp.zeros((SUB - 2, nx), F32),
        ],
        axis=0,
    )
    info_near = lax.ppermute(info, "tile", near)
    info_far = lax.ppermute(info, "tile", far)
    basis = basis_fields[0].transpose(1, 0, 2, 3).reshape(order, 3 * rows * nx)

    part_near = project(False, scal, info, info_near, info_near, basis, rows, nx)
    got_near = lax.ppermute(part_near, "tile", near)
    part_far = project(False, scal_far, info, info_far, info_far, basis, rows, nx)
    got_far = lax.ppermute(part_far, "tile", far)
    part_own = project(True, scal, info, info_near, info_far, basis, rows, nx)

    packed = gram(part_own, got_near, got_far, obs_weight, innovation)
    bit = 1
    while bit < tiles:
        packed = packed + lax.ppermute(packed, "tile", [(i, i ^ bit) for i in range(tiles)])
        bit *= 2

    other = lax.ppermute(packed, "tm", [(i, i ^ 1) for i in range(windows)])
    pairs = windows // 2
    scal_tm = jnp.stack([window % 2, window // 2]).astype(jnp.int32)
    a, j, vec, prefix, *more = pair_up(
        scal_tm, packed, other, transition, model_error[None, :], pairs > 2
    )
    incoming = jnp.zeros_like(prefix)
    for turn in range(pairs - 1):
        incoming = lax.ppermute(prefix, "tm", [(i, i + 2) for i in range(windows - 2)])
        if turn < pairs - 2:
            longer = advance_prefix(incoming, *more, vec)
            prefix = jnp.where(window // 2 == turn + 1, longer, prefix)
    mean, sums = finish(incoming, a, j, vec, basis, rows, nx)
    sums_near = lax.ppermute(sums, "tile", near)
    sums_far = lax.ppermute(sums, "tile", far)
    result = propagate_sum(
        scal, sums, sums_near, sums_far, info, info_near, info_far, rows, nx
    )
    return mean, result[None]


def solution(mesh):
    return jax.shard_map(
        on_device,
        mesh=mesh,
        in_specs=(
            P("tm", None, None, "tile", None),
            P("tile", None),
            P("tm", "tile"),
            P("tm", "tile"),
            P("tm", "tile"),
            P("tm", "tile"),
            P(),
            P(),
        ),
        out_specs=(P("tm", None), P("tm", None, "tile", None)),
        check_vma=False,
    )
```

time: 437 us -> 96.2 us (0.22); the launches traced: 429 us -> 96.1 us
  waiting for transfers between devices: 161 us -> 28 us
  matrix products: 102 us -> 0 us
  starting transfers between devices: 59.5 us -> 18 us
  Pallas kernels: 0 us -> 38.9 us
  local copies, waits for them, and re-layouts: 37.3 us -> 6.46 us
  other arithmetic: 33.6 us -> 3.89 us
  between operations: 15.8 us -> 0.85 us
  blocking collectives: 14.3 us -> 0 us
  loops' own time: 5.6 us -> 0 us
    dot_general x192 -> x0, matrix products: 102 us -> none  [the longest x191 94.3 us: matmul_high(): return jnp.dot(left, right, precision=lax.Precision.HIGHEST)]
    ppermute x19 -> x11, waiting for transfers between devices: 104 us -> 28 us  [the longest x3 13.8 us: on_device(): lax.ppermute(packed, 'tile', [(i, i ^ bit) for i in range(tiles)])]
    psum x1 -> x0, waiting for transfers between devices: 56.3 us -> none  [on_device(): gram_sum, rhs_sum = lax.psum((gram_part, rhs_part), 'tile')]
    ppermute x19 -> x11, starting transfers between devices: 59.4 us -> 18 us  [the longest x1 4.65 us: on_device(): sums_far = lax.ppermute(sums, 'tile', far)]
    pallas_call x0 -> x7, Pallas kernels: none -> 38.9 us  [the longest x1 15.8 us: pair_up(): pl.pallas_call(functools.partial(pair_kernel, full), out_shape=shapes, in...]
    sub x11 -> x0, other arithmetic: 23.1 us -> none  [the longest x4 11.7 us: advance(): height - B_COEF * mean_depth * (diff_cols(east_new) + rimmed[:, 2:, :] -...]
    slice x28 -> x0, local copies, waits for them, and re-layouts: 21.3 us -> none  [the longest x16 14.6 us: diff_cols(): return jnp.roll(values, -1, axis=-1) - jnp.roll(values, 1, axis=-1)]
    psum x1 -> x0, blocking collectives: 14.3 us -> none  [on_device(): gram_sum, rhs_sum = lax.psum((gram_part, rhs_part), 'tile')]
  transfers between devices with their start and end apart: 20 -> 11, of which waited for: 19 -> 8; matrix products, arithmetic and copies ran while one was open for 2% -> 4% of each run, Pallas kernels for 0% -> 11%
where the time goes in v1:
time: 96.2 us; the launch traced here: 96.1 us
  Pallas kernels  38.9 us (40%)
  waiting for transfers between devices  28 us (29%)
  starting transfers between devices  18 us (19%)
  local copies, waits for them, and re-layouts  6.46 us (7%)
  other arithmetic  3.89 us (4%)
    pallas_call x1, Pallas kernels, pair_up(): pl.pallas_call(functools.partial(pair_kernel, full), out_shape=shapes, in...  15.8 us
    ppermute x3, waiting for transfers between devices, on_device(): lax.ppermute(packed, 'tile', [(i, i ^ bit) for i in range(tiles)])  13.8 us
    pallas_call x3, Pallas kernels, project(): pl.pallas_call(functools.partial(project_kernel, own_slot, rows, nx), out...  10.5 us
    pallas_call x1, Pallas kernels, finish(): pl.pallas_call(functools.partial(finish_kernel, rows, nx), out_shape=[jax...  8.28 us
    ppermute x1, waiting for transfers between devices, on_device(): lax.ppermute(prefix, 'tm', [(i, i + 2) for i in range(windows - 2)])  6.44 us
    ppermute x1, starting transfers between devices, on_device(): sums_far = lax.ppermute(sums, 'tile', far)  4.65 us
    ppermute x1, starting transfers between devices, on_device(): got_far = lax.ppermute(part_far, 'tile', far)  4.58 us
    unnamed x27, local copies, waits for them, and re-layouts  4.29 us
  transfers between devices with their start and end apart: 11, of which 8 were waited for; matrix products, arithmetic and copies ran while one was open for 4% of the time, Pallas kernels for 11%

profile of v1, /device:TPU:14, one launch (start us, length us, event | category | flops | bytes accessed | tf_op | source)
XLA Modules:
  0.0 96.1 jit_solution(12002402753200891716)
XLA Ops:
  0.6 0.7 convert_element_type.6
  1.3 0.7 convert_element_type.7
  2.1 0.8 maximum_maximum_fusion.own_ref.mo
  2.8 3.4 %collective-permute-start.1 = (f32[16,256]{1,0:T(8,128)S(1)}, f32[16,256]{1,0:T(8,128)S(1)}, u32[]{:S(2)}, u32[]{:S(2)}) collective-permute-start(f32[16,256]{1,0:T(8,128)S(1)} %maximum_maximum_fusion.own_ref.mo), channel_id=1, source_target_pairs={{1,2},{3,4},{5,6},{2,1},{4,3},{6,5},{9,10},{11,12},{13,14},{10,9},... | collective-permute-start | bytes 49160 | tf_op jit(solution)/shard_map/ppermute | solution.py:572
  6.9 2.1 %copy.10 = bf16[256,3,8,256]{3,2,1,0:T(8,128)(2,1)S(1)} copy(bf16[256,3,8,256]{3,2,0,1:T(8,128)(2,1)} %bitcast.18) | data formatting | bytes 6291456 | tf_op jit(solution)/shard_map/transpose | solution.py:573
  9.0 1.0 %copy.11 = bf16[32,8,24,256]{3,1,2,0:T(8,128)(2,1)S(1)} copy(bf16[32,8,24,256]{3,2,1,0:T(8,128)(2,1)S(1)} %bitcast.17) | data formatting | bytes 6291456
  10.0 3.5 %project_partner.3 = f32[256,256]{1,0:T(8,128)S(1)} custom-call(s32[3]{0:T(128)S(1)} %pad_add_fusion.scal_ref, f32[16,256]{1,0:T(8,128)S(1)} %maximum_maximum_fusion.own_ref.mo, f32[16,256]{1,0:T(8,128)S(1)} %collective-permute-done.1.second_ref.first_ref.ms, f32[16,256]{1,0:T(8,128)S(1)} %collective-permute-done.1.second_ref.first_ref.ms, ...), custom_call_target="tpu_custom_call" | custom-call | flops 1610612736 | bytes 3145728 | tf_op jit(solution)/shard_map/project_partner/pallas_call | solution.py:231
  13.5 4.6 %collective-permute-start.3 = (f32[256,256]{1,0:T(8,128)S(1)}, f32[256,256]{1,0:T(8,128)S(1)}, u32[]{:S(2)}, u32[]{:S(2)}) collective-permute-start(f32[256,256]{1,0:T(8,128)S(1)} %project_partner.3), channel_id=1, source_target_pairs={{1,2},{3,4},{5,6},{2,1},{4,3},{6,5},{9,10},{11,12},{13,14},{10,9},... | collective-permute-start | bytes 786440 | tf_op jit(solution)/shard_map/ppermute | solution.py:578
  18.1 3.5 %project_partner.2 = f32[256,256]{1,0:T(8,128)S(1)} custom-call(s32[3]{0:T(128)S(1)} %pad_add_fusion.1.scal_ref, f32[16,256]{1,0:T(8,128)S(1)} %maximum_maximum_fusion.own_ref.mo, f32[16,256]{1,0:T(8,128)S(1)} %collective-permute-done.first_ref.second_ref.mf, f32[16,256]{1,0:T(8,128)S(1)} %collective-permute-done.first_ref.second_ref.mf, ...), custom_call_target="tpu_custom_call" | custom-call | flops 1610612736 | bytes 3145728 | tf_op jit(solution)/shard_map/project_partner/pallas_call | solution.py:231
  21.7 3.5 %project_own.1.own_ref = f32[256,256]{1,0:T(8,128)S(1)} custom-call(s32[3]{0:T(128)S(1)} %pad_add_fusion.1.scal_ref, f32[16,256]{1,0:T(8,128)S(1)} %maximum_maximum_fusion.own_ref.mo, f32[16,256]{1,0:T(8,128)S(1)} %collective-permute-done.first_ref.second_ref.mf, f32[16,256]{1,0:T(8,128)S(1)} %collective-permute-done.1.second_ref.first_ref.ms, ...), custom_call_target="tpu_custom_call" | custom-call | flops 1610612736 | bytes 3145728 | tf_op jit(solution)/shard_map/project_own/pallas_call | solution.py:231
  25.3 0.7 copy-done.1
  26.0 3.5 %collective-permute-done.2.first_ref = f32[256,256]{1,0:T(8,128)S(1)} collective-permute-done((f32[256,256]{1,0:T(8,128)S(1)}, f32[256,256]{1,0:T(8,128)S(1)}, u32[]{:S(2)}, u32[]{:S(2)}) %collective-permute-start.2) | collective-permute-done | bytes 262176 | tf_op jit(solution)/shard_map/ppermute | solution.py:576
  29.4 0.7 copy-done.8
  30.1 2.4 %gram.1 = f32[264,128]{1,0:T(8,128)} custom-call(f32[256,256]{1,0:T(8,128)} %copy-done.1, f32[256,256]{1,0:T(8,128)} %copy-done.8, f32[256,256]{1,0:T(8,128)} %copy-done.7, f32[1,256]{1,0:T(1,128)} %weight_ref.1, f32[1,256]{1,0:T(1,128)} %innovation_ref.1), custom_call_target="tpu_custom_call" | custom-call | tf_op jit(solution)/shard_map/gram/pallas_call | solution.py:303
  32.5 1.6 %collective-permute-start.4 = (f32[264,128]{1,0:T(8,128)}, f32[264,128]{1,0:T(8,128)S(1)}, u32[]{:S(2)}, u32[]{:S(2)}) collective-permute-start(f32[264,128]{1,0:T(8,128)} %gram.1), channel_id=1, source_target_pairs={{0,1},{1,0},{2,3},{3,2},{4,5},{5,4},{6,7},{7,6},{8,9},{9,8},{10,11... | collective-permute-start | bytes 405512 | tf_op jit(solution)/shard_map/ppermute | solution.py:584
  34.1 4.0 %collective-permute-done.4 = f32[264,128]{1,0:T(8,128)S(1)} collective-permute-done((f32[264,128]{1,0:T(8,128)}, f32[264,128]{1,0:T(8,128)S(1)}, u32[]{:S(2)}, u32[]{:S(2)}) %collective-permute-start.4) | collective-permute-done | bytes 135200 | tf_op jit(solution)/shard_map/ppermute | solution.py:584
  38.1 0.9 add.20
  39.2 4.9 %collective-permute-done.5 = f32[264,128]{1,0:T(8,128)S(1)} collective-permute-done((f32[264,128]{1,0:T(8,128)S(1)}, f32[264,128]{1,0:T(8,128)S(1)}, u32[]{:S(2)}, u32[]{:S(2)}) %collective-permute-start.5) | collective-permute-done | bytes 135200 | tf_op jit(solution)/shard_map/ppermute | solution.py:584
  44.1 1.2 %collective-permute-start.6 = (f32[264,128]{1,0:T(8,128)S(1)}, f32[264,128]{1,0:T(8,128)S(1)}, u32[]{:S(2)}, u32[]{:S(2)}) collective-permute-start(f32[264,128]{1,0:T(8,128)S(1)} %add.21), channel_id=1, source_target_pairs={{0,4},{1,5},{2,6},{3,7},{4,0},{5,1},{6,2},{7,3},{8,12},{9,13},{10,... | collective-permute-start | bytes 405512 | tf_op jit(solution)/shard_map/ppermute | solution.py:584
  45.3 4.9 %collective-permute-done.6 = f32[264,128]{1,0:T(8,128)S(1)} collective-permute-done((f32[264,128]{1,0:T(8,128)S(1)}, f32[264,128]{1,0:T(8,128)S(1)}, u32[]{:S(2)}, u32[]{:S(2)}) %collective-permute-start.6) | collective-permute-done | bytes 135200 | tf_op jit(solution)/shard_map/ppermute | solution.py:584
  50.3 0.7 pad_add_fusion.2.scal_ref
  51.0 0.7 collective-permute-done.7.other_ref
  51.7 0.6 copy-done.10
  52.3 15.8 %pair_up.1 = (f32[256,256]{1,0:T(8,128)}, f32[256,256]{1,0:T(8,128)}, f32[8,256]{1,0:T(8,128)}, f32[264,128]{1,0:T(8,128)}) custom-call(s32[2]{0:T(128)} %pad_add_fusion.2.scal_ref, f32[264,128]{1,0:T(8,128)} %copy-done.6, f32[264,128]{1,0:T(8,128)} %copy-done.10, f32[256,256]{1,0:T(8,128)} %transition_ref.1, f32[1,256]{1,0:T(1,128)} %bitcast.20), custom_call_target="tpu_custom_call" | custom-call | tf_op jit(solution)/shard_map/pair_up/pallas_call | solution.py:442
  68.1 1.3 %collective-permute-start.8 = (f32[264,128]{1,0:T(8,128)}, f32[264,128]{1,0:T(8,128)S(1)}, u32[]{:S(2)}, u32[]{:S(2)}) collective-permute-start(f32[264,128]{1,0:T(8,128)} %get-tuple-element.8), channel_id=1, source_target_pairs={{0,16},{8,24},{1,17},{9,25},{2,18},{10,26},{3,19},{11,27},{4,20},{... | collective-permute-start | bytes 405512 | tf_op jit(solution)/shard_map/ppermute | solution.py:595
  69.4 6.4 %collective-permute-done.8.incoming_ref = f32[264,128]{1,0:T(8,128)S(1)} collective-permute-done((f32[264,128]{1,0:T(8,128)}, f32[264,128]{1,0:T(8,128)S(1)}, u32[]{:S(2)}, u32[]{:S(2)}) %collective-permute-start.8) | collective-permute-done | bytes 135200 | tf_op jit(solution)/shard_map/ppermute | solution.py:595
  75.8 0.6 copy-done.9
  76.5 8.3 %finish.1 = (f32[1,256]{1,0:T(1,128)}, f32[24,256]{1,0:T(8,128)}) custom-call(f32[264,128]{1,0:T(8,128)} %copy-done.9, f32[256,256]{1,0:T(8,128)} %get-tuple-element.9.a_ref, f32[256,256]{1,0:T(8,128)} %get-tuple-element.10.j_ref, f32[8,256]{1,0:T(8,128)} %get-tuple-element.11.vec_ref, bf16[256,6144]{1,0:T(8,128)(2,1)} %bitcast.16), custom_call_target="tpu_custom_call" | custom-call | tf_op jit(solution)/shard_map/finish/pallas_call | solution.py:490
  84.8 4.7 %collective-permute-start.10 = (f32[24,256]{1,0:T(8,128)}, f32[24,256]{1,0:T(8,128)S(1)}, u32[]{:S(2)}, u32[]{:S(2)}) collective-permute-start(f32[24,256]{1,0:T(8,128)} %get-tuple-element.13.own_ref), channel_id=1, source_target_pairs={{1,2},{3,4},{5,6},{2,1},{4,3},{6,5},{9,10},{11,12},{13,14},{10,9},... | collective-permute-start | bytes 73736 | tf_op jit(solution)/shard_map/ppermute | solution.py:601
  90.0 1.7 %collective-permute-done.10.second_ref = f32[24,256]{1,0:T(8,128)S(1)} collective-permute-done((f32[24,256]{1,0:T(8,128)}, f32[24,256]{1,0:T(8,128)S(1)}, u32[]{:S(2)}, u32[]{:S(2)}) %collective-permute-start.10) | collective-permute-done | bytes 24608 | tf_op jit(solution)/shard_map/ppermute | solution.py:601
  91.7 1.8 %collective-permute-done.9.first_ref = f32[24,256]{1,0:T(8,128)S(1)} collective-permute-done((f32[24,256]{1,0:T(8,128)}, f32[24,256]{1,0:T(8,128)S(1)}, u32[]{:S(2)}, u32[]{:S(2)}) %collective-permute-start.9) | collective-permute-done | bytes 24608 | tf_op jit(solution)/shard_map/ppermute | solution.py:600
  94.1 2.0 %propagate_sum.1 = f32[3,8,256]{2,1,0:T(8,128)} custom-call(s32[3]{0:T(128)} %copy-done.5, f32[24,256]{1,0:T(8,128)} %get-tuple-element.13.own_ref, f32[24,256]{1,0:T(8,128)} %copy-done.12, f32[24,256]{1,0:T(8,128)} %copy-done.11, f32[16,256]{1,0:T(8,128)} %copy-done.2, f32[16,256]{1,0:T(8,128)} %copy-done.4, f32[16,256]{1,0:T(8,128)} %copy-done.3), custom_call_target="tpu_custom_call" | custom-call | tf_op jit(solution)/shard_map/propagate_sum/pallas_call | solution.py:538
  (36 shorter events, 2.2 us)
Async XLA Ops:
  2.8 18.9 %copy-start.2 = (f32[16,256]{1,0:T(8,128)}, f32[16,256]{1,0:T(8,128)S(1)}, u32[]{:S(2)}) copy-start(f32[16,256]{1,0:T(8,128)S(1)} %maximum_maximum_fusion.own_ref.mo) | copy-start | bytes 49156
  2.8 7.1 %collective-permute-start.1 = (f32[16,256]{1,0:T(8,128)S(1)}, f32[16,256]{1,0:T(8,128)S(1)}, u32[]{:S(2)}, u32[]{:S(2)}) collective-permute-start(f32[16,256]{1,0:T(8,128)S(1)} %maximum_maximum_fusion.own_ref.mo), channel_id=1, source_target_pairs={{1,2},{3,4},{5,6},{2,1},{4,3},{6,5},{9,10},{11,12},{13,14},{10,9},... | collective-permute-start | bytes 49160 | tf_op jit(solution)/shard_map/ppermute | solution.py:572
  6.3 11.8 %collective-permute-start = (f32[16,256]{1,0:T(8,128)S(1)}, f32[16,256]{1,0:T(8,128)S(1)}, u32[]{:S(2)}, u32[]{:S(2)}) collective-permute-start(f32[16,256]{1,0:T(8,128)S(1)} %maximum_maximum_fusion.own_ref.mo), channel_id=1, source_target_pairs={{0,1},{1,0},{2,3},{3,2},{4,5},{5,4},{6,7},{7,6},{8,9},{9,8},{10,11... | collective-permute-start | bytes 49160 | tf_op jit(solution)/shard_map/ppermute | solution.py:571
  6.9 14.8 %copy-start.5 = (s32[3]{0:T(128)}, s32[3]{0:T(128)S(1)}, u32[]{:S(2)}) copy-start(s32[3]{0:T(128)S(1)} %pad_add_fusion.1.scal_ref) | copy-start | bytes 40
  10.0 11.8 %copy-start = (bf16[32,8,24,256]{3,1,2,0:T(8,128)(2,1)}, bf16[32,8,24,256]{3,1,2,0:T(8,128)(2,1)S(1)}, u32[]{:S(2)}) copy-start(bf16[32,8,24,256]{3,1,2,0:T(8,128)(2,1)S(1)} %copy.11) | copy-start | bytes 9437188
  10.0 11.7 %copy-start.3 = (f32[16,256]{1,0:T(8,128)}, f32[16,256]{1,0:T(8,128)S(1)}, u32[]{:S(2)}) copy-start(f32[16,256]{1,0:T(8,128)S(1)} %collective-permute-done.1.second_ref.first_ref.ms) | copy-start | bytes 49156
  13.5 12.4 %collective-permute-start.3 = (f32[256,256]{1,0:T(8,128)S(1)}, f32[256,256]{1,0:T(8,128)S(1)}, u32[]{:S(2)}, u32[]{:S(2)}) collective-permute-start(f32[256,256]{1,0:T(8,128)S(1)} %project_partner.3), channel_id=1, source_target_pairs={{1,2},{3,4},{5,6},{2,1},{4,3},{6,5},{9,10},{11,12},{13,14},{10,9},... | collective-permute-start | bytes 786440 | tf_op jit(solution)/shard_map/ppermute | solution.py:578
  18.1 7.1 %copy-start.4 = (f32[16,256]{1,0:T(8,128)}, f32[16,256]{1,0:T(8,128)S(1)}, u32[]{:S(2)}) copy-start(f32[16,256]{1,0:T(8,128)S(1)} %collective-permute-done.first_ref.second_ref.mf) | copy-start | bytes 49156
  21.6 7.8 %collective-permute-start.2 = (f32[256,256]{1,0:T(8,128)S(1)}, f32[256,256]{1,0:T(8,128)S(1)}, u32[]{:S(2)}, u32[]{:S(2)}) collective-permute-start(f32[256,256]{1,0:T(8,128)S(1)} %project_partner.2), channel_id=1, source_target_pairs={{0,1},{1,0},{2,3},{3,2},{4,5},{5,4},{6,7},{7,6},{8,9},{9,8},{10,11... | collective-permute-start | bytes 786440 | tf_op jit(solution)/shard_map/ppermute | solution.py:576
  25.3 0.7 copy-start.1
  26.0 3.5 %copy-start.7 = (f32[256,256]{1,0:T(8,128)}, f32[256,256]{1,0:T(8,128)S(1)}, u32[]{:S(2)}) copy-start(f32[256,256]{1,0:T(8,128)S(1)} %collective-permute-done.3.second_ref) | copy-start | bytes 786436
  29.4 0.7 copy-start.8
  32.5 5.6 %collective-permute-start.4 = (f32[264,128]{1,0:T(8,128)}, f32[264,128]{1,0:T(8,128)S(1)}, u32[]{:S(2)}, u32[]{:S(2)}) collective-permute-start(f32[264,128]{1,0:T(8,128)} %gram.1), channel_id=1, source_target_pairs={{0,1},{1,0},{2,3},{3,2},{4,5},{5,4},{6,7},{7,6},{8,9},{9,8},{10,11... | collective-permute-start | bytes 405512 | tf_op jit(solution)/shard_map/ppermute | solution.py:584
  39.0 5.1 %collective-permute-start.5 = (f32[264,128]{1,0:T(8,128)S(1)}, f32[264,128]{1,0:T(8,128)S(1)}, u32[]{:S(2)}, u32[]{:S(2)}) collective-permute-start(f32[264,128]{1,0:T(8,128)S(1)} %add.20), channel_id=1, source_target_pairs={{0,2},{1,3},{2,0},{3,1},{4,6},{5,7},{6,4},{7,5},{8,10},{9,11},{10,... | collective-permute-start | bytes 405512 | tf_op jit(solution)/shard_map/ppermute | solution.py:584
  44.1 6.1 %collective-permute-start.6 = (f32[264,128]{1,0:T(8,128)S(1)}, f32[264,128]{1,0:T(8,128)S(1)}, u32[]{:S(2)}, u32[]{:S(2)}) collective-permute-start(f32[264,128]{1,0:T(8,128)S(1)} %add.21), channel_id=1, source_target_pairs={{0,4},{1,5},{2,6},{3,7},{4,0},{5,1},{6,2},{7,3},{8,12},{9,13},{10,... | collective-permute-start | bytes 405512 | tf_op jit(solution)/shard_map/ppermute | solution.py:584
  50.2 1.4 %copy-start.6 = (f32[264,128]{1,0:T(8,128)}, f32[264,128]{1,0:T(8,128)S(1)}, u32[]{:S(2)}) copy-start(f32[264,128]{1,0:T(8,128)S(1)} %add.22.mine_ref) | copy-start | bytes 405508
  50.2 1.4 %collective-permute-start.7 = (f32[264,128]{1,0:T(8,128)S(1)}, f32[264,128]{1,0:T(8,128)S(1)}, u32[]{:S(2)}, u32[]{:S(2)}) collective-permute-start(f32[264,128]{1,0:T(8,128)S(1)} %add.22.mine_ref), channel_id=1, source_target_pairs={{0,8},{8,0},{16,24},{24,16},{1,9},{9,1},{17,25},{25,17},{2,10},{10... | collective-permute-start | bytes 405512 | tf_op jit(solution)/shard_map/ppermute | solution.py:587
  51.7 0.6 copy-start.10
  68.1 7.7 %collective-permute-start.8 = (f32[264,128]{1,0:T(8,128)}, f32[264,128]{1,0:T(8,128)S(1)}, u32[]{:S(2)}, u32[]{:S(2)}) collective-permute-start(f32[264,128]{1,0:T(8,128)} %get-tuple-element.8), channel_id=1, source_target_pairs={{0,16},{8,24},{1,17},{9,25},{2,18},{10,26},{3,19},{11,27},{4,20},{... | collective-permute-start | bytes 405512 | tf_op jit(solution)/shard_map/ppermute | solution.py:595
  75.8 0.7 copy-start.9
  84.8 6.9 %collective-permute-start.10 = (f32[24,256]{1,0:T(8,128)}, f32[24,256]{1,0:T(8,128)S(1)}, u32[]{:S(2)}, u32[]{:S(2)}) collective-permute-start(f32[24,256]{1,0:T(8,128)} %get-tuple-element.13.own_ref), channel_id=1, source_target_pairs={{1,2},{3,4},{5,6},{2,1},{4,3},{6,5},{9,10},{11,12},{13,14},{10,9},... | collective-permute-start | bytes 73736 | tf_op jit(solution)/shard_map/ppermute | solution.py:601
  89.4 4.1 %collective-permute-start.9 = (f32[24,256]{1,0:T(8,128)}, f32[24,256]{1,0:T(8,128)S(1)}, u32[]{:S(2)}, u32[]{:S(2)}) collective-permute-start(f32[24,256]{1,0:T(8,128)} %get-tuple-element.13.own_ref), channel_id=1, source_target_pairs={{0,1},{1,0},{2,3},{3,2},{4,5},{5,4},{6,7},{7,6},{8,9},{9,8},{10,11... | collective-permute-start | bytes 73736 | tf_op jit(solution)/shard_map/ppermute | solution.py:600
  91.7 1.8 %copy-start.11 = (f32[24,256]{1,0:T(8,128)}, f32[24,256]{1,0:T(8,128)S(1)}, u32[]{:S(2)}) copy-start(f32[24,256]{1,0:T(8,128)S(1)} %collective-permute-done.10.second_ref) | copy-start | bytes 73732
  93.5 0.6 copy-start.12

commit v2 on v1

--- a/solution.py
+++ b/solution.py
@@ -18,16 +18,16 @@
 SUB = 8
 REACH = 2 * STEPS
 PADX = REACH + 1
+NEAR, FAR, OWN = "project_near", "project_far", "project_own"
 FINE = 16
 HIGH = lax.Precision.HIGHEST
 NT = (((1,), (1,)), ((), ()))
 NN = (((1,), (0,)), ((), ()))
 TN = (((0,), (0,)), ((), ()))
 VMEM = pl.BlockSpec(memory_space=pltpu.VMEM)
-SMEM = pl.BlockSpec(memory_space=pltpu.SMEM)
-
-
-def params(mib=60):
+
+
+def params(mib):
     return pltpu.CompilerParams(vmem_limit_bytes=mib << 20)
 
 
@@ -51,19 +51,25 @@
     return high, mid, (rest - mid.astype(F32)).astype(BF16)
 
 
-def dot3(left, right):
+def dot3(left, right, dims=NN):
     (lh, ll), (rh, rl) = left, right
-    return dot1(lh, rh) + (dot1(lh, rl) + dot1(ll, rh))
-
-
-def window_rows(own_slot, rows, scal_ref, own_ref, first_ref, second_ref, obs_ref):
-    even = scal_ref[0] == 0
+    return dot1(lh, rh, dims) + (dot1(lh, rl, dims) + dot1(ll, rh, dims))
+
+
+def before_after(first, second):
+    tile, tiles = lax.axis_index("tile"), lax.axis_size("tile")
+    even = lax.rem(tile, 2) == 0
+    before = jnp.where(even, jnp.where(tile == 0, 0.0, second), first)
+    after = jnp.where(even, first, jnp.where(tile == tiles - 1, 0.0, second))
+    return before, after
+
+
+def window_rows(slot, rows, even, own_ref, first_ref, second_ref):
     own = own_ref[0:rows, :] * B_COEF
     first = first_ref[0:rows, :] * B_COEF
-    if own_slot:
+    if slot == OWN:
         second = second_ref[0:rows, :] * B_COEF
-        above = jnp.where(even, second, first)
-        below = jnp.where(even, first, second)
+        above, below = before_after(first, second)
         domain = jnp.concatenate([above[rows // 2 :], own, below[: rows // 2]], axis=0)
         base = rows // 2
     else:
@@ -75,13 +81,14 @@
 
 
 def project_kernel(
-    own_slot, rows, nx, scal_ref, own_ref, first_ref, second_ref, basis_ref, out_ref,
+    slot, rows, nx, own_ref, first_ref, second_ref, basis_ref, out_ref,
     bmw, p, g, qp, sp, w, sh, sl,
 ):
+    own_slot = slot == OWN
     obs_ref = own_ref if own_slot else first_ref
-    domain, base = window_rows(
-        own_slot, rows, scal_ref, own_ref, first_ref, second_ref, obs_ref
-    )
+    tile, tiles = lax.axis_index("tile"), lax.axis_size("tile")
+    even = lax.rem(tile, 2) == (1 if slot == FAR else 0)
+    domain, base = window_rows(slot, rows, even, own_ref, first_ref, second_ref)
     depth = 2 * rows
     nob = obs_ref.shape[1] // LANES
     inner = REACH - 2
@@ -99,8 +106,8 @@
     y_iota = lax.broadcasted_iota(jnp.int32, (depth, LANES), 0)
     x_iota = lax.broadcasted_iota(jnp.int32, (nx, LANES), 0)
     if own_slot:
-        first_row = jnp.where(scal_ref[1] == 0, rows // 2, 0)
-        last_row = jnp.where(scal_ref[1] == scal_ref[2] - 1, rows // 2 + rows, depth)
+        first_row = jnp.where(tile == 0, rows // 2, 0)
+        last_row = jnp.where(tile == tiles - 1, rows // 2 + rows, depth)
         inside = ((y_iota >= first_row) & (y_iota < last_row)).astype(F32)
     lo, hi = SUB, SUB + depth
     zero_rows = jnp.zeros((SUB, LANES), F32)
@@ -167,7 +174,7 @@
         if own_slot:
             picked = slice(lo + rows // 2, lo + rows // 2 + rows)
         else:
-            picked = pl.ds(pl.multiple_of(jnp.where(even_of(scal_ref), lo, lo + rows), SUB), rows)
+            picked = pl.ds(pl.multiple_of(jnp.where(even, lo, lo + rows), SUB), rows)
         shift = lax.rem(col[:, lane] + (nx - REACH), nx)
         fine = jnp.broadcast_to(lax.rem(shift, FINE), (rows, LANES))
         bits = [(fine & (1 << i)) != 0 for i in range(4)]
@@ -219,19 +226,15 @@
     out_ref[...] = dot1(basis_ref[...], sh[...]) + dot1(basis_ref[...], sl[...])
 
 
-def even_of(scal_ref):
-    return scal_ref[0] == 0
-
-
-def project(own_slot, scal, own, first, second, basis, rows, nx):
+def project(slot, own, first, second, basis, rows, nx):
     order, depth_all = basis.shape
     nobs = own.shape[1]
     nob = nobs // LANES
     wide = (nob, 2 * PADX + 1, 2 * rows + 2 * SUB, LANES)
     return pl.pallas_call(
-        functools.partial(project_kernel, own_slot, rows, nx),
+        functools.partial(project_kernel, slot, rows, nx),
         out_shape=jax.ShapeDtypeStruct((order, nobs), F32),
-        in_specs=[SMEM] + [VMEM] * 4,
+        in_specs=[VMEM] * 4,
         out_specs=VMEM,
         scratch_shapes=[
             pltpu.VMEM((nob, 2 * REACH - 3, 2 * rows, LANES), F32),
@@ -249,8 +252,8 @@
             bytes_accessed=2 * order * depth_all,
             transcendentals=0,
         ),
-        name="project_own" if own_slot else "project_partner",
-    )(scal, own, first, second, basis)
+        name=slot,
+    )(own, first, second, basis)
 
 
 def triangle_masks(half):
@@ -289,13 +292,19 @@
     return jnp.concatenate([top, bottom], axis=0), vector
 
 
+def with_row(matrix, row):
+    return jnp.concatenate([matrix, jnp.broadcast_to(row, (SUB, row.shape[1]))], axis=0)
+
+
 def gram_kernel(own_ref, first_ref, second_ref, weight_ref, innovation_ref, out_ref):
-    projected = own_ref[...] + first_ref[...] + second_ref[...]
+    tile, tiles = lax.axis_index("tile"), lax.axis_size("tile")
+    inner = (tile != 0) & (tile != tiles - 1)
+    projected = own_ref[...] + first_ref[...] + jnp.where(inner, second_ref[...], 0.0)
     weight = weight_ref[...]
-    gram = dot6(projected * weight, projected, NT)
-    pulled = jnp.broadcast_to(weight * innovation_ref[...], (SUB, weight.shape[1]))
-    rhs = dot6(pulled, projected, NT)[0:1]
-    store_packed(out_ref, gram, rhs)
+    left = with_row(projected * weight, weight * innovation_ref[...])
+    result = dot3(halves(left), halves(projected), NT)
+    size = projected.shape[0]
+    store_packed(out_ref, result[:size], result[size : size + 1])
 
 
 def gram(own, first, second, weight, innovation):
@@ -305,7 +314,7 @@
         out_shape=jax.ShapeDtypeStruct((order + SUB, order // 2), F32),
         in_specs=[VMEM] * 5,
         out_specs=VMEM,
-        compiler_params=params(),
+        compiler_params=params(8),
         name="gram",
     )(own, first, second, weight, innovation)
 
@@ -317,58 +326,77 @@
 
 
 def norm_of(matrix):
-    size = jnp.abs(matrix)
-    return jnp.minimum(jnp.max(jnp.sum(size, axis=0)), jnp.max(jnp.sum(size, axis=1)))
-
-
-def invert_shifted(offdiags, refine, tol):
-    eye = identity_like(offdiags[0])
-    systems = [halves(eye + m) for m in offdiags]
-    starts, errors = [], []
-    for m in offdiags:
-        bound = norm_of(m)
-        alpha = 2.0 / (2.0 + bound)
-        error = bound / (2.0 + bound)
-        scale = 2.0 / (2.0 - error * error)
-        starts.append((scale * alpha) * (2.0 * eye - alpha * (eye + m)))
-        errors.append(error * error / (2.0 - error * error))
+    return jnp.max(jnp.sum(jnp.abs(matrix), axis=0, keepdims=True))
+
+
+def scaled(error):
+    square = error * error
+    return 2.0 / (2.0 - square), square / (2.0 - square)
+
+
+def newton_start(matrix, row, eye):
+    size = matrix.shape[0]
+    parts = halves(matrix)
+    extended = with_row(matrix, row)
+    squares = dot3(halves(extended), parts)
+    square, row_moved = squares[:size], squares[size:]
+    bound = jnp.sqrt(norm_of(square))
+    alpha = 2.0 / (2.0 + bound)
+    error0 = bound / (2.0 + bound)
+    rho0, error1 = scaled(error0)
+    rho1, error2 = scaled(error1)
+    rest = 1.0 - alpha
+    first = (rho0 * alpha) * ((2.0 - alpha) * eye - alpha * matrix)
+    first_row = (rho0 * alpha) * ((2.0 - alpha) * row - alpha * row_moved)
+    squared = (rest * rest) * eye - (2.0 * rest * alpha) * matrix + (alpha * alpha) * square
+    residual = rho0 * squared + (1.0 - error1) * eye
+    estimate = rho1 * dot3(
+        halves(jnp.concatenate([first, first_row], axis=0)), halves(residual)
+    )
+    return estimate, error2, bound
+
+
+def newton(matrices, rows, tol, eye):
+    size = eye.shape[0]
+    starts = [newton_start(m, r, eye) for m, r in zip(matrices, rows)]
+    systems = [halves(eye + m) for m in matrices]
 
     def unfinished(state):
         return functools.reduce(jnp.maximum, state[1]) > tol
 
     def turn(state):
-        estimates, errors = state
         new_estimates, new_errors = [], []
-        for system, estimate, error in zip(systems, estimates, errors):
+        for system, estimate, error in zip(systems, *state):
             parts = halves(estimate)
-            residual = 2.0 * eye - dot3(system, parts)
-            scale = 2.0 / (2.0 - error * error)
-            new_estimates.append(scale * dot3(parts, halves(residual)))
-            new_errors.append(error * error / (2.0 - error * error))
+            residual = 2.0 * eye - dot3(system, tuple(part[:size] for part in parts))
+            rho, error = scaled(error)
+            new_estimates.append(rho * dot3(parts, halves(residual)))
+            new_errors.append(error)
         return tuple(new_estimates), tuple(new_errors)
 
-    estimates, errors = lax.while_loop(unfinished, turn, (tuple(starts), tuple(errors)))
-    if not refine:
-        return estimates
-    bound = functools.reduce(jnp.maximum, [norm_of(m) for m in offdiags])
+    state = tuple(s[0] for s in starts), tuple(s[1] for s in starts)
+    estimates, unused = lax.while_loop(unfinished, turn, state)
+    return estimates, functools.reduce(jnp.maximum, [s[2] for s in starts])
+
+
+def invert_shifted(matrices, rows):
+    eye = identity_like(matrices[0])
+    size = eye.shape[0]
+    estimates, bound = newton(matrices, rows, 0.03, eye)
     turns = jnp.where(bound > 300.0, 4, 1)
 
     def polish(index, estimates):
         result = []
-        for m, estimate in zip(offdiags, estimates):
-            residual = eye - estimate - dot6(m, estimate)
-            result.append(estimate + dot3(halves(estimate), halves(residual)))
+        for m, estimate in zip(matrices, estimates):
+            inverse = estimate[:size]
+            residual = eye - inverse - dot6(m, inverse)
+            rough = residual.astype(BF16)
+            change = residual + dot1(rough, rough)
+            result.append(estimate + dot3(halves(estimate), halves(change)))
         return tuple(result)
 
-    return lax.fori_loop(0, turns, polish, estimates)
-
-
-def times(matrix, row):
-    return dot6(jnp.broadcast_to(row, (SUB, row.shape[1])), matrix, NT)[0:1]
-
-
-def times_left(matrix, row):
-    return dot6(jnp.broadcast_to(row, (SUB, row.shape[1])), matrix, NN)[0:1]
+    estimates = lax.fori_loop(0, turns, polish, estimates)
+    return [(e[:size], e[size : size + 1]) for e in estimates]
 
 
 def column(row):
@@ -377,60 +405,64 @@
 
 
 def pair_kernel(
-    full, scal_ref, mine_ref, other_ref, transition_ref, model_error_ref,
+    full, mine_ref, other_ref, transition_ref, model_error_ref,
     a_ref, j_ref, vec_ref, prefix_ref, *more,
 ):
-    lower_core = scal_ref[0] == 0
-    first_pair = scal_ref[1] == 0
+    window = lax.axis_index("tm")
+    lower_core = lax.rem(window, 2) == 0
+    moves = jnp.where(window < 2, 0.0, 1.0)
     mine, other = mine_ref[...], other_ref[...]
     q2 = model_error_ref[...]
+    size = q2.shape[1]
     root_row = jnp.sqrt(q2)
     root_col = column(root_row)
-    q2_col = column(q2)
     transition = transition_ref[...]
-    moves = [jnp.where(first_pair, 0.0, transition), transition]
-    grams, rhss = [], []
+    weighted = transition / column(q2)
+    turned = halves(weighted.T)
+    weighted = halves(weighted)
+    mats, rows = [], []
     for packed in (jnp.where(lower_core, mine, other), jnp.where(lower_core, other, mine)):
         matrix, vector = load_packed(packed)
-        grams.append(matrix)
-        rhss.append(vector)
-    precise = invert_shifted([root_col * m * root_row for m in grams], True, 2e-3)
-    elements = []
-    for inverse, rhs, move in zip(precise, rhss, moves):
-        cov = root_col * inverse * root_row
-        mean = times(cov, rhs)
-        scaled = move / q2_col
-        trans = dot6(cov, scaled)
-        prec = dot6(scaled, move - trans, TN)
-        info = times_left(scaled, mean)
-        elements.append((trans, mean, cov, info, prec))
-    (a1, b1, c1, eta1, j1), (a2, b2, c2, eta2, j2) = elements
-    (inverse,) = invert_shifted([dot6(c1, j2)], True, 1e-3)
-    outer = dot6(c1, a2, NT)
-    spread = dot6(j2, a1)
-    ahead = b1 + times(c1, eta2)
-    behind = eta2 - times(j2, b1)
-    scaled = dot6(a2, inverse)
-    back = dot6(inverse, a1)
-    cov = dot6(scaled, outer) + c2
-    trans = dot6(scaled, a1)
-    prec = dot6(back, spread, TN) + j1
-    mean = times(scaled, ahead) + b2
-    info = times_left(back, behind) + eta1
+        mats.append(root_col * matrix * root_row)
+        rows.append(root_row * vector)
+    (p1, r1), (p2, r2) = invert_shifted(mats, rows)
+    c1, b1 = root_col * p1 * root_row, r1 * root_row
+    c2, b2 = root_col * p2 * root_row, r2 * root_row
+    low = halves(with_row(c1, b1))
+    a1 = moves * dot3(low, weighted)
+    a2 = dot3(halves(with_row(c2, b2)), weighted)
+    k1 = dot3(low, turned)
+    a1, eta1 = a1[:size], a1[size : size + 1]
+    a2, eta2 = a2[:size], a2[size : size + 1]
+    rest2 = halves(transition - a2)
+    crossed = dot3(halves(k1), rest2)
+    j2 = dot3(turned, rest2)
+    j1 = moves * dot3(turned, halves(transition - a1))
+    outer = dot3(low, halves(a2), NT)
+    spread = dot3(halves(a1.T), halves(j2))
+    ((inverse, s),) = invert_shifted([crossed[:size]], [eta2 - crossed[size : size + 1]])
+    both = jnp.concatenate([a1, outer[:size]], axis=1)
+    middle = dot3(halves(with_row(inverse, s)), halves(both))
+    right = halves(middle[:size])
+    ended = dot3(halves(a2), right)
+    trans, cov = ended[:, :size], ended[:, size:] + c2
+    prec = dot3(halves(spread), tuple(part[:, :size] for part in right)) + j1
+    info = middle[size : size + 1, :size] + eta1
+    mean = outer[size : size + 1] + middle[size : size + 1, size:] + b2
     a_ref[...] = jnp.where(lower_core, a1, trans)
     j_ref[...] = jnp.where(lower_core, j1, prec)
     vec_ref[0:1] = jnp.where(lower_core, b1, mean)
     vec_ref[1:2] = jnp.where(lower_core, eta1, info)
     vec_ref[2:3] = mean
     vec_ref[3:4] = info
-    vec_ref[4:SUB] = jnp.zeros((SUB - 4, mean.shape[1]), F32)
+    vec_ref[4:SUB] = jnp.zeros((SUB - 4, size), F32)
     store_packed(prefix_ref, cov, mean)
     if full:
         for ref, value in zip(more, (trans, prec, cov)):
             ref[...] = value
 
 
-def pair_up(scal, mine, other, transition, model_error, full):
+def pair_up(mine, other, transition, model_error, full):
     order = transition.shape[0]
     square = jax.ShapeDtypeStruct((order, order), F32)
     shapes = [
@@ -442,19 +474,25 @@
     return pl.pallas_call(
         functools.partial(pair_kernel, full),
         out_shape=shapes,
-        in_specs=[SMEM] + [VMEM] * 4,
+        in_specs=[VMEM] * 4,
         out_specs=[VMEM] * len(shapes),
-        compiler_params=params(),
+        compiler_params=params(24),
         name="pair_up",
-    )(scal, mine, other, transition, model_error)
+    )(mine, other, transition, model_error)
 
 
 def advance_kernel(incoming_ref, a_ref, j_ref, c_ref, vec_ref, out_ref):
     cov0, mean0 = load_packed(incoming_ref[...])
-    (inverse,) = invert_shifted([dot6(cov0, j_ref[...])], True, 1e-3)
-    scaled = dot6(a_ref[...], inverse)
-    mean = times(scaled, mean0 + times(cov0, vec_ref[3:4])) + vec_ref[2:3]
-    cov = dot6(scaled, dot6(cov0, a_ref[...], NT)) + c_ref[...]
+    size = mean0.shape[1]
+    low = halves(with_row(cov0, mean0))
+    crossed = dot3(low, halves(j_ref[...]))
+    outer = dot3(low, halves(a_ref[...]), NT)
+    ((inverse, s),) = invert_shifted(
+        [crossed[:size]], [vec_ref[3:4] - crossed[size : size + 1]]
+    )
+    middle = dot3(halves(with_row(inverse, s)), halves(outer[:size]))
+    mean = outer[size : size + 1] + middle[size : size + 1] + vec_ref[2:3]
+    cov = dot3(halves(a_ref[...]), halves(middle[:size])) + c_ref[...]
     store_packed(out_ref, cov, mean)
 
 
@@ -464,21 +502,32 @@
         out_shape=jax.ShapeDtypeStruct(incoming.shape, F32),
         in_specs=[VMEM] * 5,
         out_specs=VMEM,
-        compiler_params=params(),
+        compiler_params=params(16),
         name="advance_prefix",
     )(incoming, a, j, c, vec)
 
 
 def finish_kernel(rows, nx, incoming_ref, a_ref, j_ref, vec_ref, basis_ref, mean_ref, sum_ref):
-    cov0, mean0 = load_packed(incoming_ref[...])
-    start = mean0 + times(cov0, vec_ref[1:2])
-    middle = dot6(cov0, j_ref[...])
-    (inverse,) = invert_shifted([middle], True, 1e-3)
-    guess = times(inverse, start)
-    guess = guess + times(inverse, start - guess - times(middle, guess))
-    mean = times(a_ref[...], guess) + vec_ref[0:1]
+    moves = jnp.where(lax.axis_index("tm") < 2, 0.0, 1.0)
+    cov0, mean0 = load_packed(incoming_ref[...] * moves)
+    size = mean0.shape[1]
+    eye = identity_like(cov0)
+    crossed = dot3(halves(with_row(cov0, mean0)), halves(j_ref[...]))
+    matrix = crossed[:size]
+    target = jnp.broadcast_to(vec_ref[1:2], (SUB, size)) - crossed[size:]
+    (estimate,), bound = newton([matrix], [target[0:1]], 0.03, eye)
+    parts = halves(matrix)
+    inverse = halves(estimate[:size])
+
+    def polish(index, s):
+        miss = target - s - dot3(halves(s), parts)
+        return s + dot3(halves(miss), inverse)
+
+    s = lax.fori_loop(0, jnp.where(bound > 300.0, 8, 3), polish, estimate[size:])
+    ahead = mean0 + dot3(halves(s), halves(cov0))
+    mean = (dot3(halves(ahead), halves(a_ref[...]), NT) + vec_ref[0:1])[0:1]
     mean_ref[...] = mean
-    pieces = jnp.concatenate(list(thirds(mean)) + [jnp.zeros((5, mean.shape[1]), BF16)], axis=0)
+    pieces = jnp.concatenate(list(thirds(mean)) + [jnp.zeros((5, size), BF16)], axis=0)
     sums = dot1(pieces, basis_ref[...])
     total = sums[0:1] + (sums[1:2] + sums[2:3])
     for i in range(3 * rows):
@@ -495,18 +544,17 @@
         ],
         in_specs=[VMEM] * 5,
         out_specs=[VMEM] * 2,
-        compiler_params=params(),
+        compiler_params=params(16),
         name="finish",
     )(incoming, a, j, vec, basis)
 
 
-def increments_kernel(rows, nx, scal_ref, own_ref, first_ref, second_ref, mo, mf, ms, out_ref):
-    even = even_of(scal_ref)
+def increments_kernel(rows, nx, own_ref, first_ref, second_ref, mo, mf, ms, out_ref):
+    tile, tiles = lax.axis_index("tile"), lax.axis_size("tile")
 
     def extend(own, first, second):
-        above = jnp.where(even, second, first)
-        below = jnp.where(even, first, second)
-        return jnp.concatenate([above, own, below], axis=0)
+        before, after = before_after(first, second)
+        return jnp.concatenate([before, own, after], axis=0)
 
     depth = extend(mo[0:rows, :], mf[0:rows, :], ms[0:rows, :]) * B_COEF
     h, u, v = [
@@ -515,8 +563,8 @@
     ]
     total = 3 * rows
     y_iota = lax.broadcasted_iota(jnp.int32, (total, nx), 0)
-    first_row = jnp.where(scal_ref[1] == 0, rows, 0)
-    last_row = jnp.where(scal_ref[1] == scal_ref[2] - 1, 2 * rows, total)
+    first_row = jnp.where(tile == 0, rows, 0)
+    last_row = jnp.where(tile == tiles - 1, 2 * rows, total)
     inside = ((y_iota >= first_row) & (y_iota < last_row)).astype(F32)
 
     def diff_cols(values):
@@ -534,15 +582,35 @@
         out_ref[f] = values[rows : 2 * rows]
 
 
-def propagate_sum(scal, own, first, second, mo, mf, ms, rows, nx):
+def propagate_sum(own, first, second, mo, mf, ms, rows, nx):
     return pl.pallas_call(
         functools.partial(increments_kernel, rows, nx),
         out_shape=jax.ShapeDtypeStruct((3, rows, nx), F32),
-        in_specs=[SMEM] + [VMEM] * 6,
+        in_specs=[VMEM] * 6,
         out_specs=VMEM,
-        compiler_params=params(),
+        compiler_params=params(8),
         name="propagate_sum",
-    )(scal, own, first, second, mo, mf, ms)
+    )(own, first, second, mo, mf, ms)
+
+
+def info_kernel(depth_ref, cells_ref, fields_ref, out_ref):
+    rows = depth_ref.shape[0]
+    out_ref[0:rows, :] = depth_ref[...]
+    out_ref[rows : 2 * rows, :] = jnp.zeros_like(depth_ref)
+    out_ref[rows : rows + 1, :] = cells_ref[...].astype(F32)
+    out_ref[rows + 1 : rows + 2, :] = fields_ref[...].astype(F32)
+
+
+def gather_info(mean_depth, obs_cells, obs_fields):
+    rows, nx = mean_depth.shape
+    return pl.pallas_call(
+        info_kernel,
+        out_shape=jax.ShapeDtypeStruct((2 * rows, nx), F32),
+        in_specs=[VMEM] * 3,
+        out_specs=VMEM,
+        compiler_params=params(4),
+        name="gather_info",
+    )(mean_depth, obs_cells, obs_fields)
 
 
 def on_device(
@@ -551,32 +619,31 @@
     order, rows, nx = basis_fields.shape[2:]
     tiles = lax.axis_size("tile")
     windows = lax.axis_size("tm")
-    tile = lax.axis_index("tile")
-    window = lax.axis_index("tm")
     near = [(i, i ^ 1) for i in range(tiles)]
-    far = [(i, i + 1) for i in range(1, tiles - 1, 2)]
-    far = far + [(b, a) for a, b in far]
-    scal = jnp.stack([tile % 2, tile, jnp.int32(tiles)]).astype(jnp.int32)
-    scal_far = jnp.stack([1 - tile % 2, tile, jnp.int32(tiles)]).astype(jnp.int32)
-
-    info = jnp.concatenate(
-        [
-            mean_depth,
-            obs_cells.astype(F32),
-            obs_fields.astype(F32),
-            jnp.zeros((SUB - 2, nx), F32),
-        ],
-        axis=0,
-    )
-    info_near = lax.ppermute(info, "tile", near)
-    info_far = lax.ppermute(info, "tile", far)
+    across = [i if i in (0, tiles - 1) else (i + 1 if i % 2 else i - 1) for i in range(tiles)]
+    far = [
+        (w * tiles + i, (w ^ 1 if across[i] == i else w) * tiles + across[i])
+        for w in range(windows)
+        for i in range(tiles)
+    ]
+
+    def swap_near(array):
+        return lax.ppermute(array, "tile", near)
+
+    def swap_far(array):
+        return lax.ppermute(array, ("tm", "tile"), far)
+
+    info = gather_info(mean_depth, obs_cells, obs_fields)
+    info_near = swap_near(info)
     basis = basis_fields[0].transpose(1, 0, 2, 3).reshape(order, 3 * rows * nx)
-
-    part_near = project(False, scal, info, info_near, info_near, basis, rows, nx)
-    got_near = lax.ppermute(part_near, "tile", near)
-    part_far = project(False, scal_far, info, info_far, info_far, basis, rows, nx)
-    got_far = lax.ppermute(part_far, "tile", far)
-    part_own = project(True, scal, info, info_near, info_far, basis, rows, nx)
+    info_later, basis = lax.optimization_barrier((info, basis))
+    info_far = swap_far(info_later)
+
+    part_near = project(NEAR, info, info_near, info_near, basis, rows, nx)
+    got_near = swap_near(part_near)
+    part_far = project(FAR, info, info_far, info_far, basis, rows, nx)
+    got_far = swap_far(part_far)
+    part_own = project(OWN, info, info_near, info_far, basis, rows, nx)
 
     packed = gram(part_own, got_near, got_far, obs_weight, innovation)
     bit = 1
@@ -586,21 +653,23 @@
 
     other = lax.ppermute(packed, "tm", [(i, i ^ 1) for i in range(windows)])
     pairs = windows // 2
-    scal_tm = jnp.stack([window % 2, window // 2]).astype(jnp.int32)
     a, j, vec, prefix, *more = pair_up(
-        scal_tm, packed, other, transition, model_error[None, :], pairs > 2
+        packed, other, transition, model_error[None, :], pairs > 2
     )
     incoming = jnp.zeros_like(prefix)
+    pair = lax.axis_index("tm") // 2
     for turn in range(pairs - 1):
-        incoming = lax.ppermute(prefix, "tm", [(i, i + 2) for i in range(windows - 2)])
+        if pairs == 2:
+            hop = [(i, i ^ 2) for i in range(windows)]
+        else:
+            hop = [(i, i + 2) for i in range(windows - 2)]
+        incoming = lax.ppermute(prefix, "tm", hop)
         if turn < pairs - 2:
             longer = advance_prefix(incoming, *more, vec)
-            prefix = jnp.where(window // 2 == turn + 1, longer, prefix)
+            prefix = jnp.where(pair == turn + 1, longer, prefix)
     mean, sums = finish(incoming, a, j, vec, basis, rows, nx)
-    sums_near = lax.ppermute(sums, "tile", near)
-    sums_far = lax.ppermute(sums, "tile", far)
     result = propagate_sum(
-        scal, sums, sums_near, sums_far, info, info_near, info_far, rows, nx
+        sums, swap_near(sums), swap_far(sums), info, info_near, info_far, rows, nx
     )
     return mean, result[None]
 

time: 96.2 us -> 70.7 us (0.73)
  the two profiles are of different devices: /device:TPU:14 before, /device:TPU:0 now
where the time goes in v2:
time: 70.7 us; the launch traced here: 70.6 us
  Pallas kernels  23.7 us (34%)
  waiting for transfers between devices  21.9 us (31%)
  starting transfers between devices  21 us (30%)
  local copies, waits for them, and re-layouts  3.12 us (4%)
  between operations  0.82 us (1%)
    ppermute x3, waiting for transfers between devices, on_device(): lax.ppermute(packed, 'tile', [(i, i ^ bit) for i in range(tiles)])  11.1 us
    ppermute x3, starting transfers between devices, swap_near(): return lax.ppermute(array, 'tile', near)  11 us
    pallas_call x1, Pallas kernels, pair_up(): pl.pallas_call(functools.partial(pair_kernel, full), out_shape=shapes, in...  9.96 us
    pallas_call x3, Pallas kernels, project(): pl.pallas_call(functools.partial(project_kernel, slot, rows, nx), out_sha...  8.69 us
    ppermute x3, starting transfers between devices, on_device(): lax.ppermute(packed, 'tile', [(i, i ^ bit) for i in range(tiles)])  7.73 us
    ppermute x3, waiting for transfers between devices, swap_near(): return lax.ppermute(array, 'tile', near)  5.24 us
    ppermute x1, waiting for transfers between devices, on_device(): incoming = lax.ppermute(prefix, 'tm', hop)  4.16 us
    pallas_call x1, Pallas kernels, finish(): pl.pallas_call(functools.partial(finish_kernel, rows, nx), out_shape=[jax...  3.52 us
  transfers between devices with their start and end apart: 11, of which 7 were waited for; matrix products, arithmetic and copies ran while one was open for 0% of the time, Pallas kernels for 12%

profile of v2, /device:TPU:0, one launch (start us, length us, event | category | flops | bytes accessed | tf_op | source)
XLA Modules:
  0.0 70.6 jit_solution(6695869009993636657)
XLA Ops:
  0.6 2.1 %copy.10 = bf16[256,3,8,256]{3,2,1,0:T(8,128)(2,1)S(1)} copy(bf16[256,3,8,256]{3,2,0,1:T(8,128)(2,1)} %bitcast.14) | data formatting | bytes 6291456 | tf_op jit(solution)/shard_map/transpose | solution.py:638
  2.7 0.0 copy-start.1
  2.7 0.0 copy-start.5
  2.7 0.0 copy-start.6
  2.8 1.0 %copy.11 = bf16[32,8,24,256]{3,1,2,0:T(8,128)(2,1)S(1)} copy(bf16[32,8,24,256]{3,2,1,0:T(8,128)(2,1)S(1)} %bitcast.13) | data formatting | bytes 6291456
  3.8 0.6 collective-permute-start.1
  4.3 4.0 %collective-permute-start = (f32[16,256]{1,0:T(8,128)S(1)}, f32[16,256]{1,0:T(8,128)S(1)}, u32[]{:S(2)}, u32[]{:S(2)}) collective-permute-start(f32[16,256]{1,0:T(8,128)S(1)} %gather_info.1.own_ref.mo), channel_id=1, source_target_pairs={{0,1},{1,0},{2,3},{3,2},{4,5},{5,4},{6,7},{7,6},{8,9},{9,8},{10,11... | collective-permute-start | bytes 49160 | tf_op jit(solution)/shard_map/ppermute | solution.py:631
  8.4 2.9 %project_far.1 = f32[256,256]{1,0:T(8,128)S(1)} custom-call(f32[16,256]{1,0:T(8,128)S(1)} %gather_info.1.own_ref.mo, f32[16,256]{1,0:T(8,128)S(1)} %collective-permute-done.1.second_ref.first_ref.ms, f32[16,256]{1,0:T(8,128)S(1)} %collective-permute-done.1.second_ref.first_ref.ms, bf16[256,6144]{1,0:T(8,128)(2,1)S(1)} %bitcast.8), custom_call_target="tpu_custom_call" | custom-call | flops 1610612736 | bytes 3145728 | tf_op jit(solution)/shard_map/project_far/pallas_call | solution.py:234
  11.3 0.1 collective-permute-start.3
  11.4 2.9 %project_near.1 = f32[256,256]{1,0:T(8,128)S(1)} custom-call(f32[16,256]{1,0:T(8,128)S(1)} %gather_info.1.own_ref.mo, f32[16,256]{1,0:T(8,128)S(1)} %collective-permute-done.first_ref.second_ref.mf, f32[16,256]{1,0:T(8,128)S(1)} %collective-permute-done.first_ref.second_ref.mf, bf16[256,6144]{1,0:T(8,128)(2,1)S(1)} %bitcast.9), custom_call_target="tpu_custom_call" | custom-call | flops 1610612736 | bytes 3145728 | tf_op jit(solution)/shard_map/project_near/pallas_call | solution.py:234
  14.3 0.0 copy-start
  14.3 0.0 copy-start.4
  14.3 4.7 %collective-permute-start.2 = (f32[256,256]{1,0:T(8,128)S(1)}, f32[256,256]{1,0:T(8,128)S(1)}, u32[]{:S(2)}, u32[]{:S(2)}) collective-permute-start(f32[256,256]{1,0:T(8,128)S(1)} %project_near.1), channel_id=1, source_target_pairs={{0,1},{1,0},{2,3},{3,2},{4,5},{5,4},{6,7},{7,6},{8,9},{9,8},{10,11... | collective-permute-start | bytes 786440 | tf_op jit(solution)/shard_map/ppermute | solution.py:631
  19.0 2.9 %project_own.1.own_ref = f32[256,256]{1,0:T(8,128)S(1)} custom-call(f32[16,256]{1,0:T(8,128)S(1)} %gather_info.1.own_ref.mo, f32[16,256]{1,0:T(8,128)S(1)} %collective-permute-done.first_ref.second_ref.mf, f32[16,256]{1,0:T(8,128)S(1)} %collective-permute-done.1.second_ref.first_ref.ms, bf16[256,6144]{1,0:T(8,128)(2,1)S(1)} %bitcast.10), custom_call_target="tpu_custom_call" | custom-call | flops 1610612736 | bytes 3145728 | tf_op jit(solution)/shard_map/project_own/pallas_call | solution.py:234
  21.9 3.4 %collective-permute-done.2.first_ref = f32[256,256]{1,0:T(8,128)S(1)} collective-permute-done((f32[256,256]{1,0:T(8,128)S(1)}, f32[256,256]{1,0:T(8,128)S(1)}, u32[]{:S(2)}, u32[]{:S(2)}) %collective-permute-start.2) | collective-permute-done | bytes 262176 | tf_op jit(solution)/shard_map/ppermute | solution.py:631
  25.4 0.4 gram.1
  25.7 2.5 %collective-permute-start.4 = (f32[264,128]{1,0:T(8,128)S(1)}, f32[264,128]{1,0:T(8,128)S(1)}, u32[]{:S(2)}, u32[]{:S(2)}) collective-permute-start(f32[264,128]{1,0:T(8,128)S(1)} %gram.1), channel_id=1, source_target_pairs={{0,1},{1,0},{2,3},{3,2},{4,5},{5,4},{6,7},{7,6},{8,9},{9,8},{10,11... | collective-permute-start | bytes 405512 | tf_op jit(solution)/shard_map/ppermute | solution.py:651
  28.3 3.5 %collective-permute-done.4 = f32[264,128]{1,0:T(8,128)S(1)} collective-permute-done((f32[264,128]{1,0:T(8,128)S(1)}, f32[264,128]{1,0:T(8,128)S(1)}, u32[]{:S(2)}, u32[]{:S(2)}) %collective-permute-start.4) | collective-permute-done | bytes 135200 | tf_op jit(solution)/shard_map/ppermute | solution.py:651
  31.8 2.1 %collective-permute-start.5 = (f32[264,128]{1,0:T(8,128)S(1)}, f32[264,128]{1,0:T(8,128)S(1)}, u32[]{:S(2)}, u32[]{:S(2)}) collective-permute-start(f32[264,128]{1,0:T(8,128)S(1)} %add.9), channel_id=1, source_target_pairs={{0,2},{1,3},{2,0},{3,1},{4,6},{5,7},{6,4},{7,5},{8,10},{9,11},{10,... | collective-permute-start | bytes 405512 | tf_op jit(solution)/shard_map/ppermute | solution.py:651
  33.9 3.0 %collective-permute-done.5 = f32[264,128]{1,0:T(8,128)S(1)} collective-permute-done((f32[264,128]{1,0:T(8,128)S(1)}, f32[264,128]{1,0:T(8,128)S(1)}, u32[]{:S(2)}, u32[]{:S(2)}) %collective-permute-start.5) | collective-permute-done | bytes 135200 | tf_op jit(solution)/shard_map/ppermute | solution.py:651
  36.9 3.1 %collective-permute-start.6 = (f32[264,128]{1,0:T(8,128)S(1)}, f32[264,128]{1,0:T(8,128)S(1)}, u32[]{:S(2)}, u32[]{:S(2)}) collective-permute-start(f32[264,128]{1,0:T(8,128)S(1)} %add.10), channel_id=1, source_target_pairs={{0,4},{1,5},{2,6},{3,7},{4,0},{5,1},{6,2},{7,3},{8,12},{9,13},{10,... | collective-permute-start | bytes 405512 | tf_op jit(solution)/shard_map/ppermute | solution.py:651
  40.0 4.6 %collective-permute-done.6 = f32[264,128]{1,0:T(8,128)S(1)} collective-permute-done((f32[264,128]{1,0:T(8,128)S(1)}, f32[264,128]{1,0:T(8,128)S(1)}, u32[]{:S(2)}, u32[]{:S(2)}) %collective-permute-start.6) | collective-permute-done | bytes 135200 | tf_op jit(solution)/shard_map/ppermute | solution.py:651
  44.6 0.1 collective-permute-start.7
  44.7 1.3 %collective-permute-done.7.other_ref = f32[264,128]{1,0:T(8,128)S(1)} collective-permute-done((f32[264,128]{1,0:T(8,128)S(1)}, f32[264,128]{1,0:T(8,128)S(1)}, u32[]{:S(2)}, u32[]{:S(2)}) %collective-permute-start.7) | collective-permute-done | bytes 135200 | tf_op jit(solution)/shard_map/ppermute | solution.py:654
  46.1 10.0 %pair_up.1 = (f32[256,256]{1,0:T(8,128)S(1)}, f32[256,256]{1,0:T(8,128)S(1)}, f32[8,256]{1,0:T(8,128)S(1)}, f32[264,128]{1,0:T(8,128)S(1)}) custom-call(f32[264,128]{1,0:T(8,128)S(1)} %add.11.mine_ref, f32[264,128]{1,0:T(8,128)S(1)} %collective-permute-done.7.other_ref, f32[256,256]{1,0:T(8,128)S(1)} %copy-done, f32[1,256]{1,0:T(1,128)S(1)} %bitcast.12), custom_call_target="tpu_custom_call" | custom-call | tf_op jit(solution)/shard_map/pair_up/pallas_call | solution.py:474
  56.0 1.5 %collective-permute-start.8 = (f32[264,128]{1,0:T(8,128)S(1)}, f32[264,128]{1,0:T(8,128)S(1)}, u32[]{:S(2)}, u32[]{:S(2)}) collective-permute-start(f32[264,128]{1,0:T(8,128)S(1)} %get-tuple-element.12), channel_id=1, source_target_pairs={{0,16},{8,24},{16,0},{24,8},{1,17},{9,25},{17,1},{25,9},{2,18},{10... | collective-permute-start | bytes 405512 | tf_op jit(solution)/shard_map/ppermute | solution.py:666
  57.6 4.2 %collective-permute-done.8.incoming_ref = f32[264,128]{1,0:T(8,128)S(1)} collective-permute-done((f32[264,128]{1,0:T(8,128)S(1)}, f32[264,128]{1,0:T(8,128)S(1)}, u32[]{:S(2)}, u32[]{:S(2)}) %collective-permute-start.8) | collective-permute-done | bytes 135200 | tf_op jit(solution)/shard_map/ppermute | solution.py:666
  61.7 3.5 %finish.1 = (f32[1,256]{1,0:T(1,128)}, f32[24,256]{1,0:T(8,128)S(1)}) custom-call(f32[264,128]{1,0:T(8,128)S(1)} %collective-permute-done.8.incoming_ref, f32[256,256]{1,0:T(8,128)S(1)} %get-tuple-element.13.a_ref, f32[256,256]{1,0:T(8,128)S(1)} %get-tuple-element.14.j_ref, f32[8,256]{1,0:T(8,128)S(1)} %get-tuple-element.15.vec_ref, ...), custom_call_target="tpu_custom_call" | custom-call | tf_op jit(solution)/shard_map/finish/pallas_call | solution.py:539
  65.3 0.0 collective-permute-start.10
  65.3 2.3 %collective-permute-start.9 = (f32[24,256]{1,0:T(8,128)S(1)}, f32[24,256]{1,0:T(8,128)S(1)}, u32[]{:S(2)}, u32[]{:S(2)}) collective-permute-start(f32[24,256]{1,0:T(8,128)S(1)} %get-tuple-element.17.own_ref), channel_id=1, source_target_pairs={{0,1},{1,0},{2,3},{3,2},{4,5},{5,4},{6,7},{7,6},{8,9},{9,8},{10,11... | collective-permute-start | bytes 73736 | tf_op jit(solution)/shard_map/ppermute | solution.py:631
  67.6 1.8 %collective-permute-done.9.first_ref = f32[24,256]{1,0:T(8,128)S(1)} collective-permute-done((f32[24,256]{1,0:T(8,128)S(1)}, f32[24,256]{1,0:T(8,128)S(1)}, u32[]{:S(2)}, u32[]{:S(2)}) %collective-permute-start.9) | collective-permute-done | bytes 24608 | tf_op jit(solution)/shard_map/ppermute | solution.py:631
  69.4 1.2 %propagate_sum.1 = f32[3,8,256]{2,1,0:T(8,128)} custom-call(f32[24,256]{1,0:T(8,128)S(1)} %get-tuple-element.17.own_ref, f32[24,256]{1,0:T(8,128)S(1)} %collective-permute-done.9.first_ref, f32[24,256]{1,0:T(8,128)S(1)} %collective-permute-done.10.second_ref, f32[16,256]{1,0:T(8,128)S(1)} %gather_info.1.own_ref.mo, ...), custom_call_target="tpu_custom_call" | custom-call | tf_op jit(solution)/shard_map/propagate_sum/pallas_call | solution.py:586
  (17 shorter events, 0.1 us)
Async XLA Ops:
  2.7 1.0 %copy-start.1 = (f32[8,256]{1,0:T(8,128)S(1)}, f32[8,256]{1,0:T(8,128)}, u32[]{:S(2)}) copy-start(f32[8,256]{1,0:T(8,128)} %depth_ref.1) | copy-start | bytes 24580
  2.7 1.0 %copy-start.5 = (s32[1,256]{1,0:T(1,128)S(1)}, s32[1,256]{1,0:T(1,128)}, u32[]{:S(2)}) copy-start(s32[1,256]{1,0:T(1,128)} %cells_ref.1) | copy-start | bytes 3076
  2.7 1.0 %copy-start.6 = (s32[1,256]{1,0:T(1,128)S(1)}, s32[1,256]{1,0:T(1,128)}, u32[]{:S(2)}) copy-start(s32[1,256]{1,0:T(1,128)} %fields_ref.1) | copy-start | bytes 3076
  3.8 4.6 %collective-permute-start.1 = (f32[16,256]{1,0:T(8,128)S(1)}, f32[16,256]{1,0:T(8,128)S(1)}, u32[]{:S(2)}, u32[]{:S(2)}) collective-permute-start(f32[16,256]{1,0:T(8,128)S(1)} %gather_info.1.own_ref.mo), channel_id=1, source_target_pairs={{0,8},{1,2},{2,1},{3,4},{4,3},{5,6},{6,5},{7,15},{8,0},{9,10},{10,... | collective-permute-start | bytes 49160 | tf_op jit(solution)/shard_map/ppermute | solution.py:634
  4.3 7.0 %collective-permute-start = (f32[16,256]{1,0:T(8,128)S(1)}, f32[16,256]{1,0:T(8,128)S(1)}, u32[]{:S(2)}, u32[]{:S(2)}) collective-permute-start(f32[16,256]{1,0:T(8,128)S(1)} %gather_info.1.own_ref.mo), channel_id=1, source_target_pairs={{0,1},{1,0},{2,3},{3,2},{4,5},{5,4},{6,7},{7,6},{8,9},{9,8},{10,11... | collective-permute-start | bytes 49160 | tf_op jit(solution)/shard_map/ppermute | solution.py:631
  11.3 10.6 %collective-permute-start.3 = (f32[256,256]{1,0:T(8,128)S(1)}, f32[256,256]{1,0:T(8,128)S(1)}, u32[]{:S(2)}, u32[]{:S(2)}) collective-permute-start(f32[256,256]{1,0:T(8,128)S(1)} %project_far.1), channel_id=1, source_target_pairs={{0,8},{1,2},{2,1},{3,4},{4,3},{5,6},{6,5},{7,15},{8,0},{9,10},{10,... | collective-permute-start | bytes 786440 | tf_op jit(solution)/shard_map/ppermute | solution.py:634
  14.3 11.1 %copy-start.2 = (f32[1,256]{1,0:T(1,128)S(1)}, f32[1,256]{1,0:T(1,128)}, u32[]{:S(2)}) copy-start(f32[1,256]{1,0:T(1,128)} %weight_ref.1) | copy-start | bytes 3076
  14.3 11.1 %copy-start.3 = (f32[1,256]{1,0:T(1,128)S(1)}, f32[1,256]{1,0:T(1,128)}, u32[]{:S(2)}) copy-start(f32[1,256]{1,0:T(1,128)} %innovation_ref.1) | copy-start | bytes 3076
  14.3 31.8 %copy-start = (f32[256,256]{1,0:T(8,128)S(1)}, f32[256,256]{1,0:T(8,128)}, u32[]{:S(2)}) copy-start(f32[256,256]{1,0:T(8,128)} %transition_ref.1) | copy-start | bytes 786436
  14.3 31.8 %copy-start.4 = (f32[256]{0:T(256)S(1)}, f32[256]{0:T(256)}, u32[]{:S(2)}) copy-start(f32[256]{0:T(256)} %param.15) | copy-start | bytes 3076
  14.3 11.0 %collective-permute-start.2 = (f32[256,256]{1,0:T(8,128)S(1)}, f32[256,256]{1,0:T(8,128)S(1)}, u32[]{:S(2)}, u32[]{:S(2)}) collective-permute-start(f32[256,256]{1,0:T(8,128)S(1)} %project_near.1), channel_id=1, source_target_pairs={{0,1},{1,0},{2,3},{3,2},{4,5},{5,4},{6,7},{7,6},{8,9},{9,8},{10,11... | collective-permute-start | bytes 786440 | tf_op jit(solution)/shard_map/ppermute | solution.py:631
  25.7 6.1 %collective-permute-start.4 = (f32[264,128]{1,0:T(8,128)S(1)}, f32[264,128]{1,0:T(8,128)S(1)}, u32[]{:S(2)}, u32[]{:S(2)}) collective-permute-start(f32[264,128]{1,0:T(8,128)S(1)} %gram.1), channel_id=1, source_target_pairs={{0,1},{1,0},{2,3},{3,2},{4,5},{5,4},{6,7},{7,6},{8,9},{9,8},{10,11... | collective-permute-start | bytes 405512 | tf_op jit(solution)/shard_map/ppermute | solution.py:651
  31.8 5.1 %collective-permute-start.5 = (f32[264,128]{1,0:T(8,128)S(1)}, f32[264,128]{1,0:T(8,128)S(1)}, u32[]{:S(2)}, u32[]{:S(2)}) collective-permute-start(f32[264,128]{1,0:T(8,128)S(1)} %add.9), channel_id=1, source_target_pairs={{0,2},{1,3},{2,0},{3,1},{4,6},{5,7},{6,4},{7,5},{8,10},{9,11},{10,... | collective-permute-start | bytes 405512 | tf_op jit(solution)/shard_map/ppermute | solution.py:651
  36.9 7.7 %collective-permute-start.6 = (f32[264,128]{1,0:T(8,128)S(1)}, f32[264,128]{1,0:T(8,128)S(1)}, u32[]{:S(2)}, u32[]{:S(2)}) collective-permute-start(f32[264,128]{1,0:T(8,128)S(1)} %add.10), channel_id=1, source_target_pairs={{0,4},{1,5},{2,6},{3,7},{4,0},{5,1},{6,2},{7,3},{8,12},{9,13},{10,... | collective-permute-start | bytes 405512 | tf_op jit(solution)/shard_map/ppermute | solution.py:651
  44.6 1.4 %collective-permute-start.7 = (f32[264,128]{1,0:T(8,128)S(1)}, f32[264,128]{1,0:T(8,128)S(1)}, u32[]{:S(2)}, u32[]{:S(2)}) collective-permute-start(f32[264,128]{1,0:T(8,128)S(1)} %add.11.mine_ref), channel_id=1, source_target_pairs={{0,8},{8,0},{16,24},{24,16},{1,9},{9,1},{17,25},{25,17},{2,10},{10... | collective-permute-start | bytes 405512 | tf_op jit(solution)/shard_map/ppermute | solution.py:654
  56.0 5.7 %collective-permute-start.8 = (f32[264,128]{1,0:T(8,128)S(1)}, f32[264,128]{1,0:T(8,128)S(1)}, u32[]{:S(2)}, u32[]{:S(2)}) collective-permute-start(f32[264,128]{1,0:T(8,128)S(1)} %get-tuple-element.12), channel_id=1, source_target_pairs={{0,16},{8,24},{16,0},{24,8},{1,17},{9,25},{17,1},{25,9},{2,18},{10... | collective-permute-start | bytes 405512 | tf_op jit(solution)/shard_map/ppermute | solution.py:666
  65.3 2.3 %collective-permute-start.10 = (f32[24,256]{1,0:T(8,128)S(1)}, f32[24,256]{1,0:T(8,128)S(1)}, u32[]{:S(2)}, u32[]{:S(2)}) collective-permute-start(f32[24,256]{1,0:T(8,128)S(1)} %get-tuple-element.17.own_ref), channel_id=1, source_target_pairs={{0,8},{1,2},{2,1},{3,4},{4,3},{5,6},{6,5},{7,15},{8,0},{9,10},{10,... | collective-permute-start | bytes 73736 | tf_op jit(solution)/shard_map/ppermute | solution.py:634
  65.3 4.1 %collective-permute-start.9 = (f32[24,256]{1,0:T(8,128)S(1)}, f32[24,256]{1,0:T(8,128)S(1)}, u32[]{:S(2)}, u32[]{:S(2)}) collective-permute-start(f32[24,256]{1,0:T(8,128)S(1)} %get-tuple-element.17.own_ref), channel_id=1, source_target_pairs={{0,1},{1,0},{2,3},{3,2},{4,5},{5,4},{6,7},{7,6},{8,9},{9,8},{10,11... | collective-permute-start | bytes 73736 | tf_op jit(solution)/shard_map/ppermute | solution.py:631

commit v3 on v2

--- a/solution.py
+++ b/solution.py
@@ -6,6 +6,7 @@
 from jax.experimental import pallas as pl
 from jax.experimental.pallas import tpu as pltpu
 from jax.sharding import PartitionSpec as P
+
 
 STEPS = 4
 A_COEF = 0.5
@@ -20,10 +21,10 @@
 PADX = REACH + 1
 NEAR, FAR, OWN = "project_near", "project_far", "project_own"
 FINE = 16
+NARROW = 16.0
 HIGH = lax.Precision.HIGHEST
 NT = (((1,), (1,)), ((), ()))
 NN = (((1,), (0,)), ((), ()))
-TN = (((0,), (0,)), ((), ()))
 VMEM = pl.BlockSpec(memory_space=pltpu.VMEM)
 
 
@@ -171,18 +172,22 @@
                     change = change + at(p, dx)
                 p[ob, dx + PADX, lo:hi] = change
 
-        if own_slot:
-            picked = slice(lo + rows // 2, lo + rows // 2 + rows)
-        else:
-            picked = pl.ds(pl.multiple_of(jnp.where(even, lo, lo + rows), SUB), rows)
-        shift = lax.rem(col[:, lane] + (nx - REACH), nx)
-        fine = jnp.broadcast_to(lax.rem(shift, FINE), (rows, LANES))
-        bits = [(fine & (1 << i)) != 0 for i in range(4)]
-        coarse = jnp.broadcast_to(shift // FINE, (FINE, LANES))
-        blocks = nx // FINE
-        marks = [(coarse == block).astype(F32).astype(BF16) for block in range(blocks)]
-        zero = jnp.zeros((rows, LANES), F32)
-        for f in range(3):
+    if own_slot:
+        picked = slice(lo + rows // 2, lo + rows // 2 + rows)
+    else:
+        picked = pl.ds(pl.multiple_of(jnp.where(even, lo, lo + rows), SUB), rows)
+    zero = jnp.zeros((rows, LANES), F32)
+    blocks = nx // FINE
+    shift = lax.rem(col + (nx - REACH), nx)
+    depth_f = rows * nx
+    total = None
+    for f in range(3):
+        for ob in range(nob):
+            lane = slice(ob * LANES, (ob + 1) * LANES)
+            fine = jnp.broadcast_to(lax.rem(shift[:, lane], FINE), (rows, LANES))
+            bits = [(fine & (1 << i)) != 0 for i in range(4)]
+            coarse = jnp.broadcast_to(shift[:, lane] // FINE, (FINE, LANES))
+            marks = [(coarse == block).astype(F32).astype(BF16) for block in range(blocks)]
             values = [None] * (2 * FINE)
             for dx in range(-REACH, REACH + 1):
                 if f == 0:
@@ -213,9 +218,9 @@
                         )
                 values = moved
             for e in range(2 * FINE):
-                w[e * rows : (e + 1) * rows, :] = zero if values[e] is None else values[e]
+                w[f, ob, e * rows : (e + 1) * rows, :] = zero if values[e] is None else values[e]
             for y in range(rows):
-                both = halves(w[pl.ds(y, 2 * FINE, stride=rows), :])
+                both = halves(w[f, ob, pl.ds(y, 2 * FINE, stride=rows), :])
                 for part, ref in zip(both, (sh, sl)):
                     near, far = part[:FINE], part[FINE:]
                     for block in range(blocks):
@@ -223,7 +228,11 @@
                         ref[start_row : start_row + FINE, lane] = (
                             near * marks[block] + far * marks[block - 1]
                         )
-    out_ref[...] = dot1(basis_ref[...], sh[...]) + dot1(basis_ref[...], sl[...])
+        span = slice(f * depth_f, (f + 1) * depth_f)
+        basis = basis_ref[:, span]
+        part = dot1(basis, sh[span, :]) + dot1(basis, sl[span, :])
+        total = part if total is None else total + part
+    out_ref[...] = total
 
 
 def project(slot, own, first, second, basis, rows, nx):
@@ -242,7 +251,7 @@
             pltpu.VMEM(wide, F32),
             pltpu.VMEM(wide, F32),
             pltpu.VMEM(wide, F32),
-            pltpu.VMEM((2 * FINE * rows, LANES), F32),
+            pltpu.VMEM((3, nob, 2 * FINE * rows, LANES), F32),
             pltpu.VMEM((depth_all, nobs), BF16),
             pltpu.VMEM((depth_all, nobs), BF16),
         ],
@@ -252,7 +261,6 @@
             bytes_accessed=2 * order * depth_all,
             transcendentals=0,
         ),
-        name=slot,
     )(own, first, second, basis)
 
 
@@ -326,82 +334,129 @@
 
 
 def norm_of(matrix):
-    return jnp.max(jnp.sum(jnp.abs(matrix), axis=0, keepdims=True))
+    sums = jnp.sum(jnp.abs(matrix), axis=0, keepdims=True)
+    return jnp.broadcast_to(jnp.max(sums, axis=1, keepdims=True), sums.shape)
 
 
 def scaled(error):
     square = error * error
-    return 2.0 / (2.0 - square), square / (2.0 - square)
-
-
-def newton_start(matrix, row, eye):
-    size = matrix.shape[0]
-    parts = halves(matrix)
-    extended = with_row(matrix, row)
-    squares = dot3(halves(extended), parts)
-    square, row_moved = squares[:size], squares[size:]
+    rho = 2.0 / (2.0 - square)
+    return rho, 0.5 * square * rho
+
+
+def chebyshev_start(matrix, square, eye):
     bound = jnp.sqrt(norm_of(square))
     alpha = 2.0 / (2.0 + bound)
-    error0 = bound / (2.0 + bound)
-    rho0, error1 = scaled(error0)
-    rho1, error2 = scaled(error1)
+    error0 = 0.5 * bound * alpha
+    rho, error = scaled(error0)
     rest = 1.0 - alpha
-    first = (rho0 * alpha) * ((2.0 - alpha) * eye - alpha * matrix)
-    first_row = (rho0 * alpha) * ((2.0 - alpha) * row - alpha * row_moved)
-    squared = (rest * rest) * eye - (2.0 * rest * alpha) * matrix + (alpha * alpha) * square
-    residual = rho0 * squared + (1.0 - error1) * eye
-    estimate = rho1 * dot3(
-        halves(jnp.concatenate([first, first_row], axis=0)), halves(residual)
+    factor = rho * alpha
+    residual = rho * (
+        (rest * rest) * eye - (2.0 * rest * alpha) * matrix + (alpha * alpha) * square
+    ) - error * eye
+    return factor * (2.0 - alpha), factor * alpha, residual, error, bound
+
+
+def rough_turns(state, eye):
+    size = eye.shape[0]
+    new = []
+    for estimate, residual, error in state:
+        rho, error = scaled(error)
+        part = residual.astype(BF16)
+        moved = dot1(jnp.concatenate([estimate.astype(BF16), part], axis=0), part)
+        new.append((rho * (estimate + moved[:size]), rho * moved[size:] - error * eye, error))
+    return new
+
+
+def polish(matrix, part, estimate, eye, exact):
+    pieces = halves(estimate)
+    moved = dot6(matrix, estimate) if exact else dot3(part, pieces)
+    residual = eye - estimate - moved
+    rough = residual.astype(BF16)
+    change = residual + dot1(rough, rough)
+    return estimate + dot3(pieces, halves(change))
+
+
+def invert_any(matrix, part, c0, c1, error, eye):
+    def unsure(state):
+        return jnp.max(state[1]) > 0.03
+
+    def turn(state):
+        estimate, error = state
+        pieces = halves(estimate)
+        residual = 2.0 * eye - estimate - dot3(part, pieces)
+        rho, error = scaled(error)
+        return rho * dot3(pieces, halves(residual)), error
+
+    estimate, error = lax.while_loop(unsure, turn, (c0 * eye - c1 * matrix, error))
+    return lax.fori_loop(
+        0, 4, lambda index, value: polish(matrix, part, value, eye, True), estimate
     )
-    return estimate, error2, bound
-
-
-def newton(matrices, rows, tol, eye):
-    size = eye.shape[0]
-    starts = [newton_start(m, r, eye) for m, r in zip(matrices, rows)]
-    systems = [halves(eye + m) for m in matrices]
-
-    def unfinished(state):
-        return functools.reduce(jnp.maximum, state[1]) > tol
-
-    def turn(state):
-        new_estimates, new_errors = [], []
-        for system, estimate, error in zip(systems, *state):
-            parts = halves(estimate)
-            residual = 2.0 * eye - dot3(system, tuple(part[:size] for part in parts))
-            rho, error = scaled(error)
-            new_estimates.append(rho * dot3(parts, halves(residual)))
-            new_errors.append(error)
-        return tuple(new_estimates), tuple(new_errors)
-
-    state = tuple(s[0] for s in starts), tuple(s[1] for s in starts)
-    estimates, unused = lax.while_loop(unfinished, turn, state)
-    return estimates, functools.reduce(jnp.maximum, [s[2] for s in starts])
-
-
-def invert_shifted(matrices, rows):
+
+
+def invert_shifted(matrices, parts, turns):
     eye = identity_like(matrices[0])
-    size = eye.shape[0]
-    estimates, bound = newton(matrices, rows, 0.03, eye)
-    turns = jnp.where(bound > 300.0, 4, 1)
-
-    def polish(index, estimates):
-        result = []
-        for m, estimate in zip(matrices, estimates):
-            inverse = estimate[:size]
-            residual = eye - inverse - dot6(m, inverse)
-            rough = residual.astype(BF16)
-            change = residual + dot1(rough, rough)
-            result.append(estimate + dot3(halves(estimate), halves(change)))
-        return tuple(result)
-
-    estimates = lax.fori_loop(0, turns, polish, estimates)
-    return [(e[:size], e[size : size + 1]) for e in estimates]
+    state, starts, bounds = [], [], []
+    for matrix, part in zip(matrices, parts):
+        square = dot1(part[0], part[0])
+        c0, c1, residual, error, bound = chebyshev_start(matrix, square, eye)
+        state.append((c0 * eye - c1 * matrix, residual, error))
+        starts.append((c0, c1, error))
+        bounds.append(bound)
+    narrow = jnp.max(functools.reduce(jnp.maximum, bounds)) < NARROW
+    for _ in range(turns):
+        state = rough_turns(state, eye)
+    last = functools.reduce(jnp.maximum, [one[2] for one in state])
+    enough = narrow & (jnp.max(last) < 0.04)
+    quick = tuple(
+        polish(m, part, one[0], eye, False) for m, part, one in zip(matrices, parts, state)
+    )
+
+    def careful():
+        return tuple(
+            invert_any(m, part, *start, eye) for m, part, start in zip(matrices, parts, starts)
+        )
+
+    return lax.cond(enough, lambda: quick, careful)
+
+
+def solve_shifted(matrix, parts, row):
+    eye = identity_like(matrix)
+    row_parts = halves(row)
+    extended = tuple(jnp.concatenate(two, axis=0) for two in zip(row_parts, parts))
+    squares = dot3(extended, parts)
+    moved, square = squares[:SUB], squares[SUB:]
+    c0, c1, residual, error, _ = chebyshev_start(matrix, square, eye)
+    rho, last = scaled(error)
+    part = halves(residual)
+    start = c0 * row - c1 * moved
+    both = tuple(jnp.concatenate(two, axis=0) for two in zip(halves(start), part))
+    moved = dot3(both, part)
+    current = rho * (start + moved[:SUB])
+    part = halves(rho * moved[SUB:] - last * eye)
+    once = dot3(halves(current), part)
+    quick = current + once + dot3(halves(once), part)
+
+    def careful():
+        inverse = invert_any(matrix, parts, c0, c1, error, eye)
+        pieces = halves(inverse)
+
+        def correct(index, value):
+            miss = row - value - dot6(value, matrix)
+            return value + dot3(halves(miss), pieces)
+
+        return lax.fori_loop(0, 3, correct, dot3(row_parts, pieces))
+
+    return lax.cond(jnp.max(last) < 0.03, lambda: quick, careful)
 
 
 def column(row):
     size = row.shape[1]
     return jnp.broadcast_to(row, (size, size)).T
+
+
+def row_dot(row, parts, dims=NN):
+    return dot3(halves(jnp.broadcast_to(row, (SUB, row.shape[1]))), parts, dims)[0:1]
 
 
 def pair_kernel(
@@ -425,30 +480,40 @@
         matrix, vector = load_packed(packed)
         mats.append(root_col * matrix * root_row)
         rows.append(root_row * vector)
-    (p1, r1), (p2, r2) = invert_shifted(mats, rows)
-    c1, b1 = root_col * p1 * root_row, r1 * root_row
-    c2, b2 = root_col * p2 * root_row, r2 * root_row
-    low = halves(with_row(c1, b1))
-    a1 = moves * dot3(low, weighted)
-    a2 = dot3(halves(with_row(c2, b2)), weighted)
+    p1, p2 = invert_shifted(mats, [halves(m) for m in mats], 2)
+    c1, c2 = root_col * p1 * root_row, root_col * p2 * root_row
+    low = halves(c1)
+    a2 = dot3(halves(c2), weighted)
     k1 = dot3(low, turned)
-    a1, eta1 = a1[:size], a1[size : size + 1]
-    a2, eta2 = a2[:size], a2[size : size + 1]
     rest2 = halves(transition - a2)
     crossed = dot3(halves(k1), rest2)
+    a1 = moves * dot3(low, weighted)
+    b1 = row_dot(rows[0], halves(p1)) * root_row
+    b2 = row_dot(rows[1], halves(p2)) * root_row
+    eta1 = moves * row_dot(b1, weighted)
+    eta2 = row_dot(b2, weighted)
     j2 = dot3(turned, rest2)
     j1 = moves * dot3(turned, halves(transition - a1))
-    outer = dot3(low, halves(a2), NT)
-    spread = dot3(halves(a1.T), halves(j2))
-    ((inverse, s),) = invert_shifted([crossed[:size]], [eta2 - crossed[size : size + 1]])
-    both = jnp.concatenate([a1, outer[:size]], axis=1)
-    middle = dot3(halves(with_row(inverse, s)), halves(both))
-    right = halves(middle[:size])
-    ended = dot3(halves(a2), right)
+    a2_parts = halves(a2)
+    a1_parts = halves(a1)
+    j2_parts = halves(j2)
+    outer = dot3(low, a2_parts, NT)
+    ahead = row_dot(b1, a2_parts, NT) + b2
+    behind = eta2 - row_dot(b1, j2_parts)
+    spread = dot3(halves(a1.T), j2_parts)
+    (inverse,) = invert_shifted([crossed], [halves(crossed)], 1)
+    inverse = halves(inverse)
+    both = tuple(
+        jnp.concatenate(two, axis=1) for two in zip(a1_parts, halves(outer))
+    )
+    right = halves(dot3(inverse, both))
+    s = row_dot(behind, inverse)
+    ended = dot3(a2_parts, right)
+    ended_rows = row_dot(s, both)
     trans, cov = ended[:, :size], ended[:, size:] + c2
     prec = dot3(halves(spread), tuple(part[:, :size] for part in right)) + j1
-    info = middle[size : size + 1, :size] + eta1
-    mean = outer[size : size + 1] + middle[size : size + 1, size:] + b2
+    info = ended_rows[:, :size] + eta1
+    mean = ended_rows[:, size:] + ahead
     a_ref[...] = jnp.where(lower_core, a1, trans)
     j_ref[...] = jnp.where(lower_core, j1, prec)
     vec_ref[0:1] = jnp.where(lower_core, b1, mean)
@@ -483,16 +548,17 @@
 
 def advance_kernel(incoming_ref, a_ref, j_ref, c_ref, vec_ref, out_ref):
     cov0, mean0 = load_packed(incoming_ref[...])
-    size = mean0.shape[1]
-    low = halves(with_row(cov0, mean0))
-    crossed = dot3(low, halves(j_ref[...]))
-    outer = dot3(low, halves(a_ref[...]), NT)
-    ((inverse, s),) = invert_shifted(
-        [crossed[:size]], [vec_ref[3:4] - crossed[size : size + 1]]
-    )
-    middle = dot3(halves(with_row(inverse, s)), halves(outer[:size]))
-    mean = outer[size : size + 1] + middle[size : size + 1] + vec_ref[2:3]
-    cov = dot3(halves(a_ref[...]), halves(middle[:size])) + c_ref[...]
+    low = halves(cov0)
+    forward = halves(a_ref[...])
+    back = halves(j_ref[...])
+    crossed = dot3(low, back)
+    outer = halves(dot3(low, forward, NT))
+    behind = vec_ref[3:4] - row_dot(mean0, back)
+    (inverse,) = invert_shifted([crossed], [halves(crossed)], 1)
+    inverse = halves(inverse)
+    s = row_dot(behind, inverse)
+    mean = row_dot(mean0, forward, NT) + row_dot(s, outer) + vec_ref[2:3]
+    cov = dot3(forward, halves(dot3(inverse, outer))) + c_ref[...]
     store_packed(out_ref, cov, mean)
 
 
@@ -511,27 +577,21 @@
     moves = jnp.where(lax.axis_index("tm") < 2, 0.0, 1.0)
     cov0, mean0 = load_packed(incoming_ref[...] * moves)
     size = mean0.shape[1]
-    eye = identity_like(cov0)
-    crossed = dot3(halves(with_row(cov0, mean0)), halves(j_ref[...]))
+    low = halves(with_row(cov0, mean0))
+    crossed = dot3(low, halves(j_ref[...]))
+    outer = dot3(low, halves(a_ref[...]), NT)
     matrix = crossed[:size]
     target = jnp.broadcast_to(vec_ref[1:2], (SUB, size)) - crossed[size:]
-    (estimate,), bound = newton([matrix], [target[0:1]], 0.03, eye)
-    parts = halves(matrix)
-    inverse = halves(estimate[:size])
-
-    def polish(index, s):
-        miss = target - s - dot3(halves(s), parts)
-        return s + dot3(halves(miss), inverse)
-
-    s = lax.fori_loop(0, jnp.where(bound > 300.0, 8, 3), polish, estimate[size:])
-    ahead = mean0 + dot3(halves(s), halves(cov0))
-    mean = (dot3(halves(ahead), halves(a_ref[...]), NT) + vec_ref[0:1])[0:1]
+    s = solve_shifted(matrix, halves(matrix), target)
+    mean = (dot3(halves(s), halves(outer[:size])) + outer[size:] + vec_ref[0:1])[0:1]
     mean_ref[...] = mean
     pieces = jnp.concatenate(list(thirds(mean)) + [jnp.zeros((5, size), BF16)], axis=0)
-    sums = dot1(pieces, basis_ref[...])
-    total = sums[0:1] + (sums[1:2] + sums[2:3])
-    for i in range(3 * rows):
-        sum_ref[i : i + 1, :] = total[:, i * nx : (i + 1) * nx]
+    for f in range(3):
+        sums = dot1(pieces, basis_ref[:, f * rows * nx : (f + 1) * rows * nx])
+        total = sums[0:1] + (sums[1:2] + sums[2:3])
+        for y in range(rows):
+            i = f * rows + y
+            sum_ref[i : i + 1, :] = total[:, y * nx : (y + 1) * nx]
 
 
 def finish(incoming, a, j, vec, basis, rows, nx):
@@ -573,7 +633,7 @@
     def diff_rows(values):
         return pltpu.roll(values, total - 1, 0) - pltpu.roll(values, 1, 0)
 
-    for step in range(STEPS):
+    for _ in range(STEPS):
         east = u + CORIOLIS * v - A_COEF * diff_cols(h)
         north = (v - CORIOLIS * u - A_COEF * diff_rows(h)) * inside
         h = h - depth * (diff_cols(east) + diff_rows(north))
@@ -593,12 +653,21 @@
     )(own, first, second, mo, mf, ms)
 
 
-def info_kernel(depth_ref, cells_ref, fields_ref, out_ref):
+def info_kernel(depth_ref, cells_ref, fields_ref, out_ref, cells, fields, sems):
     rows = depth_ref.shape[0]
-    out_ref[0:rows, :] = depth_ref[...]
-    out_ref[rows : 2 * rows, :] = jnp.zeros_like(depth_ref)
-    out_ref[rows : rows + 1, :] = cells_ref[...].astype(F32)
-    out_ref[rows + 1 : rows + 2, :] = fields_ref[...].astype(F32)
+    copies = [
+        pltpu.make_async_copy(source, target, sems.at[i])
+        for i, (source, target) in enumerate((
+            (depth_ref, out_ref.at[0:rows]), (cells_ref, cells), (fields_ref, fields),
+        ))
+    ]
+    for copy in copies:
+        copy.start()
+    out_ref[rows : 2 * rows, :] = jnp.zeros(depth_ref.shape, F32)
+    for copy in copies:
+        copy.wait()
+    out_ref[rows : rows + 1, :] = cells[...].astype(F32)
+    out_ref[rows + 1 : rows + 2, :] = fields[...].astype(F32)
 
 
 def gather_info(mean_depth, obs_cells, obs_fields):
@@ -606,9 +675,14 @@
     return pl.pallas_call(
         info_kernel,
         out_shape=jax.ShapeDtypeStruct((2 * rows, nx), F32),
-        in_specs=[VMEM] * 3,
+        in_specs=[pl.BlockSpec(memory_space=pl.ANY)] * 3,
         out_specs=VMEM,
-        compiler_params=params(4),
+        scratch_shapes=[
+            pltpu.VMEM(obs_cells.shape, jnp.int32),
+            pltpu.VMEM(obs_fields.shape, jnp.int32),
+            pltpu.SemaphoreType.DMA((3,)),
+        ],
+        compiler_params=params(60),
         name="gather_info",
     )(mean_depth, obs_cells, obs_fields)
 
@@ -635,15 +709,16 @@
 
     info = gather_info(mean_depth, obs_cells, obs_fields)
     info_near = swap_near(info)
+    info_far = swap_far(info)
     basis = basis_fields[0].transpose(1, 0, 2, 3).reshape(order, 3 * rows * nx)
-    info_later, basis = lax.optimization_barrier((info, basis))
-    info_far = swap_far(info_later)
 
     part_near = project(NEAR, info, info_near, info_near, basis, rows, nx)
     got_near = swap_near(part_near)
+    info_far, unused = lax.optimization_barrier((info_far, part_near))
     part_far = project(FAR, info, info_far, info_far, basis, rows, nx)
     got_far = swap_far(part_far)
-    part_own = project(OWN, info, info_near, info_far, basis, rows, nx)
+    info_own, unused = lax.optimization_barrier((info, part_far))
+    part_own = project(OWN, info_own, info_near, info_far, basis, rows, nx)
 
     packed = gram(part_own, got_near, got_far, obs_weight, innovation)
     bit = 1
@@ -668,9 +743,9 @@
             longer = advance_prefix(incoming, *more, vec)
             prefix = jnp.where(pair == turn + 1, longer, prefix)
     mean, sums = finish(incoming, a, j, vec, basis, rows, nx)
-    result = propagate_sum(
-        sums, swap_near(sums), swap_far(sums), info, info_near, info_far, rows, nx
-    )
+    sums_near = swap_near(sums)
+    sums_far = swap_far(sums)
+    result = propagate_sum(sums, sums_near, sums_far, info, info_near, info_far, rows, nx)
     return mean, result[None]
 
 

time: 70.7 us -> 81 us (1.15)
  the two profiles are of different devices: /device:TPU:0 before, /device:TPU:14 now
where the time goes in v3:
time: 81 us; the launch traced here: 79.5 us
  Pallas kernels  33.3 us (41%)
  waiting for transfers between devices  31.4 us (39%)
  starting transfers between devices  10.8 us (13%)
  local copies, waits for them, and re-layouts  3.1 us (4%)
    pallas_call x1, Pallas kernels, pair_up(): pl.pallas_call(functools.partial(pair_kernel, full), out_shape=shapes, in...  18.8 us
    ppermute x3, waiting for transfers between devices, on_device(): lax.ppermute(packed, 'tile', [(i, i ^ bit) for i in range(tiles)])  13.9 us
    pallas_call x3, Pallas kernels, project(): pl.pallas_call(functools.partial(project_kernel, slot, rows, nx), out_sha...  9.13 us
    ppermute x1, waiting for transfers between devices, on_device(): incoming = lax.ppermute(prefix, 'tm', hop)  5.62 us
    ppermute x3, waiting for transfers between devices, swap_near(): return lax.ppermute(array, 'tile', near)  5.53 us
    ppermute x3, waiting for transfers between devices, swap_far(): return lax.ppermute(array, ('tm', 'tile'), far)  5.04 us
    ppermute x3, starting transfers between devices, swap_far(): return lax.ppermute(array, ('tm', 'tile'), far)  4.66 us
    ppermute x3, starting transfers between devices, swap_near(): return lax.ppermute(array, 'tile', near)  3.68 us
  transfers between devices with their start and end apart: 11, of which 9 were waited for; matrix products, arithmetic and copies ran while one was open for 4% of the time, Pallas kernels for 8%

profile of v3, /device:TPU:14, one launch (start us, length us, event | category | flops | bytes accessed | tf_op | source)
XLA Modules:
  0.0 79.5 jit_solution(15696898459973538538)
XLA Ops:
  0.6 1.3 %gather_info.1.own_ref.mo = f32[16,256]{1,0:T(8,128)} custom-call(f32[8,256]{1,0:T(8,128)} %depth_ref.1, s32[1,256]{1,0:T(1,128)} %cells_ref.1, s32[1,256]{1,0:T(1,128)} %fields_ref.1), custom_call_target="tpu_custom_call" | custom-call | tf_op jit(solution)/shard_map/gather_info/pallas_call | solution.py:675
  2.0 0.6 collective-permute-start.1
  2.6 2.5 %collective-permute-start = (f32[16,256]{1,0:T(8,128)}, f32[16,256]{1,0:T(8,128)S(1)}, u32[]{:S(2)}, u32[]{:S(2)}) collective-permute-start(f32[16,256]{1,0:T(8,128)} %gather_info.1.own_ref.mo), channel_id=1, source_target_pairs={{0,8},{1,2},{2,1},{3,4},{4,3},{5,6},{6,5},{7,15},{8,0},{9,10},{10,... | collective-permute-start | bytes 49160 | tf_op jit(solution)/shard_map/ppermute | solution.py:708
  5.1 2.1 %copy.10 = bf16[256,3,8,256]{3,2,1,0:T(8,128)(2,1)S(1)} copy(bf16[256,3,8,256]{3,2,0,1:T(8,128)(2,1)} %bitcast.14) | data formatting | bytes 6291456 | tf_op jit(solution)/shard_map/transpose | solution.py:713
  7.2 0.0 copy-start.1
  7.2 1.0 %copy.11 = bf16[32,8,24,256]{3,1,2,0:T(8,128)(2,1)S(1)} copy(bf16[32,8,24,256]{3,2,1,0:T(8,128)(2,1)S(1)} %bitcast.13) | data formatting | bytes 6291456
  8.2 3.1 %shard_map.95 = f32[256,256]{1,0:T(8,128)S(1)} custom-call(f32[16,256]{1,0:T(8,128)S(1)} %copy-done.1, f32[16,256]{1,0:T(8,128)S(1)} %collective-permute-done.1.first_ref.second_ref.mf, f32[16,256]{1,0:T(8,128)S(1)} %collective-permute-done.1.first_ref.second_ref.mf, bf16[256,6144]{1,0:T(8,128)(2,1)S(1)} %bitcast.8), custom_call_target="tpu_custom_call" | custom-call | flops 1610612736 | bytes 3145728 | tf_op jit(solution)/shard_map/pallas_call | solution.py:243
  11.3 3.1 %shard_map.96 = f32[256,256]{1,0:T(8,128)S(1)} custom-call(f32[16,256]{1,0:T(8,128)S(1)} %copy-done.1, f32[16,256]{1,0:T(8,128)S(1)} %collective-permute-done.first_ref.second_ref.ms, f32[16,256]{1,0:T(8,128)S(1)} %collective-permute-done.first_ref.second_ref.ms, bf16[256,6144]{1,0:T(8,128)(2,1)S(1)} %bitcast.9), custom_call_target="tpu_custom_call" | custom-call | flops 1610612736 | bytes 3145728 | tf_op jit(solution)/shard_map/pallas_call | solution.py:243
  14.4 0.0 copy-start.2
  14.4 0.5 collective-permute-start.3
  14.9 1.5 %collective-permute-start.2 = (f32[256,256]{1,0:T(8,128)S(1)}, f32[256,256]{1,0:T(8,128)S(1)}, u32[]{:S(2)}, u32[]{:S(2)}) collective-permute-start(f32[256,256]{1,0:T(8,128)S(1)} %shard_map.95), channel_id=1, source_target_pairs={{0,1},{1,0},{2,3},{3,2},{4,5},{5,4},{6,7},{7,6},{8,9},{9,8},{10,11... | collective-permute-start | bytes 786440 | tf_op jit(solution)/shard_map/ppermute | solution.py:705
  16.4 3.0 %shard_map.97.own_ref = f32[256,256]{1,0:T(8,128)S(1)} custom-call(f32[16,256]{1,0:T(8,128)S(1)} %copy-done.1, f32[16,256]{1,0:T(8,128)S(1)} %collective-permute-done.1.first_ref.second_ref.mf, f32[16,256]{1,0:T(8,128)S(1)} %collective-permute-done.first_ref.second_ref.ms, bf16[256,6144]{1,0:T(8,128)(2,1)S(1)} %bitcast.10), custom_call_target="tpu_custom_call" | custom-call | flops 1610612736 | bytes 3145728 | tf_op jit(solution)/shard_map/pallas_call | solution.py:243
  19.4 3.6 %collective-permute-done.3.second_ref = f32[256,256]{1,0:T(8,128)S(1)} collective-permute-done((f32[256,256]{1,0:T(8,128)S(1)}, f32[256,256]{1,0:T(8,128)S(1)}, u32[]{:S(2)}, u32[]{:S(2)}) %collective-permute-start.3) | collective-permute-done | bytes 262176 | tf_op jit(solution)/shard_map/ppermute | solution.py:708
  23.0 4.8 %collective-permute-done.2.first_ref = f32[256,256]{1,0:T(8,128)S(1)} collective-permute-done((f32[256,256]{1,0:T(8,128)S(1)}, f32[256,256]{1,0:T(8,128)S(1)}, u32[]{:S(2)}, u32[]{:S(2)}) %collective-permute-start.2) | collective-permute-done | bytes 262176 | tf_op jit(solution)/shard_map/ppermute | solution.py:705
  27.7 0.4 gram.1
  28.1 0.2 collective-permute-start.4
  28.3 4.8 %collective-permute-done.4 = f32[264,128]{1,0:T(8,128)S(1)} collective-permute-done((f32[264,128]{1,0:T(8,128)S(1)}, f32[264,128]{1,0:T(8,128)S(1)}, u32[]{:S(2)}, u32[]{:S(2)}) %collective-permute-start.4) | collective-permute-done | bytes 135200 | tf_op jit(solution)/shard_map/ppermute | solution.py:726
  33.2 0.5 collective-permute-start.5
  33.7 4.6 %collective-permute-done.5 = f32[264,128]{1,0:T(8,128)S(1)} collective-permute-done((f32[264,128]{1,0:T(8,128)S(1)}, f32[264,128]{1,0:T(8,128)S(1)}, u32[]{:S(2)}, u32[]{:S(2)}) %collective-permute-start.5) | collective-permute-done | bytes 135200 | tf_op jit(solution)/shard_map/ppermute | solution.py:726
  38.3 1.6 %collective-permute-start.6 = (f32[264,128]{1,0:T(8,128)S(1)}, f32[264,128]{1,0:T(8,128)S(1)}, u32[]{:S(2)}, u32[]{:S(2)}) collective-permute-start(f32[264,128]{1,0:T(8,128)S(1)} %add.10), channel_id=1, source_target_pairs={{0,4},{1,5},{2,6},{3,7},{4,0},{5,1},{6,2},{7,3},{8,12},{9,13},{10,... | collective-permute-start | bytes 405512 | tf_op jit(solution)/shard_map/ppermute | solution.py:726
  39.8 4.5 %collective-permute-done.6 = f32[264,128]{1,0:T(8,128)S(1)} collective-permute-done((f32[264,128]{1,0:T(8,128)S(1)}, f32[264,128]{1,0:T(8,128)S(1)}, u32[]{:S(2)}, u32[]{:S(2)}) %collective-permute-start.6) | collective-permute-done | bytes 135200 | tf_op jit(solution)/shard_map/ppermute | solution.py:726
  44.4 0.1 collective-permute-start.7
  44.4 1.3 %collective-permute-done.7.other_ref = f32[264,128]{1,0:T(8,128)S(1)} collective-permute-done((f32[264,128]{1,0:T(8,128)S(1)}, f32[264,128]{1,0:T(8,128)S(1)}, u32[]{:S(2)}, u32[]{:S(2)}) %collective-permute-start.7) | collective-permute-done | bytes 135200 | tf_op jit(solution)/shard_map/ppermute | solution.py:729
  45.8 18.8 %pair_up.1 = (f32[256,256]{1,0:T(8,128)S(1)}, f32[256,256]{1,0:T(8,128)S(1)}, f32[8,256]{1,0:T(8,128)S(1)}, f32[264,128]{1,0:T(8,128)S(1)}) custom-call(f32[264,128]{1,0:T(8,128)S(1)} %add.11.mine_ref, f32[264,128]{1,0:T(8,128)S(1)} %collective-permute-done.7.other_ref, f32[256,256]{1,0:T(8,128)S(1)} %copy-done, f32[1,256]{1,0:T(1,128)S(1)} %bitcast.12), custom_call_target="tpu_custom_call" | custom-call | tf_op jit(solution)/shard_map/pair_up/pallas_call | solution.py:539
  64.6 0.1 collective-permute-start.8
  64.7 5.6 %collective-permute-done.8.incoming_ref = f32[264,128]{1,0:T(8,128)S(1)} collective-permute-done((f32[264,128]{1,0:T(8,128)S(1)}, f32[264,128]{1,0:T(8,128)S(1)}, u32[]{:S(2)}, u32[]{:S(2)}) %collective-permute-start.8) | collective-permute-done | bytes 135200 | tf_op jit(solution)/shard_map/ppermute | solution.py:741
  70.3 2.5 %finish.1 = (f32[1,256]{1,0:T(1,128)}, f32[24,256]{1,0:T(8,128)S(1)}) custom-call(f32[264,128]{1,0:T(8,128)S(1)} %collective-permute-done.8.incoming_ref, f32[256,256]{1,0:T(8,128)S(1)} %get-tuple-element.13.a_ref, f32[256,256]{1,0:T(8,128)S(1)} %get-tuple-element.14.j_ref, f32[8,256]{1,0:T(8,128)S(1)} %get-tuple-element.15.vec_ref, ...), custom_call_target="tpu_custom_call" | custom-call | tf_op jit(solution)/shard_map/finish/pallas_call | solution.py:599
  72.8 1.7 %collective-permute-start.10 = (f32[24,256]{1,0:T(8,128)S(1)}, f32[24,256]{1,0:T(8,128)S(1)}, u32[]{:S(2)}, u32[]{:S(2)}) collective-permute-start(f32[24,256]{1,0:T(8,128)S(1)} %get-tuple-element.17.own_ref), channel_id=1, source_target_pairs={{0,8},{1,2},{2,1},{3,4},{4,3},{5,6},{6,5},{7,15},{8,0},{9,10},{10,... | collective-permute-start | bytes 73736 | tf_op jit(solution)/shard_map/ppermute | solution.py:708
  74.5 1.6 %collective-permute-start.9 = (f32[24,256]{1,0:T(8,128)S(1)}, f32[24,256]{1,0:T(8,128)S(1)}, u32[]{:S(2)}, u32[]{:S(2)}) collective-permute-start(f32[24,256]{1,0:T(8,128)S(1)} %get-tuple-element.17.own_ref), channel_id=1, source_target_pairs={{0,1},{1,0},{2,3},{3,2},{4,5},{5,4},{6,7},{7,6},{8,9},{9,8},{10,11... | collective-permute-start | bytes 73736 | tf_op jit(solution)/shard_map/ppermute | solution.py:705
  76.1 1.5 %collective-permute-done.10.second_ref = f32[24,256]{1,0:T(8,128)S(1)} collective-permute-done((f32[24,256]{1,0:T(8,128)S(1)}, f32[24,256]{1,0:T(8,128)S(1)}, u32[]{:S(2)}, u32[]{:S(2)}) %collective-permute-start.10) | collective-permute-done | bytes 24608 | tf_op jit(solution)/shard_map/ppermute | solution.py:708
  77.6 0.8 collective-permute-done.9.first_ref
  78.3 1.2 %propagate_sum.1 = f32[3,8,256]{2,1,0:T(8,128)} custom-call(f32[24,256]{1,0:T(8,128)S(1)} %get-tuple-element.17.own_ref, f32[24,256]{1,0:T(8,128)S(1)} %collective-permute-done.9.first_ref, f32[24,256]{1,0:T(8,128)S(1)} %collective-permute-done.10.second_ref, f32[16,256]{1,0:T(8,128)S(1)} %copy-done.1, ...), custom_call_target="tpu_custom_call" | custom-call | tf_op jit(solution)/shard_map/propagate_sum/pallas_call | solution.py:646
  (13 shorter events, 0.1 us)
Async XLA Ops:
  2.0 6.2 %collective-permute-start.1 = (f32[16,256]{1,0:T(8,128)}, f32[16,256]{1,0:T(8,128)S(1)}, u32[]{:S(2)}, u32[]{:S(2)}) collective-permute-start(f32[16,256]{1,0:T(8,128)} %gather_info.1.own_ref.mo), channel_id=1, source_target_pairs={{0,1},{1,0},{2,3},{3,2},{4,5},{5,4},{6,7},{7,6},{8,9},{9,8},{10,11... | collective-permute-start | bytes 49160 | tf_op jit(solution)/shard_map/ppermute | solution.py:705
  2.6 8.7 %collective-permute-start = (f32[16,256]{1,0:T(8,128)}, f32[16,256]{1,0:T(8,128)S(1)}, u32[]{:S(2)}, u32[]{:S(2)}) collective-permute-start(f32[16,256]{1,0:T(8,128)} %gather_info.1.own_ref.mo), channel_id=1, source_target_pairs={{0,8},{1,2},{2,1},{3,4},{4,3},{5,6},{6,5},{7,15},{8,0},{9,10},{10,... | collective-permute-start | bytes 49160 | tf_op jit(solution)/shard_map/ppermute | solution.py:708
  7.2 1.0 %copy-start.1 = (f32[16,256]{1,0:T(8,128)S(1)}, f32[16,256]{1,0:T(8,128)}, u32[]{:S(2)}) copy-start(f32[16,256]{1,0:T(8,128)} %gather_info.1.own_ref.mo) | copy-start | bytes 49156
  14.4 13.4 %copy-start.2 = (f32[1,256]{1,0:T(1,128)S(1)}, f32[1,256]{1,0:T(1,128)}, u32[]{:S(2)}) copy-start(f32[1,256]{1,0:T(1,128)} %weight_ref.1) | copy-start | bytes 3076
  14.4 13.3 %copy-start.3 = (f32[1,256]{1,0:T(1,128)S(1)}, f32[1,256]{1,0:T(1,128)}, u32[]{:S(2)}) copy-start(f32[1,256]{1,0:T(1,128)} %innovation_ref.1) | copy-start | bytes 3076
  14.4 31.4 %copy-start = (f32[256,256]{1,0:T(8,128)S(1)}, f32[256,256]{1,0:T(8,128)}, u32[]{:S(2)}) copy-start(f32[256,256]{1,0:T(8,128)} %transition_ref.1) | copy-start | bytes 786436
  14.4 31.4 %copy-start.4 = (f32[256]{0:T(256)S(1)}, f32[256]{0:T(256)}, u32[]{:S(2)}) copy-start(f32[256]{0:T(256)} %param.15) | copy-start | bytes 3076
  14.4 8.5 %collective-permute-start.3 = (f32[256,256]{1,0:T(8,128)S(1)}, f32[256,256]{1,0:T(8,128)S(1)}, u32[]{:S(2)}, u32[]{:S(2)}) collective-permute-start(f32[256,256]{1,0:T(8,128)S(1)} %shard_map.96), channel_id=1, source_target_pairs={{0,8},{1,2},{2,1},{3,4},{4,3},{5,6},{6,5},{7,15},{8,0},{9,10},{10,... | collective-permute-start | bytes 786440 | tf_op jit(solution)/shard_map/ppermute | solution.py:708
  14.9 12.8 %collective-permute-start.2 = (f32[256,256]{1,0:T(8,128)S(1)}, f32[256,256]{1,0:T(8,128)S(1)}, u32[]{:S(2)}, u32[]{:S(2)}) collective-permute-start(f32[256,256]{1,0:T(8,128)S(1)} %shard_map.95), channel_id=1, source_target_pairs={{0,1},{1,0},{2,3},{3,2},{4,5},{5,4},{6,7},{7,6},{8,9},{9,8},{10,11... | collective-permute-start | bytes 786440 | tf_op jit(solution)/shard_map/ppermute | solution.py:705
  28.1 5.1 %collective-permute-start.4 = (f32[264,128]{1,0:T(8,128)S(1)}, f32[264,128]{1,0:T(8,128)S(1)}, u32[]{:S(2)}, u32[]{:S(2)}) collective-permute-start(f32[264,128]{1,0:T(8,128)S(1)} %gram.1), channel_id=1, source_target_pairs={{0,1},{1,0},{2,3},{3,2},{4,5},{5,4},{6,7},{7,6},{8,9},{9,8},{10,11... | collective-permute-start | bytes 405512 | tf_op jit(solution)/shard_map/ppermute | solution.py:726
  33.2 5.1 %collective-permute-start.5 = (f32[264,128]{1,0:T(8,128)S(1)}, f32[264,128]{1,0:T(8,128)S(1)}, u32[]{:S(2)}, u32[]{:S(2)}) collective-permute-start(f32[264,128]{1,0:T(8,128)S(1)} %add.9), channel_id=1, source_target_pairs={{0,2},{1,3},{2,0},{3,1},{4,6},{5,7},{6,4},{7,5},{8,10},{9,11},{10,... | collective-permute-start | bytes 405512 | tf_op jit(solution)/shard_map/ppermute | solution.py:726
  38.3 6.1 %collective-permute-start.6 = (f32[264,128]{1,0:T(8,128)S(1)}, f32[264,128]{1,0:T(8,128)S(1)}, u32[]{:S(2)}, u32[]{:S(2)}) collective-permute-start(f32[264,128]{1,0:T(8,128)S(1)} %add.10), channel_id=1, source_target_pairs={{0,4},{1,5},{2,6},{3,7},{4,0},{5,1},{6,2},{7,3},{8,12},{9,13},{10,... | collective-permute-start | bytes 405512 | tf_op jit(solution)/shard_map/ppermute | solution.py:726
  44.4 1.4 %collective-permute-start.7 = (f32[264,128]{1,0:T(8,128)S(1)}, f32[264,128]{1,0:T(8,128)S(1)}, u32[]{:S(2)}, u32[]{:S(2)}) collective-permute-start(f32[264,128]{1,0:T(8,128)S(1)} %add.11.mine_ref), channel_id=1, source_target_pairs={{0,8},{8,0},{16,24},{24,16},{1,9},{9,1},{17,25},{25,17},{2,10},{10... | collective-permute-start | bytes 405512 | tf_op jit(solution)/shard_map/ppermute | solution.py:729
  64.6 5.7 %collective-permute-start.8 = (f32[264,128]{1,0:T(8,128)S(1)}, f32[264,128]{1,0:T(8,128)S(1)}, u32[]{:S(2)}, u32[]{:S(2)}) collective-permute-start(f32[264,128]{1,0:T(8,128)S(1)} %get-tuple-element.12), channel_id=1, source_target_pairs={{0,16},{8,24},{16,0},{24,8},{1,17},{9,25},{17,1},{25,9},{2,18},{10... | collective-permute-start | bytes 405512 | tf_op jit(solution)/shard_map/ppermute | solution.py:741
  72.8 4.7 %collective-permute-start.10 = (f32[24,256]{1,0:T(8,128)S(1)}, f32[24,256]{1,0:T(8,128)S(1)}, u32[]{:S(2)}, u32[]{:S(2)}) collective-permute-start(f32[24,256]{1,0:T(8,128)S(1)} %get-tuple-element.17.own_ref), channel_id=1, source_target_pairs={{0,8},{1,2},{2,1},{3,4},{4,3},{5,6},{6,5},{7,15},{8,0},{9,10},{10,... | collective-permute-start | bytes 73736 | tf_op jit(solution)/shard_map/ppermute | solution.py:708
  74.5 3.8 %collective-permute-start.9 = (f32[24,256]{1,0:T(8,128)S(1)}, f32[24,256]{1,0:T(8,128)S(1)}, u32[]{:S(2)}, u32[]{:S(2)}) collective-permute-start(f32[24,256]{1,0:T(8,128)S(1)} %get-tuple-element.17.own_ref), channel_id=1, source_target_pairs={{0,1},{1,0},{2,3},{3,2},{4,5},{5,4},{6,7},{7,6},{8,9},{9,8},{10,11... | collective-permute-start | bytes 73736 | tf_op jit(solution)/shard_map/ppermute | solution.py:705

commit v4 on v3

--- a/solution.py
+++ b/solution.py
@@ -229,14 +229,15 @@
                             near * marks[block] + far * marks[block - 1]
                         )
         span = slice(f * depth_f, (f + 1) * depth_f)
-        basis = basis_ref[:, span]
+        basis = basis_ref[f]
         part = dot1(basis, sh[span, :]) + dot1(basis, sl[span, :])
         total = part if total is None else total + part
     out_ref[...] = total
 
 
 def project(slot, own, first, second, basis, rows, nx):
-    order, depth_all = basis.shape
+    order = basis.shape[1]
+    depth_all = 3 * rows * nx
     nobs = own.shape[1]
     nob = nobs // LANES
     wide = (nob, 2 * PADX + 1, 2 * rows + 2 * SUB, LANES)
@@ -587,7 +588,7 @@
     mean_ref[...] = mean
     pieces = jnp.concatenate(list(thirds(mean)) + [jnp.zeros((5, size), BF16)], axis=0)
     for f in range(3):
-        sums = dot1(pieces, basis_ref[:, f * rows * nx : (f + 1) * rows * nx])
+        sums = dot1(pieces, basis_ref[f])
         total = sums[0:1] + (sums[1:2] + sums[2:3])
         for y in range(rows):
             i = f * rows + y
@@ -651,6 +652,39 @@
         compiler_params=params(8),
         name="propagate_sum",
     )(own, first, second, mo, mf, ms)
+
+
+def layout_kernel(fields_ref, out_ref, held, sems, *spread):
+    count, order, rows, nx = fields_ref.shape
+    copies = [
+        pltpu.make_async_copy(fields_ref.at[f], held.at[f], sems.at[f]) for f in range(count)
+    ]
+    for copy in copies:
+        copy.start()
+    for f, copy in enumerate(copies):
+        copy.wait()
+        for ob, ref in enumerate(spread):
+            lane = slice(ob * LANES, (ob + 1) * LANES)
+            ref[...] = held[f, :, :, lane].astype(F32).reshape(order * rows, LANES)
+            for y in range(rows):
+                start = y * nx + ob * LANES
+                out_ref[f, :, start : start + LANES] = ref[
+                    pl.ds(y, order, stride=rows), :
+                ].astype(BF16)
+
+
+def lay_out(fields):
+    count, order, rows, nx = fields.shape
+    return pl.pallas_call(
+        layout_kernel,
+        out_shape=jax.ShapeDtypeStruct((count, order, rows * nx), BF16),
+        in_specs=[pl.BlockSpec(memory_space=pl.ANY)],
+        out_specs=VMEM,
+        scratch_shapes=[pltpu.VMEM(fields.shape, BF16), pltpu.SemaphoreType.DMA((count,))]
+        + [pltpu.VMEM((order * rows, LANES), F32)] * (nx // LANES),
+        compiler_params=params(50),
+        name="lay_out",
+    )(fields)
 
 
 def info_kernel(depth_ref, cells_ref, fields_ref, out_ref, cells, fields, sems):
@@ -690,7 +724,7 @@
 def on_device(
     basis_fields, mean_depth, obs_cells, obs_fields, obs_weight, innovation, transition, model_error
 ):
-    order, rows, nx = basis_fields.shape[2:]
+    _, rows, nx = basis_fields.shape[2:]
     tiles = lax.axis_size("tile")
     windows = lax.axis_size("tm")
     near = [(i, i ^ 1) for i in range(tiles)]
@@ -710,7 +744,7 @@
     info = gather_info(mean_depth, obs_cells, obs_fields)
     info_near = swap_near(info)
     info_far = swap_far(info)
-    basis = basis_fields[0].transpose(1, 0, 2, 3).reshape(order, 3 * rows * nx)
+    basis = lay_out(basis_fields[0])
 
     part_near = project(NEAR, info, info_near, info_near, basis, rows, nx)
     got_near = swap_near(part_near)

time: 81 us -> 80.8 us (level)
  local copies, waits for them, and re-layouts: 3.1 us -> 0.03 us
  Pallas kernels: 33.3 us -> 36.3 us
    pallas_call x0 -> x1, Pallas kernels: none -> 2.92 us  [lay_out(): pl.pallas_call(layout_kernel, out_shape=jax.ShapeDtypeStruct((count, orde...]
    transpose x1 -> x0, local copies, waits for them, and re-layouts: 2.09 us -> none  [on_device(): basis = basis_fields[0].transpose(1, 0, 2, 3).reshape(order, 3 * rows * nx)]
    unnamed x11 -> x10, local copies, waits for them, and re-layouts: 1.01 us -> 0.03 us
  transfers between devices with their start and end apart: 11 -> 11, of which waited for: 9 -> 9; matrix products, arithmetic and copies ran while one was open for 4% -> 0% of each run, Pallas kernels for 8% -> 11%
where the time goes in v4:
time: 80.8 us; the launch traced here: 79.4 us
  Pallas kernels  36.3 us (45%)
  waiting for transfers between devices  31.4 us (39%)
  starting transfers between devices  10.8 us (13%)
    pallas_call x1, Pallas kernels, pair_up(): pl.pallas_call(functools.partial(pair_kernel, full), out_shape=shapes, in...  18.8 us
    ppermute x3, waiting for transfers between devices, on_device(): lax.ppermute(packed, 'tile', [(i, i ^ bit) for i in range(tiles)])  13.9 us
    pallas_call x3, Pallas kernels, project(): pl.pallas_call(functools.partial(project_kernel, slot, rows, nx), out_sha...  9.13 us
    ppermute x1, waiting for transfers between devices, on_device(): incoming = lax.ppermute(prefix, 'tm', hop)  5.62 us
    ppermute x3, waiting for transfers between devices, swap_near(): return lax.ppermute(array, 'tile', near)  5.53 us
    ppermute x3, waiting for transfers between devices, swap_far(): return lax.ppermute(array, ('tm', 'tile'), far)  5.04 us
    ppermute x3, starting transfers between devices, swap_far(): return lax.ppermute(array, ('tm', 'tile'), far)  4.66 us
    ppermute x3, starting transfers between devices, swap_near(): return lax.ppermute(array, 'tile', near)  3.68 us
  transfers between devices with their start and end apart: 11, of which 9 were waited for; matrix products, arithmetic and copies ran while one was open for 0% of the time, Pallas kernels for 11%

profile of v4, /device:TPU:14, one launch (start us, length us, event | category | flops | bytes accessed | tf_op | source)
XLA Modules:
  0.0 79.4 jit_solution(9658725031283846684)
XLA Ops:
  0.6 1.3 %gather_info.1.own_ref.mo = f32[16,256]{1,0:T(8,128)} custom-call(f32[8,256]{1,0:T(8,128)} %depth_ref.1, s32[1,256]{1,0:T(1,128)} %cells_ref.1, s32[1,256]{1,0:T(1,128)} %fields_ref.1), custom_call_target="tpu_custom_call" | custom-call | tf_op jit(solution)/shard_map/gather_info/pallas_call | solution.py:709
  2.0 0.6 collective-permute-start.1
  2.6 2.5 %collective-permute-start = (f32[16,256]{1,0:T(8,128)}, f32[16,256]{1,0:T(8,128)S(1)}, u32[]{:S(2)}, u32[]{:S(2)}) collective-permute-start(f32[16,256]{1,0:T(8,128)} %gather_info.1.own_ref.mo), channel_id=1, source_target_pairs={{0,8},{1,2},{2,1},{3,4},{4,3},{5,6},{6,5},{7,15},{8,0},{9,10},{10,... | collective-permute-start | bytes 49160 | tf_op jit(solution)/shard_map/ppermute | solution.py:742
  5.1 2.9 %lay_out.1.basis_ref = bf16[3,256,2048]{2,1,0:T(8,128)(2,1)S(1)} custom-call(bf16[3,256,8,256]{3,2,1,0:T(8,128)(2,1)} %bitcast.4), custom_call_target="tpu_custom_call" | custom-call | tf_op jit(solution)/shard_map/lay_out/pallas_call | solution.py:678
  8.0 3.1 %shard_map.95 = f32[256,256]{1,0:T(8,128)S(1)} custom-call(f32[16,256]{1,0:T(8,128)S(1)} %copy-done.1, f32[16,256]{1,0:T(8,128)S(1)} %collective-permute-done.1.first_ref.second_ref.mf, f32[16,256]{1,0:T(8,128)S(1)} %collective-permute-done.1.first_ref.second_ref.mf, bf16[3,256,2048]{2,1,0:T(8,128)(2,1)S(1)} %lay_out.1.basis_ref), custom_call_target="tpu_custom_call" | custom-call | flops 1610612736 | bytes 3145728 | tf_op jit(solution)/shard_map/pallas_call | solution.py:244
  11.1 3.1 %shard_map.96 = f32[256,256]{1,0:T(8,128)S(1)} custom-call(f32[16,256]{1,0:T(8,128)S(1)} %copy-done.1, f32[16,256]{1,0:T(8,128)S(1)} %collective-permute-done.first_ref.second_ref.ms, f32[16,256]{1,0:T(8,128)S(1)} %collective-permute-done.first_ref.second_ref.ms, bf16[3,256,2048]{2,1,0:T(8,128)(2,1)S(1)} %lay_out.1.basis_ref), custom_call_target="tpu_custom_call" | custom-call | flops 1610612736 | bytes 3145728 | tf_op jit(solution)/shard_map/pallas_call | solution.py:244
  14.2 0.0 copy-start.2
  14.2 0.0 copy-start.3
  14.2 0.0 copy-start
  14.2 0.5 collective-permute-start.3
  14.7 1.5 %collective-permute-start.2 = (f32[256,256]{1,0:T(8,128)S(1)}, f32[256,256]{1,0:T(8,128)S(1)}, u32[]{:S(2)}, u32[]{:S(2)}) collective-permute-start(f32[256,256]{1,0:T(8,128)S(1)} %shard_map.95), channel_id=1, source_target_pairs={{0,1},{1,0},{2,3},{3,2},{4,5},{5,4},{6,7},{7,6},{8,9},{9,8},{10,11... | collective-permute-start | bytes 786440 | tf_op jit(solution)/shard_map/ppermute | solution.py:739
  16.2 3.0 %shard_map.97.own_ref = f32[256,256]{1,0:T(8,128)S(1)} custom-call(f32[16,256]{1,0:T(8,128)S(1)} %copy-done.1, f32[16,256]{1,0:T(8,128)S(1)} %collective-permute-done.1.first_ref.second_ref.mf, f32[16,256]{1,0:T(8,128)S(1)} %collective-permute-done.first_ref.second_ref.ms, bf16[3,256,2048]{2,1,0:T(8,128)(2,1)S(1)} %lay_out.1.basis_ref), custom_call_target="tpu_custom_call" | custom-call | flops 1610612736 | bytes 3145728 | tf_op jit(solution)/shard_map/pallas_call | solution.py:244
  19.2 3.6 %collective-permute-done.3.second_ref = f32[256,256]{1,0:T(8,128)S(1)} collective-permute-done((f32[256,256]{1,0:T(8,128)S(1)}, f32[256,256]{1,0:T(8,128)S(1)}, u32[]{:S(2)}, u32[]{:S(2)}) %collective-permute-start.3) | collective-permute-done | bytes 262176 | tf_op jit(solution)/shard_map/ppermute | solution.py:742
  22.8 4.8 %collective-permute-done.2.first_ref = f32[256,256]{1,0:T(8,128)S(1)} collective-permute-done((f32[256,256]{1,0:T(8,128)S(1)}, f32[256,256]{1,0:T(8,128)S(1)}, u32[]{:S(2)}, u32[]{:S(2)}) %collective-permute-start.2) | collective-permute-done | bytes 262176 | tf_op jit(solution)/shard_map/ppermute | solution.py:739
  27.5 0.4 gram.1
  27.9 0.2 collective-permute-start.4
  28.1 4.8 %collective-permute-done.4 = f32[264,128]{1,0:T(8,128)S(1)} collective-permute-done((f32[264,128]{1,0:T(8,128)S(1)}, f32[264,128]{1,0:T(8,128)S(1)}, u32[]{:S(2)}, u32[]{:S(2)}) %collective-permute-start.4) | collective-permute-done | bytes 135200 | tf_op jit(solution)/shard_map/ppermute | solution.py:760
  33.0 0.5 collective-permute-start.5
  33.5 4.6 %collective-permute-done.5 = f32[264,128]{1,0:T(8,128)S(1)} collective-permute-done((f32[264,128]{1,0:T(8,128)S(1)}, f32[264,128]{1,0:T(8,128)S(1)}, u32[]{:S(2)}, u32[]{:S(2)}) %collective-permute-start.5) | collective-permute-done | bytes 135200 | tf_op jit(solution)/shard_map/ppermute | solution.py:760
  38.1 1.6 %collective-permute-start.6 = (f32[264,128]{1,0:T(8,128)S(1)}, f32[264,128]{1,0:T(8,128)S(1)}, u32[]{:S(2)}, u32[]{:S(2)}) collective-permute-start(f32[264,128]{1,0:T(8,128)S(1)} %add.10), channel_id=1, source_target_pairs={{0,4},{1,5},{2,6},{3,7},{4,0},{5,1},{6,2},{7,3},{8,12},{9,13},{10,... | collective-permute-start | bytes 405512 | tf_op jit(solution)/shard_map/ppermute | solution.py:760
  39.7 4.5 %collective-permute-done.6 = f32[264,128]{1,0:T(8,128)S(1)} collective-permute-done((f32[264,128]{1,0:T(8,128)S(1)}, f32[264,128]{1,0:T(8,128)S(1)}, u32[]{:S(2)}, u32[]{:S(2)}) %collective-permute-start.6) | collective-permute-done | bytes 135200 | tf_op jit(solution)/shard_map/ppermute | solution.py:760
  44.2 0.1 collective-permute-start.7
  44.3 1.3 %collective-permute-done.7.other_ref = f32[264,128]{1,0:T(8,128)S(1)} collective-permute-done((f32[264,128]{1,0:T(8,128)S(1)}, f32[264,128]{1,0:T(8,128)S(1)}, u32[]{:S(2)}, u32[]{:S(2)}) %collective-permute-start.7) | collective-permute-done | bytes 135200 | tf_op jit(solution)/shard_map/ppermute | solution.py:763
  45.6 18.8 %pair_up.1 = (f32[256,256]{1,0:T(8,128)S(1)}, f32[256,256]{1,0:T(8,128)S(1)}, f32[8,256]{1,0:T(8,128)S(1)}, f32[264,128]{1,0:T(8,128)S(1)}) custom-call(f32[264,128]{1,0:T(8,128)S(1)} %add.11.mine_ref, f32[264,128]{1,0:T(8,128)S(1)} %collective-permute-done.7.other_ref, f32[256,256]{1,0:T(8,128)S(1)} %copy-done, f32[1,256]{1,0:T(1,128)S(1)} %bitcast.3), custom_call_target="tpu_custom_call" | custom-call | tf_op jit(solution)/shard_map/pair_up/pallas_call | solution.py:540
  64.5 0.1 collective-permute-start.8
  64.5 5.6 %collective-permute-done.8.incoming_ref = f32[264,128]{1,0:T(8,128)S(1)} collective-permute-done((f32[264,128]{1,0:T(8,128)S(1)}, f32[264,128]{1,0:T(8,128)S(1)}, u32[]{:S(2)}, u32[]{:S(2)}) %collective-permute-start.8) | collective-permute-done | bytes 135200 | tf_op jit(solution)/shard_map/ppermute | solution.py:775
  70.2 2.5 %finish.1 = (f32[1,256]{1,0:T(1,128)}, f32[24,256]{1,0:T(8,128)S(1)}) custom-call(f32[264,128]{1,0:T(8,128)S(1)} %collective-permute-done.8.incoming_ref, f32[256,256]{1,0:T(8,128)S(1)} %get-tuple-element.13.a_ref, f32[256,256]{1,0:T(8,128)S(1)} %get-tuple-element.14.j_ref, f32[8,256]{1,0:T(8,128)S(1)} %get-tuple-element.15.vec_ref, ...), custom_call_target="tpu_custom_call" | custom-call | tf_op jit(solution)/shard_map/finish/pallas_call | solution.py:600
  72.6 1.7 %collective-permute-start.10 = (f32[24,256]{1,0:T(8,128)S(1)}, f32[24,256]{1,0:T(8,128)S(1)}, u32[]{:S(2)}, u32[]{:S(2)}) collective-permute-start(f32[24,256]{1,0:T(8,128)S(1)} %get-tuple-element.17.own_ref), channel_id=1, source_target_pairs={{0,8},{1,2},{2,1},{3,4},{4,3},{5,6},{6,5},{7,15},{8,0},{9,10},{10,... | collective-permute-start | bytes 73736 | tf_op jit(solution)/shard_map/ppermute | solution.py:742
  74.3 1.6 %collective-permute-start.9 = (f32[24,256]{1,0:T(8,128)S(1)}, f32[24,256]{1,0:T(8,128)S(1)}, u32[]{:S(2)}, u32[]{:S(2)}) collective-permute-start(f32[24,256]{1,0:T(8,128)S(1)} %get-tuple-element.17.own_ref), channel_id=1, source_target_pairs={{0,1},{1,0},{2,3},{3,2},{4,5},{5,4},{6,7},{7,6},{8,9},{9,8},{10,11... | collective-permute-start | bytes 73736 | tf_op jit(solution)/shard_map/ppermute | solution.py:739
  75.9 1.5 %collective-permute-done.10.second_ref = f32[24,256]{1,0:T(8,128)S(1)} collective-permute-done((f32[24,256]{1,0:T(8,128)S(1)}, f32[24,256]{1,0:T(8,128)S(1)}, u32[]{:S(2)}, u32[]{:S(2)}) %collective-permute-start.10) | collective-permute-done | bytes 24608 | tf_op jit(solution)/shard_map/ppermute | solution.py:742
  77.4 0.8 collective-permute-done.9.first_ref
  78.2 1.2 %propagate_sum.1 = f32[3,8,256]{2,1,0:T(8,128)} custom-call(f32[24,256]{1,0:T(8,128)S(1)} %get-tuple-element.17.own_ref, f32[24,256]{1,0:T(8,128)S(1)} %collective-permute-done.9.first_ref, f32[24,256]{1,0:T(8,128)S(1)} %collective-permute-done.10.second_ref, f32[16,256]{1,0:T(8,128)S(1)} %copy-done.1, ...), custom_call_target="tpu_custom_call" | custom-call | tf_op jit(solution)/shard_map/propagate_sum/pallas_call | solution.py:647
  (12 shorter events, 0.1 us)
Async XLA Ops:
  2.0 6.0 %collective-permute-start.1 = (f32[16,256]{1,0:T(8,128)}, f32[16,256]{1,0:T(8,128)S(1)}, u32[]{:S(2)}, u32[]{:S(2)}) collective-permute-start(f32[16,256]{1,0:T(8,128)} %gather_info.1.own_ref.mo), channel_id=1, source_target_pairs={{0,1},{1,0},{2,3},{3,2},{4,5},{5,4},{6,7},{7,6},{8,9},{9,8},{10,11... | collective-permute-start | bytes 49160 | tf_op jit(solution)/shard_map/ppermute | solution.py:739
  2.6 8.5 %collective-permute-start = (f32[16,256]{1,0:T(8,128)}, f32[16,256]{1,0:T(8,128)S(1)}, u32[]{:S(2)}, u32[]{:S(2)}) collective-permute-start(f32[16,256]{1,0:T(8,128)} %gather_info.1.own_ref.mo), channel_id=1, source_target_pairs={{0,8},{1,2},{2,1},{3,4},{4,3},{5,6},{6,5},{7,15},{8,0},{9,10},{10,... | collective-permute-start | bytes 49160 | tf_op jit(solution)/shard_map/ppermute | solution.py:742
  5.1 2.9 %copy-start.1 = (f32[16,256]{1,0:T(8,128)S(1)}, f32[16,256]{1,0:T(8,128)}, u32[]{:S(2)}) copy-start(f32[16,256]{1,0:T(8,128)} %gather_info.1.own_ref.mo) | copy-start | bytes 49156
  14.2 13.4 %copy-start.2 = (f32[1,256]{1,0:T(1,128)S(1)}, f32[1,256]{1,0:T(1,128)}, u32[]{:S(2)}) copy-start(f32[1,256]{1,0:T(1,128)} %weight_ref.1) | copy-start | bytes 3076
  14.2 13.3 %copy-start.3 = (f32[1,256]{1,0:T(1,128)S(1)}, f32[1,256]{1,0:T(1,128)}, u32[]{:S(2)}) copy-start(f32[1,256]{1,0:T(1,128)} %innovation_ref.1) | copy-start | bytes 3076
  14.2 31.4 %copy-start = (f32[256,256]{1,0:T(8,128)S(1)}, f32[256,256]{1,0:T(8,128)}, u32[]{:S(2)}) copy-start(f32[256,256]{1,0:T(8,128)} %transition_ref.1) | copy-start | bytes 786436
  14.2 31.4 %copy-start.4 = (f32[256]{0:T(256)S(1)}, f32[256]{0:T(256)}, u32[]{:S(2)}) copy-start(f32[256]{0:T(256)} %param.15) | copy-start | bytes 3076
  14.2 8.5 %collective-permute-start.3 = (f32[256,256]{1,0:T(8,128)S(1)}, f32[256,256]{1,0:T(8,128)S(1)}, u32[]{:S(2)}, u32[]{:S(2)}) collective-permute-start(f32[256,256]{1,0:T(8,128)S(1)} %shard_map.96), channel_id=1, source_target_pairs={{0,8},{1,2},{2,1},{3,4},{4,3},{5,6},{6,5},{7,15},{8,0},{9,10},{10,... | collective-permute-start | bytes 786440 | tf_op jit(solution)/shard_map/ppermute | solution.py:742
  14.7 12.8 %collective-permute-start.2 = (f32[256,256]{1,0:T(8,128)S(1)}, f32[256,256]{1,0:T(8,128)S(1)}, u32[]{:S(2)}, u32[]{:S(2)}) collective-permute-start(f32[256,256]{1,0:T(8,128)S(1)} %shard_map.95), channel_id=1, source_target_pairs={{0,1},{1,0},{2,3},{3,2},{4,5},{5,4},{6,7},{7,6},{8,9},{9,8},{10,11... | collective-permute-start | bytes 786440 | tf_op jit(solution)/shard_map/ppermute | solution.py:739
  27.9 5.1 %collective-permute-start.4 = (f32[264,128]{1,0:T(8,128)S(1)}, f32[264,128]{1,0:T(8,128)S(1)}, u32[]{:S(2)}, u32[]{:S(2)}) collective-permute-start(f32[264,128]{1,0:T(8,128)S(1)} %gram.1), channel_id=1, source_target_pairs={{0,1},{1,0},{2,3},{3,2},{4,5},{5,4},{6,7},{7,6},{8,9},{9,8},{10,11... | collective-permute-start | bytes 405512 | tf_op jit(solution)/shard_map/ppermute | solution.py:760
  33.0 5.1 %collective-permute-start.5 = (f32[264,128]{1,0:T(8,128)S(1)}, f32[264,128]{1,0:T(8,128)S(1)}, u32[]{:S(2)}, u32[]{:S(2)}) collective-permute-start(f32[264,128]{1,0:T(8,128)S(1)} %add.9), channel_id=1, source_target_pairs={{0,2},{1,3},{2,0},{3,1},{4,6},{5,7},{6,4},{7,5},{8,10},{9,11},{10,... | collective-permute-start | bytes 405512 | tf_op jit(solution)/shard_map/ppermute | solution.py:760
  38.1 6.1 %collective-permute-start.6 = (f32[264,128]{1,0:T(8,128)S(1)}, f32[264,128]{1,0:T(8,128)S(1)}, u32[]{:S(2)}, u32[]{:S(2)}) collective-permute-start(f32[264,128]{1,0:T(8,128)S(1)} %add.10), channel_id=1, source_target_pairs={{0,4},{1,5},{2,6},{3,7},{4,0},{5,1},{6,2},{7,3},{8,12},{9,13},{10,... | collective-permute-start | bytes 405512 | tf_op jit(solution)/shard_map/ppermute | solution.py:760
  44.2 1.4 %collective-permute-start.7 = (f32[264,128]{1,0:T(8,128)S(1)}, f32[264,128]{1,0:T(8,128)S(1)}, u32[]{:S(2)}, u32[]{:S(2)}) collective-permute-start(f32[264,128]{1,0:T(8,128)S(1)} %add.11.mine_ref), channel_id=1, source_target_pairs={{0,8},{8,0},{16,24},{24,16},{1,9},{9,1},{17,25},{25,17},{2,10},{10... | collective-permute-start | bytes 405512 | tf_op jit(solution)/shard_map/ppermute | solution.py:763
  64.5 5.7 %collective-permute-start.8 = (f32[264,128]{1,0:T(8,128)S(1)}, f32[264,128]{1,0:T(8,128)S(1)}, u32[]{:S(2)}, u32[]{:S(2)}) collective-permute-start(f32[264,128]{1,0:T(8,128)S(1)} %get-tuple-element.12), channel_id=1, source_target_pairs={{0,16},{8,24},{16,0},{24,8},{1,17},{9,25},{17,1},{25,9},{2,18},{10... | collective-permute-start | bytes 405512 | tf_op jit(solution)/shard_map/ppermute | solution.py:775
  72.6 4.7 %collective-permute-start.10 = (f32[24,256]{1,0:T(8,128)S(1)}, f32[24,256]{1,0:T(8,128)S(1)}, u32[]{:S(2)}, u32[]{:S(2)}) collective-permute-start(f32[24,256]{1,0:T(8,128)S(1)} %get-tuple-element.17.own_ref), channel_id=1, source_target_pairs={{0,8},{1,2},{2,1},{3,4},{4,3},{5,6},{6,5},{7,15},{8,0},{9,10},{10,... | collective-permute-start | bytes 73736 | tf_op jit(solution)/shard_map/ppermute | solution.py:742
  74.3 3.8 %collective-permute-start.9 = (f32[24,256]{1,0:T(8,128)S(1)}, f32[24,256]{1,0:T(8,128)S(1)}, u32[]{:S(2)}, u32[]{:S(2)}) collective-permute-start(f32[24,256]{1,0:T(8,128)S(1)} %get-tuple-element.17.own_ref), channel_id=1, source_target_pairs={{0,1},{1,0},{2,3},{3,2},{4,5},{5,4},{6,7},{7,6},{8,9},{9,8},{10,11... | collective-permute-start | bytes 73736 | tf_op jit(solution)/shard_map/ppermute | solution.py:739

commit v5 on v4

--- a/solution.py
+++ b/solution.py
@@ -55,6 +55,16 @@
 def dot3(left, right, dims=NN):
     (lh, ll), (rh, rl) = left, right
     return dot1(lh, rh, dims) + (dot1(lh, rl, dims) + dot1(ll, rh, dims))
+
+
+def tile_dot(rows, parts, dims=NN):
+    both = jnp.concatenate(halves(rows), axis=0)
+    result = dot1(both, parts[0], dims) + dot1(both, parts[1], dims)
+    return result[:SUB] + result[SUB:]
+
+
+def row_dot(row, parts, dims=NN):
+    return tile_dot(jnp.broadcast_to(row, (SUB, row.shape[1])), parts, dims)[0:1]
 
 
 def before_after(first, second):
@@ -435,8 +445,8 @@
     moved = dot3(both, part)
     current = rho * (start + moved[:SUB])
     part = halves(rho * moved[SUB:] - last * eye)
-    once = dot3(halves(current), part)
-    quick = current + once + dot3(halves(once), part)
+    once = tile_dot(current, part)
+    quick = current + once + tile_dot(once, part)
 
     def careful():
         inverse = invert_any(matrix, parts, c0, c1, error, eye)
@@ -454,10 +464,6 @@
 def column(row):
     size = row.shape[1]
     return jnp.broadcast_to(row, (size, size)).T
-
-
-def row_dot(row, parts, dims=NN):
-    return dot3(halves(jnp.broadcast_to(row, (SUB, row.shape[1]))), parts, dims)[0:1]
 
 
 def pair_kernel(
@@ -584,7 +590,7 @@
     matrix = crossed[:size]
     target = jnp.broadcast_to(vec_ref[1:2], (SUB, size)) - crossed[size:]
     s = solve_shifted(matrix, halves(matrix), target)
-    mean = (dot3(halves(s), halves(outer[:size])) + outer[size:] + vec_ref[0:1])[0:1]
+    mean = (tile_dot(s, halves(outer[:size])) + outer[size:] + vec_ref[0:1])[0:1]
     mean_ref[...] = mean
     pieces = jnp.concatenate(list(thirds(mean)) + [jnp.zeros((5, size), BF16)], axis=0)
     for f in range(3):
@@ -628,17 +634,24 @@
     last_row = jnp.where(tile == tiles - 1, 2 * rows, total)
     inside = ((y_iota >= first_row) & (y_iota < last_row)).astype(F32)
 
-    def diff_cols(values):
-        return pltpu.roll(values, nx - 1, 1) - pltpu.roll(values, 1, 1)
-
-    def diff_rows(values):
-        return pltpu.roll(values, total - 1, 0) - pltpu.roll(values, 1, 0)
-
+    def cols(values, by):
+        return pltpu.roll(values, by % nx, 1)
+
+    def lines(values, by):
+        return pltpu.roll(values, by % total, 0)
+
+    after, before = lines(inside, -1), lines(inside, 1)
     for _ in range(STEPS):
-        east = u + CORIOLIS * v - A_COEF * diff_cols(h)
-        north = (v - CORIOLIS * u - A_COEF * diff_rows(h)) * inside
-        h = h - depth * (diff_cols(east) + diff_rows(north))
-        u, v = east, north
+        east, north = u + CORIOLIS * v, v - CORIOLIS * u
+        slope_cols = cols(east, -1) - cols(east, 1) - A_COEF * (
+            (cols(h, -2) - h) - (h - cols(h, 2))
+        )
+        slope_lines = after * (lines(north, -1) - A_COEF * (lines(h, -2) - h)) - before * (
+            lines(north, 1) - A_COEF * (h - lines(h, 2))
+        )
+        u = east - A_COEF * (cols(h, -1) - cols(h, 1))
+        v = inside * (north - A_COEF * (lines(h, -1) - lines(h, 1)))
+        h = h - depth * (slope_cols + slope_lines)
     for f, values in enumerate((h, u, v)):
         out_ref[f] = values[rows : 2 * rows]
 
@@ -757,9 +770,15 @@
     packed = gram(part_own, got_near, got_far, obs_weight, innovation)
     bit = 1
     while bit < tiles:
-        packed = packed + lax.ppermute(packed, "tile", [(i, i ^ bit) for i in range(tiles)])
-        bit *= 2
-
+        reach = 3 if bit * 2 < tiles else 1
+        parts = [
+            lax.ppermute(packed, "tile", [(i, i ^ (bit * by)) for i in range(tiles)])
+            for by in range(1, reach + 1)
+        ]
+        packed = packed + parts[0]
+        if reach == 3:
+            packed = packed + (parts[1] + parts[2])
+        bit *= reach + 1
     other = lax.ppermute(packed, "tm", [(i, i ^ 1) for i in range(windows)])
     pairs = windows // 2
     a, j, vec, prefix, *more = pair_up(

time: 80.8 us -> 80.5 us (level)
  the two profiles are of different devices: /device:TPU:14 before, /device:TPU:22 now
where the time goes in v5:
time: 80.5 us; the launch traced here: 80.3 us
  Pallas kernels  35.9 us (45%)
  waiting for transfers between devices  29.8 us (37%)
  starting transfers between devices  13.7 us (17%)
    pallas_call x1, Pallas kernels, pair_up(): pl.pallas_call(functools.partial(pair_kernel, full), out_shape=shapes, in...  18.8 us
    ppermute x4, waiting for transfers between devices, on_device(): lax.ppermute(packed, 'tile', [(i, i ^ bit * by) for i in range(tiles)])  10.7 us
    pallas_call x3, Pallas kernels, project(): pl.pallas_call(functools.partial(project_kernel, slot, rows, nx), out_sha...  9.12 us
    ppermute x3, starting transfers between devices, swap_far(): return lax.ppermute(array, ('tm', 'tile'), far)  7.54 us
    ppermute x3, waiting for transfers between devices, swap_near(): return lax.ppermute(array, 'tile', near)  6.77 us
    ppermute x1, waiting for transfers between devices, on_device(): incoming = lax.ppermute(prefix, 'tm', hop)  5.63 us
    ppermute x3, waiting for transfers between devices, swap_far(): return lax.ppermute(array, ('tm', 'tile'), far)  5.39 us
    ppermute x4, starting transfers between devices, on_device(): lax.ppermute(packed, 'tile', [(i, i ^ bit * by) for i in range(tiles)])  3.95 us
  transfers between devices with their start and end apart: 12, of which 10 were waited for; matrix products, arithmetic and copies ran while one was open for 0% of the time, Pallas kernels for 11%

profile of v5, /device:TPU:22, one launch (start us, length us, event | category | flops | bytes accessed | tf_op | source)
XLA Modules:
  0.0 80.3 jit_solution(15739265505995142127)
XLA Ops:
  0.6 1.3 %gather_info.1.own_ref.mo = f32[16,256]{1,0:T(8,128)} custom-call(f32[8,256]{1,0:T(8,128)} %depth_ref.1, s32[1,256]{1,0:T(1,128)} %cells_ref.1, s32[1,256]{1,0:T(1,128)} %fields_ref.1), custom_call_target="tpu_custom_call" | custom-call | tf_op jit(solution)/shard_map/gather_info/pallas_call | solution.py:722
  2.0 0.6 collective-permute-start.1
  2.6 2.5 %collective-permute-start = (f32[16,256]{1,0:T(8,128)}, f32[16,256]{1,0:T(8,128)S(1)}, u32[]{:S(2)}, u32[]{:S(2)}) collective-permute-start(f32[16,256]{1,0:T(8,128)} %gather_info.1.own_ref.mo), channel_id=1, source_target_pairs={{0,8},{1,2},{2,1},{3,4},{4,3},{5,6},{6,5},{7,15},{8,0},{9,10},{10,... | collective-permute-start | bytes 49160 | tf_op jit(solution)/shard_map/ppermute | solution.py:755
  5.1 2.9 %lay_out.1.basis_ref = bf16[3,256,2048]{2,1,0:T(8,128)(2,1)S(1)} custom-call(bf16[3,256,8,256]{3,2,1,0:T(8,128)(2,1)} %bitcast.4), custom_call_target="tpu_custom_call" | custom-call | tf_op jit(solution)/shard_map/lay_out/pallas_call | solution.py:691
  8.0 3.1 %shard_map.95 = f32[256,256]{1,0:T(8,128)S(1)} custom-call(f32[16,256]{1,0:T(8,128)S(1)} %copy-done.1, f32[16,256]{1,0:T(8,128)S(1)} %collective-permute-done.1.first_ref.second_ref.mf, f32[16,256]{1,0:T(8,128)S(1)} %collective-permute-done.1.first_ref.second_ref.mf, bf16[3,256,2048]{2,1,0:T(8,128)(2,1)S(1)} %lay_out.1.basis_ref), custom_call_target="tpu_custom_call" | custom-call | flops 1610612736 | bytes 3145728 | tf_op jit(solution)/shard_map/pallas_call | solution.py:254
  11.1 3.1 %shard_map.96 = f32[256,256]{1,0:T(8,128)S(1)} custom-call(f32[16,256]{1,0:T(8,128)S(1)} %copy-done.1, f32[16,256]{1,0:T(8,128)S(1)} %collective-permute-done.first_ref.second_ref.ms, f32[16,256]{1,0:T(8,128)S(1)} %collective-permute-done.first_ref.second_ref.ms, bf16[3,256,2048]{2,1,0:T(8,128)(2,1)S(1)} %lay_out.1.basis_ref), custom_call_target="tpu_custom_call" | custom-call | flops 1610612736 | bytes 3145728 | tf_op jit(solution)/shard_map/pallas_call | solution.py:254
  14.2 0.0 copy-start
  14.2 0.0 copy-start.4
  14.2 0.5 collective-permute-start.3
  14.7 1.5 %collective-permute-start.2 = (f32[256,256]{1,0:T(8,128)S(1)}, f32[256,256]{1,0:T(8,128)S(1)}, u32[]{:S(2)}, u32[]{:S(2)}) collective-permute-start(f32[256,256]{1,0:T(8,128)S(1)} %shard_map.95), channel_id=1, source_target_pairs={{0,1},{1,0},{2,3},{3,2},{4,5},{5,4},{6,7},{7,6},{8,9},{9,8},{10,11... | collective-permute-start | bytes 786440 | tf_op jit(solution)/shard_map/ppermute | solution.py:752
  16.2 3.0 %shard_map.97.own_ref = f32[256,256]{1,0:T(8,128)S(1)} custom-call(f32[16,256]{1,0:T(8,128)S(1)} %copy-done.1, f32[16,256]{1,0:T(8,128)S(1)} %collective-permute-done.1.first_ref.second_ref.mf, f32[16,256]{1,0:T(8,128)S(1)} %collective-permute-done.first_ref.second_ref.ms, bf16[3,256,2048]{2,1,0:T(8,128)(2,1)S(1)} %lay_out.1.basis_ref), custom_call_target="tpu_custom_call" | custom-call | flops 1610612736 | bytes 3145728 | tf_op jit(solution)/shard_map/pallas_call | solution.py:254
  19.2 3.6 %collective-permute-done.3.second_ref = f32[256,256]{1,0:T(8,128)S(1)} collective-permute-done((f32[256,256]{1,0:T(8,128)S(1)}, f32[256,256]{1,0:T(8,128)S(1)}, u32[]{:S(2)}, u32[]{:S(2)}) %collective-permute-start.3) | collective-permute-done | bytes 262176 | tf_op jit(solution)/shard_map/ppermute | solution.py:755
  22.8 4.8 %collective-permute-done.2.first_ref = f32[256,256]{1,0:T(8,128)S(1)} collective-permute-done((f32[256,256]{1,0:T(8,128)S(1)}, f32[256,256]{1,0:T(8,128)S(1)}, u32[]{:S(2)}, u32[]{:S(2)}) %collective-permute-start.2) | collective-permute-done | bytes 262176 | tf_op jit(solution)/shard_map/ppermute | solution.py:752
  27.5 0.4 gram.1
  27.9 1.2 %collective-permute-start.6 = (f32[264,128]{1,0:T(8,128)S(1)}, f32[264,128]{1,0:T(8,128)S(1)}, u32[]{:S(2)}, u32[]{:S(2)}) collective-permute-start(f32[264,128]{1,0:T(8,128)S(1)} %gram.1), channel_id=1, source_target_pairs={{0,3},{1,2},{2,1},{3,0},{4,7},{5,6},{6,5},{7,4},{8,11},{9,10},{10,... | collective-permute-start | bytes 405512 | tf_op jit(solution)/shard_map/ppermute | solution.py:775
  29.1 0.4 collective-permute-start.5
  29.6 1.9 %collective-permute-start.4 = (f32[264,128]{1,0:T(8,128)S(1)}, f32[264,128]{1,0:T(8,128)S(1)}, u32[]{:S(2)}, u32[]{:S(2)}) collective-permute-start(f32[264,128]{1,0:T(8,128)S(1)} %gram.1), channel_id=1, source_target_pairs={{0,1},{1,0},{2,3},{3,2},{4,5},{5,4},{6,7},{7,6},{8,9},{9,8},{10,11... | collective-permute-start | bytes 405512 | tf_op jit(solution)/shard_map/ppermute | solution.py:775
  31.5 3.6 %collective-permute-done.6 = f32[264,128]{1,0:T(8,128)S(1)} collective-permute-done((f32[264,128]{1,0:T(8,128)S(1)}, f32[264,128]{1,0:T(8,128)S(1)}, u32[]{:S(2)}, u32[]{:S(2)}) %collective-permute-start.6) | collective-permute-done | bytes 135200 | tf_op jit(solution)/shard_map/ppermute | solution.py:775
  35.1 0.9 %collective-permute-done.5 = f32[264,128]{1,0:T(8,128)S(1)} collective-permute-done((f32[264,128]{1,0:T(8,128)S(1)}, f32[264,128]{1,0:T(8,128)S(1)}, u32[]{:S(2)}, u32[]{:S(2)}) %collective-permute-start.5) | collective-permute-done | bytes 135200 | tf_op jit(solution)/shard_map/ppermute | solution.py:775
  36.0 0.5 collective-permute-done.4
  36.5 0.4 collective-permute-start.7
  36.9 5.6 %collective-permute-done.7 = f32[264,128]{1,0:T(8,128)S(1)} collective-permute-done((f32[264,128]{1,0:T(8,128)S(1)}, f32[264,128]{1,0:T(8,128)S(1)}, u32[]{:S(2)}, u32[]{:S(2)}) %collective-permute-start.7) | collective-permute-done | bytes 135200 | tf_op jit(solution)/shard_map/ppermute | solution.py:775
  42.6 0.1 collective-permute-start.8
  42.7 1.3 %collective-permute-done.8.other_ref = f32[264,128]{1,0:T(8,128)S(1)} collective-permute-done((f32[264,128]{1,0:T(8,128)S(1)}, f32[264,128]{1,0:T(8,128)S(1)}, u32[]{:S(2)}, u32[]{:S(2)}) %collective-permute-start.8) | collective-permute-done | bytes 135200 | tf_op jit(solution)/shard_map/ppermute | solution.py:782
  44.0 18.8 %pair_up.1 = (f32[256,256]{1,0:T(8,128)S(1)}, f32[256,256]{1,0:T(8,128)S(1)}, f32[8,256]{1,0:T(8,128)S(1)}, f32[264,128]{1,0:T(8,128)S(1)}) custom-call(f32[264,128]{1,0:T(8,128)S(1)} %add.15.mine_ref, f32[264,128]{1,0:T(8,128)S(1)} %collective-permute-done.8.other_ref, f32[256,256]{1,0:T(8,128)S(1)} %copy-done, f32[1,256]{1,0:T(1,128)S(1)} %bitcast.3), custom_call_target="tpu_custom_call" | custom-call | tf_op jit(solution)/shard_map/pair_up/pallas_call | solution.py:546
  62.8 0.1 collective-permute-start.9
  62.9 5.6 %collective-permute-done.9.incoming_ref = f32[264,128]{1,0:T(8,128)S(1)} collective-permute-done((f32[264,128]{1,0:T(8,128)S(1)}, f32[264,128]{1,0:T(8,128)S(1)}, u32[]{:S(2)}, u32[]{:S(2)}) %collective-permute-start.9) | collective-permute-done | bytes 135200 | tf_op jit(solution)/shard_map/ppermute | solution.py:794
  68.5 2.5 %finish.1 = (f32[1,256]{1,0:T(1,128)}, f32[24,256]{1,0:T(8,128)S(1)}) custom-call(f32[264,128]{1,0:T(8,128)S(1)} %collective-permute-done.9.incoming_ref, f32[256,256]{1,0:T(8,128)S(1)} %get-tuple-element.13.a_ref, f32[256,256]{1,0:T(8,128)S(1)} %get-tuple-element.14.j_ref, f32[8,256]{1,0:T(8,128)S(1)} %get-tuple-element.15.vec_ref, ...), custom_call_target="tpu_custom_call" | custom-call | tf_op jit(solution)/shard_map/finish/pallas_call | solution.py:606
  71.0 4.6 %collective-permute-start.11 = (f32[24,256]{1,0:T(8,128)S(1)}, f32[24,256]{1,0:T(8,128)S(1)}, u32[]{:S(2)}, u32[]{:S(2)}) collective-permute-start(f32[24,256]{1,0:T(8,128)S(1)} %get-tuple-element.17.own_ref), channel_id=1, source_target_pairs={{0,8},{1,2},{2,1},{3,4},{4,3},{5,6},{6,5},{7,15},{8,0},{9,10},{10,... | collective-permute-start | bytes 73736 | tf_op jit(solution)/shard_map/ppermute | solution.py:755
  75.5 1.8 %collective-permute-done.11.second_ref = f32[24,256]{1,0:T(8,128)S(1)} collective-permute-done((f32[24,256]{1,0:T(8,128)S(1)}, f32[24,256]{1,0:T(8,128)S(1)}, u32[]{:S(2)}, u32[]{:S(2)}) %collective-permute-start.11) | collective-permute-done | bytes 24608 | tf_op jit(solution)/shard_map/ppermute | solution.py:755
  77.4 2.0 %collective-permute-done.10.first_ref = f32[24,256]{1,0:T(8,128)S(1)} collective-permute-done((f32[24,256]{1,0:T(8,128)S(1)}, f32[24,256]{1,0:T(8,128)S(1)}, u32[]{:S(2)}, u32[]{:S(2)}) %collective-permute-start.10) | collective-permute-done | bytes 24608 | tf_op jit(solution)/shard_map/ppermute | solution.py:752
  79.4 0.9 %propagate_sum.1 = f32[3,8,256]{2,1,0:T(8,128)} custom-call(f32[24,256]{1,0:T(8,128)S(1)} %get-tuple-element.17.own_ref, f32[24,256]{1,0:T(8,128)S(1)} %collective-permute-done.10.first_ref, f32[24,256]{1,0:T(8,128)S(1)} %collective-permute-done.11.second_ref, f32[16,256]{1,0:T(8,128)S(1)} %copy-done.1, ...), custom_call_target="tpu_custom_call" | custom-call | tf_op jit(solution)/shard_map/propagate_sum/pallas_call | solution.py:660
  (13 shorter events, 0.1 us)
Async XLA Ops:
  2.0 6.0 %collective-permute-start.1 = (f32[16,256]{1,0:T(8,128)}, f32[16,256]{1,0:T(8,128)S(1)}, u32[]{:S(2)}, u32[]{:S(2)}) collective-permute-start(f32[16,256]{1,0:T(8,128)} %gather_info.1.own_ref.mo), channel_id=1, source_target_pairs={{0,1},{1,0},{2,3},{3,2},{4,5},{5,4},{6,7},{7,6},{8,9},{9,8},{10,11... | collective-permute-start | bytes 49160 | tf_op jit(solution)/shard_map/ppermute | solution.py:752
  2.6 8.5 %collective-permute-start = (f32[16,256]{1,0:T(8,128)}, f32[16,256]{1,0:T(8,128)S(1)}, u32[]{:S(2)}, u32[]{:S(2)}) collective-permute-start(f32[16,256]{1,0:T(8,128)} %gather_info.1.own_ref.mo), channel_id=1, source_target_pairs={{0,8},{1,2},{2,1},{3,4},{4,3},{5,6},{6,5},{7,15},{8,0},{9,10},{10,... | collective-permute-start | bytes 49160 | tf_op jit(solution)/shard_map/ppermute | solution.py:755
  5.1 2.9 %copy-start.1 = (f32[16,256]{1,0:T(8,128)S(1)}, f32[16,256]{1,0:T(8,128)}, u32[]{:S(2)}) copy-start(f32[16,256]{1,0:T(8,128)} %gather_info.1.own_ref.mo) | copy-start | bytes 49156
  14.2 13.4 %copy-start.2 = (f32[1,256]{1,0:T(1,128)S(1)}, f32[1,256]{1,0:T(1,128)}, u32[]{:S(2)}) copy-start(f32[1,256]{1,0:T(1,128)} %weight_ref.1) | copy-start | bytes 3076
  14.2 13.4 %copy-start.3 = (f32[1,256]{1,0:T(1,128)S(1)}, f32[1,256]{1,0:T(1,128)}, u32[]{:S(2)}) copy-start(f32[1,256]{1,0:T(1,128)} %innovation_ref.1) | copy-start | bytes 3076
  14.2 29.8 %copy-start = (f32[256,256]{1,0:T(8,128)S(1)}, f32[256,256]{1,0:T(8,128)}, u32[]{:S(2)}) copy-start(f32[256,256]{1,0:T(8,128)} %transition_ref.1) | copy-start | bytes 786436
  14.2 29.8 %copy-start.4 = (f32[256]{0:T(256)S(1)}, f32[256]{0:T(256)}, u32[]{:S(2)}) copy-start(f32[256]{0:T(256)} %param.15) | copy-start | bytes 3076
  14.2 8.5 %collective-permute-start.3 = (f32[256,256]{1,0:T(8,128)S(1)}, f32[256,256]{1,0:T(8,128)S(1)}, u32[]{:S(2)}, u32[]{:S(2)}) collective-permute-start(f32[256,256]{1,0:T(8,128)S(1)} %shard_map.96), channel_id=1, source_target_pairs={{0,8},{1,2},{2,1},{3,4},{4,3},{5,6},{6,5},{7,15},{8,0},{9,10},{10,... | collective-permute-start | bytes 786440 | tf_op jit(solution)/shard_map/ppermute | solution.py:755
  14.7 12.8 %collective-permute-start.2 = (f32[256,256]{1,0:T(8,128)S(1)}, f32[256,256]{1,0:T(8,128)S(1)}, u32[]{:S(2)}, u32[]{:S(2)}) collective-permute-start(f32[256,256]{1,0:T(8,128)S(1)} %shard_map.95), channel_id=1, source_target_pairs={{0,1},{1,0},{2,3},{3,2},{4,5},{5,4},{6,7},{7,6},{8,9},{9,8},{10,11... | collective-permute-start | bytes 786440 | tf_op jit(solution)/shard_map/ppermute | solution.py:752
  27.9 7.2 %collective-permute-start.6 = (f32[264,128]{1,0:T(8,128)S(1)}, f32[264,128]{1,0:T(8,128)S(1)}, u32[]{:S(2)}, u32[]{:S(2)}) collective-permute-start(f32[264,128]{1,0:T(8,128)S(1)} %gram.1), channel_id=1, source_target_pairs={{0,3},{1,2},{2,1},{3,0},{4,7},{5,6},{6,5},{7,4},{8,11},{9,10},{10,... | collective-permute-start | bytes 405512 | tf_op jit(solution)/shard_map/ppermute | solution.py:775
  29.1 6.8 %collective-permute-start.5 = (f32[264,128]{1,0:T(8,128)S(1)}, f32[264,128]{1,0:T(8,128)S(1)}, u32[]{:S(2)}, u32[]{:S(2)}) collective-permute-start(f32[264,128]{1,0:T(8,128)S(1)} %gram.1), channel_id=1, source_target_pairs={{0,2},{1,3},{2,0},{3,1},{4,6},{5,7},{6,4},{7,5},{8,10},{9,11},{10,... | collective-permute-start | bytes 405512 | tf_op jit(solution)/shard_map/ppermute | solution.py:775
  29.6 6.9 %collective-permute-start.4 = (f32[264,128]{1,0:T(8,128)S(1)}, f32[264,128]{1,0:T(8,128)S(1)}, u32[]{:S(2)}, u32[]{:S(2)}) collective-permute-start(f32[264,128]{1,0:T(8,128)S(1)} %gram.1), channel_id=1, source_target_pairs={{0,1},{1,0},{2,3},{3,2},{4,5},{5,4},{6,7},{7,6},{8,9},{9,8},{10,11... | collective-permute-start | bytes 405512 | tf_op jit(solution)/shard_map/ppermute | solution.py:775
  36.5 6.0 %collective-permute-start.7 = (f32[264,128]{1,0:T(8,128)S(1)}, f32[264,128]{1,0:T(8,128)S(1)}, u32[]{:S(2)}, u32[]{:S(2)}) collective-permute-start(f32[264,128]{1,0:T(8,128)S(1)} %add_add_fusion), channel_id=1, source_target_pairs={{0,4},{1,5},{2,6},{3,7},{4,0},{5,1},{6,2},{7,3},{8,12},{9,13},{10,... | collective-permute-start | bytes 405512 | tf_op jit(solution)/shard_map/ppermute | solution.py:775
  42.6 1.4 %collective-permute-start.8 = (f32[264,128]{1,0:T(8,128)S(1)}, f32[264,128]{1,0:T(8,128)S(1)}, u32[]{:S(2)}, u32[]{:S(2)}) collective-permute-start(f32[264,128]{1,0:T(8,128)S(1)} %add.15.mine_ref), channel_id=1, source_target_pairs={{0,8},{8,0},{16,24},{24,16},{1,9},{9,1},{17,25},{25,17},{2,10},{10... | collective-permute-start | bytes 405512 | tf_op jit(solution)/shard_map/ppermute | solution.py:782
  62.8 5.7 %collective-permute-start.9 = (f32[264,128]{1,0:T(8,128)S(1)}, f32[264,128]{1,0:T(8,128)S(1)}, u32[]{:S(2)}, u32[]{:S(2)}) collective-permute-start(f32[264,128]{1,0:T(8,128)S(1)} %get-tuple-element.12), channel_id=1, source_target_pairs={{0,16},{8,24},{16,0},{24,8},{1,17},{9,25},{17,1},{25,9},{2,18},{10... | collective-permute-start | bytes 405512 | tf_op jit(solution)/shard_map/ppermute | solution.py:794
  71.0 6.4 %collective-permute-start.11 = (f32[24,256]{1,0:T(8,128)S(1)}, f32[24,256]{1,0:T(8,128)S(1)}, u32[]{:S(2)}, u32[]{:S(2)}) collective-permute-start(f32[24,256]{1,0:T(8,128)S(1)} %get-tuple-element.17.own_ref), channel_id=1, source_target_pairs={{0,8},{1,2},{2,1},{3,4},{4,3},{5,6},{6,5},{7,15},{8,0},{9,10},{10,... | collective-permute-start | bytes 73736 | tf_op jit(solution)/shard_map/ppermute | solution.py:755
  75.5 3.8 %collective-permute-start.10 = (f32[24,256]{1,0:T(8,128)S(1)}, f32[24,256]{1,0:T(8,128)S(1)}, u32[]{:S(2)}, u32[]{:S(2)}) collective-permute-start(f32[24,256]{1,0:T(8,128)S(1)} %get-tuple-element.17.own_ref), channel_id=1, source_target_pairs={{0,1},{1,0},{2,3},{3,2},{4,5},{5,4},{6,7},{7,6},{8,9},{9,8},{10,11... | collective-permute-start | bytes 73736 | tf_op jit(solution)/shard_map/ppermute | solution.py:752

commit v6 on v5

--- a/solution.py
+++ b/solution.py
@@ -466,22 +466,24 @@
     return jnp.broadcast_to(row, (size, size)).T
 
 
+def moves_and_maps(transition_ref, model_error_ref):
+    moves = jnp.where(lax.axis_index("tm") < 2, 0.0, 1.0)
+    weighted = transition_ref[...] / column(model_error_ref[...])
+    return moves, halves(weighted), halves(weighted.T)
+
+
 def pair_kernel(
     full, mine_ref, other_ref, transition_ref, model_error_ref,
-    a_ref, j_ref, vec_ref, prefix_ref, *more,
+    prefix_ref, c1_ref, a2_ref, inverse_ref, vec_ref, *more,
 ):
-    window = lax.axis_index("tm")
-    lower_core = lax.rem(window, 2) == 0
-    moves = jnp.where(window < 2, 0.0, 1.0)
+    lower_core = lax.rem(lax.axis_index("tm"), 2) == 0
     mine, other = mine_ref[...], other_ref[...]
     q2 = model_error_ref[...]
     size = q2.shape[1]
     root_row = jnp.sqrt(q2)
     root_col = column(root_row)
     transition = transition_ref[...]
-    weighted = transition / column(q2)
-    turned = halves(weighted.T)
-    weighted = halves(weighted)
+    _, weighted, turned = moves_and_maps(transition_ref, model_error_ref)
     mats, rows = [], []
     for packed in (jnp.where(lower_core, mine, other), jnp.where(lower_core, other, mine)):
         matrix, vector = load_packed(packed)
@@ -494,55 +496,65 @@
     k1 = dot3(low, turned)
     rest2 = halves(transition - a2)
     crossed = dot3(halves(k1), rest2)
-    a1 = moves * dot3(low, weighted)
     b1 = row_dot(rows[0], halves(p1)) * root_row
     b2 = row_dot(rows[1], halves(p2)) * root_row
+    a2_parts = halves(a2)
+    outer = halves(dot3(low, a2_parts, NT))
+    ahead = row_dot(b1, a2_parts, NT) + b2
+    behind = row_dot(b2, weighted) - row_dot(row_dot(b1, turned), rest2)
+    (inverse,) = invert_shifted([crossed], [halves(crossed)], 1)
+    parts = halves(inverse)
+    cov = dot3(a2_parts, halves(dot3(parts, outer))) + c2
+    s = row_dot(behind, parts)
+    mean = row_dot(s, outer) + ahead
+    store_packed(prefix_ref, cov, mean)
+    c1_ref[...] = c1
+    a2_ref[...] = a2
+    inverse_ref[...] = inverse
+    vec_ref[0:1] = b1
+    vec_ref[1:2] = s
+    vec_ref[2:3] = mean
+    vec_ref[3:SUB] = jnp.zeros((SUB - 3, size), F32)
+    if full:
+        more[0][...] = cov
+
+
+def rest_kernel(
+    full, c1_ref, a2_ref, inverse_ref, given_ref, transition_ref, model_error_ref,
+    a_ref, j_ref, vec_ref, *more,
+):
+    lower_core = lax.rem(lax.axis_index("tm"), 2) == 0
+    transition = transition_ref[...]
+    moves, weighted, turned = moves_and_maps(transition_ref, model_error_ref)
+    b1, s, mean = given_ref[0:1], given_ref[1:2], given_ref[2:3]
+    a1 = moves * dot3(halves(c1_ref[...]), weighted)
     eta1 = moves * row_dot(b1, weighted)
-    eta2 = row_dot(b2, weighted)
-    j2 = dot3(turned, rest2)
+    j2 = dot3(turned, halves(transition - a2_ref[...]))
     j1 = moves * dot3(turned, halves(transition - a1))
-    a2_parts = halves(a2)
     a1_parts = halves(a1)
-    j2_parts = halves(j2)
-    outer = dot3(low, a2_parts, NT)
-    ahead = row_dot(b1, a2_parts, NT) + b2
-    behind = eta2 - row_dot(b1, j2_parts)
-    spread = dot3(halves(a1.T), j2_parts)
-    (inverse,) = invert_shifted([crossed], [halves(crossed)], 1)
-    inverse = halves(inverse)
-    both = tuple(
-        jnp.concatenate(two, axis=1) for two in zip(a1_parts, halves(outer))
-    )
-    right = halves(dot3(inverse, both))
-    s = row_dot(behind, inverse)
-    ended = dot3(a2_parts, right)
-    ended_rows = row_dot(s, both)
-    trans, cov = ended[:, :size], ended[:, size:] + c2
-    prec = dot3(halves(spread), tuple(part[:, :size] for part in right)) + j1
-    info = ended_rows[:, :size] + eta1
-    mean = ended_rows[:, size:] + ahead
+    spread = dot3(halves(a1.T), halves(j2))
+    right = halves(dot3(halves(inverse_ref[...]), a1_parts))
+    trans = dot3(halves(a2_ref[...]), right)
+    prec = dot3(halves(spread), right) + j1
+    info = row_dot(s, a1_parts) + eta1
     a_ref[...] = jnp.where(lower_core, a1, trans)
     j_ref[...] = jnp.where(lower_core, j1, prec)
     vec_ref[0:1] = jnp.where(lower_core, b1, mean)
     vec_ref[1:2] = jnp.where(lower_core, eta1, info)
     vec_ref[2:3] = mean
     vec_ref[3:4] = info
-    vec_ref[4:SUB] = jnp.zeros((SUB - 4, size), F32)
-    store_packed(prefix_ref, cov, mean)
+    vec_ref[4:SUB] = jnp.zeros((SUB - 4, mean.shape[1]), F32)
     if full:
-        for ref, value in zip(more, (trans, prec, cov)):
-            ref[...] = value
+        more[0][...] = trans
+        more[1][...] = prec
 
 
 def pair_up(mine, other, transition, model_error, full):
     order = transition.shape[0]
     square = jax.ShapeDtypeStruct((order, order), F32)
-    shapes = [
-        square,
-        square,
-        jax.ShapeDtypeStruct((SUB, order), F32),
-        jax.ShapeDtypeStruct(mine.shape, F32),
-    ] + [square] * (3 if full else 0)
+    rows = jax.ShapeDtypeStruct((SUB, order), F32)
+    shapes = [jax.ShapeDtypeStruct(mine.shape, F32), square, square, square, rows]
+    shapes = shapes + [square] * (1 if full else 0)
     return pl.pallas_call(
         functools.partial(pair_kernel, full),
         out_shape=shapes,
@@ -551,6 +563,21 @@
         compiler_params=params(24),
         name="pair_up",
     )(mine, other, transition, model_error)
+
+
+def pair_rest(c1, a2, inverse, given, transition, model_error, full):
+    order = transition.shape[0]
+    square = jax.ShapeDtypeStruct((order, order), F32)
+    rows = jax.ShapeDtypeStruct((SUB, order), F32)
+    shapes = [square, square, rows] + [square] * (2 if full else 0)
+    return pl.pallas_call(
+        functools.partial(rest_kernel, full),
+        out_shape=shapes,
+        in_specs=[VMEM] * 6,
+        out_specs=[VMEM] * len(shapes),
+        compiler_params=params(24),
+        name="pair_rest",
+    )(c1, a2, inverse, given, transition, model_error)
 
 
 def advance_kernel(incoming_ref, a_ref, j_ref, c_ref, vec_ref, out_ref):
@@ -781,9 +808,10 @@
         bit *= reach + 1
     other = lax.ppermute(packed, "tm", [(i, i ^ 1) for i in range(windows)])
     pairs = windows // 2
-    a, j, vec, prefix, *more = pair_up(
-        packed, other, transition, model_error[None, :], pairs > 2
-    )
+    full = pairs > 2
+    errors = model_error[None, :]
+    prefix, c1, a2, inverse, given, *covs = pair_up(packed, other, transition, errors, full)
+    a, j, vec, *wide = pair_rest(c1, a2, inverse, given, transition, errors, full)
     incoming = jnp.zeros_like(prefix)
     pair = lax.axis_index("tm") // 2
     for turn in range(pairs - 1):
@@ -793,7 +821,7 @@
             hop = [(i, i + 2) for i in range(windows - 2)]
         incoming = lax.ppermute(prefix, "tm", hop)
         if turn < pairs - 2:
-            longer = advance_prefix(incoming, *more, vec)
+            longer = advance_prefix(incoming, *wide, *covs, vec)
             prefix = jnp.where(pair == turn + 1, longer, prefix)
     mean, sums = finish(incoming, a, j, vec, basis, rows, nx)
     sums_near = swap_near(sums)

time: 80.5 us -> 79.9 us (level)
  waiting for transfers between devices: 29.8 us -> 28.4 us
  Pallas kernels: 35.9 us -> 36.8 us
    ppermute x1, waiting for transfers between devices: 5.63 us -> 4.19 us  [on_device(): incoming = lax.ppermute(prefix, 'tm', hop)]
    pallas_call x0 -> x1, Pallas kernels: none -> 1.43 us  [pair_rest(): pl.pallas_call(functools.partial(rest_kernel, full), out_shape=shapes, in...]
  transfers between devices with their start and end apart: 12 -> 12, of which waited for: 10 -> 10; matrix products, arithmetic and copies ran while one was open for 0% -> 0% of each run, Pallas kernels for 11% -> 13%
where the time goes in v6:
time: 79.9 us; the launch traced here: 79.7 us
  Pallas kernels  36.8 us (46%)
  waiting for transfers between devices  28.4 us (36%)
  starting transfers between devices  13.7 us (17%)
    pallas_call x1, Pallas kernels, pair_up(): pl.pallas_call(functools.partial(pair_kernel, full), out_shape=shapes, in...  18.2 us
    ppermute x4, waiting for transfers between devices, on_device(): lax.ppermute(packed, 'tile', [(i, i ^ bit * by) for i in range(tiles)])  10.7 us
    pallas_call x3, Pallas kernels, project(): pl.pallas_call(functools.partial(project_kernel, slot, rows, nx), out_sha...  9.12 us
    ppermute x3, starting transfers between devices, swap_far(): return lax.ppermute(array, ('tm', 'tile'), far)  7.54 us
    ppermute x3, waiting for transfers between devices, swap_near(): return lax.ppermute(array, 'tile', near)  6.76 us
    ppermute x3, waiting for transfers between devices, swap_far(): return lax.ppermute(array, ('tm', 'tile'), far)  5.39 us
    ppermute x1, waiting for transfers between devices, on_device(): incoming = lax.ppermute(prefix, 'tm', hop)  4.19 us
    ppermute x4, starting transfers between devices, on_device(): lax.ppermute(packed, 'tile', [(i, i ^ bit * by) for i in range(tiles)])  3.95 us
  transfers between devices with their start and end apart: 12, of which 10 were waited for; matrix products, arithmetic and copies ran while one was open for 0% of the time, Pallas kernels for 13%

profile of v6, /device:TPU:22, one launch (start us, length us, event | category | flops | bytes accessed | tf_op | source)
XLA Modules:
  0.0 79.7 jit_solution(15864908789054741096)
XLA Ops:
  0.6 1.3 %gather_info.1.own_ref.mo = f32[16,256]{1,0:T(8,128)} custom-call(f32[8,256]{1,0:T(8,128)} %depth_ref.1, s32[1,256]{1,0:T(1,128)} %cells_ref.1, s32[1,256]{1,0:T(1,128)} %fields_ref.1), custom_call_target="tpu_custom_call" | custom-call | tf_op jit(solution)/shard_map/gather_info/pallas_call | solution.py:749
  2.0 0.6 collective-permute-start.1
  2.6 2.5 %collective-permute-start = (f32[16,256]{1,0:T(8,128)}, f32[16,256]{1,0:T(8,128)S(1)}, u32[]{:S(2)}, u32[]{:S(2)}) collective-permute-start(f32[16,256]{1,0:T(8,128)} %gather_info.1.own_ref.mo), channel_id=1, source_target_pairs={{0,8},{1,2},{2,1},{3,4},{4,3},{5,6},{6,5},{7,15},{8,0},{9,10},{10,... | collective-permute-start | bytes 49160 | tf_op jit(solution)/shard_map/ppermute | solution.py:782
  5.1 2.9 %lay_out.1.basis_ref = bf16[3,256,2048]{2,1,0:T(8,128)(2,1)S(1)} custom-call(bf16[3,256,8,256]{3,2,1,0:T(8,128)(2,1)} %bitcast.5), custom_call_target="tpu_custom_call" | custom-call | tf_op jit(solution)/shard_map/lay_out/pallas_call | solution.py:718
  8.0 3.1 %shard_map.95 = f32[256,256]{1,0:T(8,128)S(1)} custom-call(f32[16,256]{1,0:T(8,128)S(1)} %copy-done.1, f32[16,256]{1,0:T(8,128)S(1)} %collective-permute-done.1.first_ref.second_ref.mf, f32[16,256]{1,0:T(8,128)S(1)} %collective-permute-done.1.first_ref.second_ref.mf, bf16[3,256,2048]{2,1,0:T(8,128)(2,1)S(1)} %lay_out.1.basis_ref), custom_call_target="tpu_custom_call" | custom-call | flops 1610612736 | bytes 3145728 | tf_op jit(solution)/shard_map/pallas_call | solution.py:254
  11.1 3.1 %shard_map.96 = f32[256,256]{1,0:T(8,128)S(1)} custom-call(f32[16,256]{1,0:T(8,128)S(1)} %copy-done.1, f32[16,256]{1,0:T(8,128)S(1)} %collective-permute-done.first_ref.second_ref.ms, f32[16,256]{1,0:T(8,128)S(1)} %collective-permute-done.first_ref.second_ref.ms, bf16[3,256,2048]{2,1,0:T(8,128)(2,1)S(1)} %lay_out.1.basis_ref), custom_call_target="tpu_custom_call" | custom-call | flops 1610612736 | bytes 3145728 | tf_op jit(solution)/shard_map/pallas_call | solution.py:254
  14.2 0.0 copy-start
  14.2 0.5 collective-permute-start.3
  14.7 1.5 %collective-permute-start.2 = (f32[256,256]{1,0:T(8,128)S(1)}, f32[256,256]{1,0:T(8,128)S(1)}, u32[]{:S(2)}, u32[]{:S(2)}) collective-permute-start(f32[256,256]{1,0:T(8,128)S(1)} %shard_map.95), channel_id=1, source_target_pairs={{0,1},{1,0},{2,3},{3,2},{4,5},{5,4},{6,7},{7,6},{8,9},{9,8},{10,11... | collective-permute-start | bytes 786440 | tf_op jit(solution)/shard_map/ppermute | solution.py:779
  16.2 3.0 %shard_map.97.own_ref = f32[256,256]{1,0:T(8,128)S(1)} custom-call(f32[16,256]{1,0:T(8,128)S(1)} %copy-done.1, f32[16,256]{1,0:T(8,128)S(1)} %collective-permute-done.1.first_ref.second_ref.mf, f32[16,256]{1,0:T(8,128)S(1)} %collective-permute-done.first_ref.second_ref.ms, bf16[3,256,2048]{2,1,0:T(8,128)(2,1)S(1)} %lay_out.1.basis_ref), custom_call_target="tpu_custom_call" | custom-call | flops 1610612736 | bytes 3145728 | tf_op jit(solution)/shard_map/pallas_call | solution.py:254
  19.2 3.6 %collective-permute-done.3.second_ref = f32[256,256]{1,0:T(8,128)S(1)} collective-permute-done((f32[256,256]{1,0:T(8,128)S(1)}, f32[256,256]{1,0:T(8,128)S(1)}, u32[]{:S(2)}, u32[]{:S(2)}) %collective-permute-start.3) | collective-permute-done | bytes 262176 | tf_op jit(solution)/shard_map/ppermute | solution.py:782
  22.8 4.8 %collective-permute-done.2.first_ref = f32[256,256]{1,0:T(8,128)S(1)} collective-permute-done((f32[256,256]{1,0:T(8,128)S(1)}, f32[256,256]{1,0:T(8,128)S(1)}, u32[]{:S(2)}, u32[]{:S(2)}) %collective-permute-start.2) | collective-permute-done | bytes 262176 | tf_op jit(solution)/shard_map/ppermute | solution.py:779
  27.5 0.4 gram.1
  27.9 1.2 %collective-permute-start.6 = (f32[264,128]{1,0:T(8,128)S(1)}, f32[264,128]{1,0:T(8,128)S(1)}, u32[]{:S(2)}, u32[]{:S(2)}) collective-permute-start(f32[264,128]{1,0:T(8,128)S(1)} %gram.1), channel_id=1, source_target_pairs={{0,3},{1,2},{2,1},{3,0},{4,7},{5,6},{6,5},{7,4},{8,11},{9,10},{10,... | collective-permute-start | bytes 405512 | tf_op jit(solution)/shard_map/ppermute | solution.py:802
  29.1 0.4 collective-permute-start.5
  29.6 1.9 %collective-permute-start.4 = (f32[264,128]{1,0:T(8,128)S(1)}, f32[264,128]{1,0:T(8,128)S(1)}, u32[]{:S(2)}, u32[]{:S(2)}) collective-permute-start(f32[264,128]{1,0:T(8,128)S(1)} %gram.1), channel_id=1, source_target_pairs={{0,1},{1,0},{2,3},{3,2},{4,5},{5,4},{6,7},{7,6},{8,9},{9,8},{10,11... | collective-permute-start | bytes 405512 | tf_op jit(solution)/shard_map/ppermute | solution.py:802
  31.5 3.6 %collective-permute-done.6 = f32[264,128]{1,0:T(8,128)S(1)} collective-permute-done((f32[264,128]{1,0:T(8,128)S(1)}, f32[264,128]{1,0:T(8,128)S(1)}, u32[]{:S(2)}, u32[]{:S(2)}) %collective-permute-start.6) | collective-permute-done | bytes 135200 | tf_op jit(solution)/shard_map/ppermute | solution.py:802
  35.1 0.9 %collective-permute-done.5 = f32[264,128]{1,0:T(8,128)S(1)} collective-permute-done((f32[264,128]{1,0:T(8,128)S(1)}, f32[264,128]{1,0:T(8,128)S(1)}, u32[]{:S(2)}, u32[]{:S(2)}) %collective-permute-start.5) | collective-permute-done | bytes 135200 | tf_op jit(solution)/shard_map/ppermute | solution.py:802
  36.0 0.5 collective-permute-done.4
  36.5 0.4 collective-permute-start.7
  36.9 5.6 %collective-permute-done.7 = f32[264,128]{1,0:T(8,128)S(1)} collective-permute-done((f32[264,128]{1,0:T(8,128)S(1)}, f32[264,128]{1,0:T(8,128)S(1)}, u32[]{:S(2)}, u32[]{:S(2)}) %collective-permute-start.7) | collective-permute-done | bytes 135200 | tf_op jit(solution)/shard_map/ppermute | solution.py:802
  42.6 0.1 collective-permute-start.8
  42.7 1.3 %collective-permute-done.8.other_ref = f32[264,128]{1,0:T(8,128)S(1)} collective-permute-done((f32[264,128]{1,0:T(8,128)S(1)}, f32[264,128]{1,0:T(8,128)S(1)}, u32[]{:S(2)}, u32[]{:S(2)}) %collective-permute-start.8) | collective-permute-done | bytes 135200 | tf_op jit(solution)/shard_map/ppermute | solution.py:809
  44.0 18.2 %pair_up.1 = (f32[264,128]{1,0:T(8,128)S(1)}, f32[256,256]{1,0:T(8,128)S(1)}, f32[256,256]{1,0:T(8,128)S(1)}, f32[256,256]{1,0:T(8,128)S(1)}, f32[8,256]{1,0:T(8,128)S(1)}) custom-call(f32[264,128]{1,0:T(8,128)S(1)} %add.15.mine_ref, f32[264,128]{1,0:T(8,128)S(1)} %collective-permute-done.8.other_ref, f32[256,256]{1,0:T(8,128)S(1)} %copy-done, ...), custom_call_target="tpu_custom_call" | custom-call | tf_op jit(solution)/shard_map/pair_up/pallas_call | solution.py:558
  62.2 0.0 collective-permute-start.9
  62.3 1.4 %pair_rest.1 = (f32[256,256]{1,0:T(8,128)S(1)}, f32[256,256]{1,0:T(8,128)S(1)}, f32[8,256]{1,0:T(8,128)S(1)}) custom-call(f32[256,256]{1,0:T(8,128)S(1)} %get-tuple-element.17.c1_ref, f32[256,256]{1,0:T(8,128)S(1)} %get-tuple-element.18.a2_ref, f32[256,256]{1,0:T(8,128)S(1)} %get-tuple-element.19.inverse_ref, f32[8,256]{1,0:T(8,128)S(1)} %get-tuple-element.20.given_ref, ...), custom_call_target="tpu_custom_call" | custom-call | tf_op jit(solution)/shard_map/pair_rest/pallas_call | solution.py:573
  63.7 4.2 %collective-permute-done.9.incoming_ref = f32[264,128]{1,0:T(8,128)S(1)} collective-permute-done((f32[264,128]{1,0:T(8,128)S(1)}, f32[264,128]{1,0:T(8,128)S(1)}, u32[]{:S(2)}, u32[]{:S(2)}) %collective-permute-start.9) | collective-permute-done | bytes 135200 | tf_op jit(solution)/shard_map/ppermute | solution.py:822
  67.9 2.5 %finish.1 = (f32[1,256]{1,0:T(1,128)}, f32[24,256]{1,0:T(8,128)S(1)}) custom-call(f32[264,128]{1,0:T(8,128)S(1)} %collective-permute-done.9.incoming_ref, f32[256,256]{1,0:T(8,128)S(1)} %get-tuple-element.21.a_ref, f32[256,256]{1,0:T(8,128)S(1)} %get-tuple-element.22.j_ref, f32[8,256]{1,0:T(8,128)S(1)} %get-tuple-element.23.vec_ref, ...), custom_call_target="tpu_custom_call" | custom-call | tf_op jit(solution)/shard_map/finish/pallas_call | solution.py:633
  70.4 4.6 %collective-permute-start.11 = (f32[24,256]{1,0:T(8,128)S(1)}, f32[24,256]{1,0:T(8,128)S(1)}, u32[]{:S(2)}, u32[]{:S(2)}) collective-permute-start(f32[24,256]{1,0:T(8,128)S(1)} %get-tuple-element.25.own_ref), channel_id=1, source_target_pairs={{0,8},{1,2},{2,1},{3,4},{4,3},{5,6},{6,5},{7,15},{8,0},{9,10},{10,... | collective-permute-start | bytes 73736 | tf_op jit(solution)/shard_map/ppermute | solution.py:782
  74.9 1.8 %collective-permute-done.11.second_ref = f32[24,256]{1,0:T(8,128)S(1)} collective-permute-done((f32[24,256]{1,0:T(8,128)S(1)}, f32[24,256]{1,0:T(8,128)S(1)}, u32[]{:S(2)}, u32[]{:S(2)}) %collective-permute-start.11) | collective-permute-done | bytes 24608 | tf_op jit(solution)/shard_map/ppermute | solution.py:782
  76.8 2.0 %collective-permute-done.10.first_ref = f32[24,256]{1,0:T(8,128)S(1)} collective-permute-done((f32[24,256]{1,0:T(8,128)S(1)}, f32[24,256]{1,0:T(8,128)S(1)}, u32[]{:S(2)}, u32[]{:S(2)}) %collective-permute-start.10) | collective-permute-done | bytes 24608 | tf_op jit(solution)/shard_map/ppermute | solution.py:779
  78.8 0.9 %propagate_sum.1 = f32[3,8,256]{2,1,0:T(8,128)} custom-call(f32[24,256]{1,0:T(8,128)S(1)} %get-tuple-element.25.own_ref, f32[24,256]{1,0:T(8,128)S(1)} %collective-permute-done.10.first_ref, f32[24,256]{1,0:T(8,128)S(1)} %collective-permute-done.11.second_ref, f32[16,256]{1,0:T(8,128)S(1)} %copy-done.1, ...), custom_call_target="tpu_custom_call" | custom-call | tf_op jit(solution)/shard_map/propagate_sum/pallas_call | solution.py:687
  (14 shorter events, 0.1 us)
Async XLA Ops:
  2.0 6.0 %collective-permute-start.1 = (f32[16,256]{1,0:T(8,128)}, f32[16,256]{1,0:T(8,128)S(1)}, u32[]{:S(2)}, u32[]{:S(2)}) collective-permute-start(f32[16,256]{1,0:T(8,128)} %gather_info.1.own_ref.mo), channel_id=1, source_target_pairs={{0,1},{1,0},{2,3},{3,2},{4,5},{5,4},{6,7},{7,6},{8,9},{9,8},{10,11... | collective-permute-start | bytes 49160 | tf_op jit(solution)/shard_map/ppermute | solution.py:779
  2.6 8.5 %collective-permute-start = (f32[16,256]{1,0:T(8,128)}, f32[16,256]{1,0:T(8,128)S(1)}, u32[]{:S(2)}, u32[]{:S(2)}) collective-permute-start(f32[16,256]{1,0:T(8,128)} %gather_info.1.own_ref.mo), channel_id=1, source_target_pairs={{0,8},{1,2},{2,1},{3,4},{4,3},{5,6},{6,5},{7,15},{8,0},{9,10},{10,... | collective-permute-start | bytes 49160 | tf_op jit(solution)/shard_map/ppermute | solution.py:782
  5.1 2.9 %copy-start.1 = (f32[16,256]{1,0:T(8,128)S(1)}, f32[16,256]{1,0:T(8,128)}, u32[]{:S(2)}) copy-start(f32[16,256]{1,0:T(8,128)} %gather_info.1.own_ref.mo) | copy-start | bytes 49156
  14.2 13.4 %copy-start.3 = (f32[1,256]{1,0:T(1,128)S(1)}, f32[1,256]{1,0:T(1,128)}, u32[]{:S(2)}) copy-start(f32[1,256]{1,0:T(1,128)} %weight_ref.1) | copy-start | bytes 3076
  14.2 13.4 %copy-start.4 = (f32[1,256]{1,0:T(1,128)S(1)}, f32[1,256]{1,0:T(1,128)}, u32[]{:S(2)}) copy-start(f32[1,256]{1,0:T(1,128)} %innovation_ref.1) | copy-start | bytes 3076
  14.2 29.8 %copy-start = (f32[256,256]{1,0:T(8,128)S(1)}, f32[256,256]{1,0:T(8,128)}, u32[]{:S(2)}) copy-start(f32[256,256]{1,0:T(8,128)} %transition_ref.3) | copy-start | bytes 786436
  14.2 29.8 %copy-start.2 = (f32[256]{0:T(256)S(1)}, f32[256]{0:T(256)}, u32[]{:S(2)}) copy-start(f32[256]{0:T(256)} %param.15) | copy-start | bytes 3076
  14.2 8.5 %collective-permute-start.3 = (f32[256,256]{1,0:T(8,128)S(1)}, f32[256,256]{1,0:T(8,128)S(1)}, u32[]{:S(2)}, u32[]{:S(2)}) collective-permute-start(f32[256,256]{1,0:T(8,128)S(1)} %shard_map.96), channel_id=1, source_target_pairs={{0,8},{1,2},{2,1},{3,4},{4,3},{5,6},{6,5},{7,15},{8,0},{9,10},{10,... | collective-permute-start | bytes 786440 | tf_op jit(solution)/shard_map/ppermute | solution.py:782
  14.7 12.8 %collective-permute-start.2 = (f32[256,256]{1,0:T(8,128)S(1)}, f32[256,256]{1,0:T(8,128)S(1)}, u32[]{:S(2)}, u32[]{:S(2)}) collective-permute-start(f32[256,256]{1,0:T(8,128)S(1)} %shard_map.95), channel_id=1, source_target_pairs={{0,1},{1,0},{2,3},{3,2},{4,5},{5,4},{6,7},{7,6},{8,9},{9,8},{10,11... | collective-permute-start | bytes 786440 | tf_op jit(solution)/shard_map/ppermute | solution.py:779
  27.9 7.2 %collective-permute-start.6 = (f32[264,128]{1,0:T(8,128)S(1)}, f32[264,128]{1,0:T(8,128)S(1)}, u32[]{:S(2)}, u32[]{:S(2)}) collective-permute-start(f32[264,128]{1,0:T(8,128)S(1)} %gram.1), channel_id=1, source_target_pairs={{0,3},{1,2},{2,1},{3,0},{4,7},{5,6},{6,5},{7,4},{8,11},{9,10},{10,... | collective-permute-start | bytes 405512 | tf_op jit(solution)/shard_map/ppermute | solution.py:802
  29.1 6.8 %collective-permute-start.5 = (f32[264,128]{1,0:T(8,128)S(1)}, f32[264,128]{1,0:T(8,128)S(1)}, u32[]{:S(2)}, u32[]{:S(2)}) collective-permute-start(f32[264,128]{1,0:T(8,128)S(1)} %gram.1), channel_id=1, source_target_pairs={{0,2},{1,3},{2,0},{3,1},{4,6},{5,7},{6,4},{7,5},{8,10},{9,11},{10,... | collective-permute-start | bytes 405512 | tf_op jit(solution)/shard_map/ppermute | solution.py:802
  29.6 6.9 %collective-permute-start.4 = (f32[264,128]{1,0:T(8,128)S(1)}, f32[264,128]{1,0:T(8,128)S(1)}, u32[]{:S(2)}, u32[]{:S(2)}) collective-permute-start(f32[264,128]{1,0:T(8,128)S(1)} %gram.1), channel_id=1, source_target_pairs={{0,1},{1,0},{2,3},{3,2},{4,5},{5,4},{6,7},{7,6},{8,9},{9,8},{10,11... | collective-permute-start | bytes 405512 | tf_op jit(solution)/shard_map/ppermute | solution.py:802
  36.5 6.0 %collective-permute-start.7 = (f32[264,128]{1,0:T(8,128)S(1)}, f32[264,128]{1,0:T(8,128)S(1)}, u32[]{:S(2)}, u32[]{:S(2)}) collective-permute-start(f32[264,128]{1,0:T(8,128)S(1)} %add_add_fusion), channel_id=1, source_target_pairs={{0,4},{1,5},{2,6},{3,7},{4,0},{5,1},{6,2},{7,3},{8,12},{9,13},{10,... | collective-permute-start | bytes 405512 | tf_op jit(solution)/shard_map/ppermute | solution.py:802
  42.6 1.4 %collective-permute-start.8 = (f32[264,128]{1,0:T(8,128)S(1)}, f32[264,128]{1,0:T(8,128)S(1)}, u32[]{:S(2)}, u32[]{:S(2)}) collective-permute-start(f32[264,128]{1,0:T(8,128)S(1)} %add.15.mine_ref), channel_id=1, source_target_pairs={{0,8},{8,0},{16,24},{24,16},{1,9},{9,1},{17,25},{25,17},{2,10},{10... | collective-permute-start | bytes 405512 | tf_op jit(solution)/shard_map/ppermute | solution.py:809
  62.2 5.7 %collective-permute-start.9 = (f32[264,128]{1,0:T(8,128)S(1)}, f32[264,128]{1,0:T(8,128)S(1)}, u32[]{:S(2)}, u32[]{:S(2)}) collective-permute-start(f32[264,128]{1,0:T(8,128)S(1)} %get-tuple-element.16), channel_id=1, source_target_pairs={{0,16},{8,24},{16,0},{24,8},{1,17},{9,25},{17,1},{25,9},{2,18},{10... | collective-permute-start | bytes 405512 | tf_op jit(solution)/shard_map/ppermute | solution.py:822
  70.4 6.4 %collective-permute-start.11 = (f32[24,256]{1,0:T(8,128)S(1)}, f32[24,256]{1,0:T(8,128)S(1)}, u32[]{:S(2)}, u32[]{:S(2)}) collective-permute-start(f32[24,256]{1,0:T(8,128)S(1)} %get-tuple-element.25.own_ref), channel_id=1, source_target_pairs={{0,8},{1,2},{2,1},{3,4},{4,3},{5,6},{6,5},{7,15},{8,0},{9,10},{10,... | collective-permute-start | bytes 73736 | tf_op jit(solution)/shard_map/ppermute | solution.py:782
  74.9 3.8 %collective-permute-start.10 = (f32[24,256]{1,0:T(8,128)S(1)}, f32[24,256]{1,0:T(8,128)S(1)}, u32[]{:S(2)}, u32[]{:S(2)}) collective-permute-start(f32[24,256]{1,0:T(8,128)S(1)} %get-tuple-element.25.own_ref), channel_id=1, source_target_pairs={{0,1},{1,0},{2,3},{3,2},{4,5},{5,4},{6,7},{7,6},{8,9},{9,8},{10,11... | collective-permute-start | bytes 73736 | tf_op jit(solution)/shard_map/ppermute | solution.py:779
